TPU v7x, 32 devices: a whole 2x2x4 slice. The times are simulated.
32 devices in a mesh: rows: 8 (over z, y), seq: 4 (over x, core).
Axes of the slice: x: 2, y: 2, z: 4, core: 2. Of those that a mesh axis runs over, the one named last changes fastest.
Arguments:
- layer_input: bfloat16 [16, 512, 768], P('rows', 'seq'), may hold values from -6 to 6
- memory: bfloat16 [16, 512, 768], P('rows', 'seq'), may hold values from -6 to 6
- output_grad: bfloat16 [16, 512, 768], P('rows', 'seq'), may hold values from -6 to 6
- segments: int32 [16, 512], P('rows'), may hold values from 0 to 3, never falling along the last dimension, each value on 1 to 256 neighbouring positions
- buckets: int32 [512], replicated, may hold values from 0 to 31, as said below
- self_query: bfloat16 [768, 768], P('rows', 'seq'), may hold values from -0.21875 to 0.21875
- self_key: bfloat16 [768, 768], P('rows', 'seq'), may hold values from -0.21875 to 0.21875
- self_value: bfloat16 [768, 768], P('rows', 'seq'), may hold values from -0.21875 to 0.21875
- self_output: bfloat16 [768, 768], P('rows', 'seq'), may hold values from -1.25 to 1.25
- cross_query: bfloat16 [768, 768], P('rows', 'seq'), may hold values from -0.21875 to 0.21875
- cross_key: bfloat16 [768, 768], P('rows', 'seq'), may hold values from -0.21875 to 0.21875
- cross_value: bfloat16 [768, 768], P('rows', 'seq'), may hold values from -0.21875 to 0.21875
- cross_output: bfloat16 [768, 768], P('rows', 'seq'), may hold values from -1.75 to 1.75
- gate_weight: bfloat16 [768, 2048], P('rows', 'seq'), may hold values from -0.21875 to 0.21875
- up_weight: bfloat16 [768, 2048], P('rows', 'seq'), may hold values from -0.21875 to 0.21875
- down_weight: bfloat16 [2048, 768], P('rows', 'seq'), may hold values from -0.125 to 0.125
- norm_gains: bfloat16 [3, 768], P(None, 'rows'), may hold values from 0.5 to 1.5
- position_bias: bfloat16 [32, 12], replicated, may hold values from -3 to 3
Outputs:
- mixed: bfloat16 [16, 512, 768], P('rows', 'seq')
- input_grad: float32 [16, 512, 768], P('rows', 'seq')
- memory_grad: float32 [16, 512, 768], P('rows', 'seq')
- self_query_grad: float32 [768, 768], P('rows', 'seq')
- self_key_grad: float32 [768, 768], P('rows', 'seq')
- self_value_grad: float32 [768, 768], P('rows', 'seq')
- self_output_grad: float32 [768, 768], P('rows', 'seq')
- cross_query_grad: float32 [768, 768], P('rows', 'seq')
- cross_key_grad: float32 [768, 768], P('rows', 'seq')
- cross_value_grad: float32 [768, 768], P('rows', 'seq')
- cross_output_grad: float32 [768, 768], P('rows', 'seq')
- gate_weight_grad: float32 [768, 2048], P('rows', 'seq')
- up_weight_grad: float32 [768, 2048], P('rows', 'seq')
- down_weight_grad: float32 [2048, 768], P('rows', 'seq')
- norm_gains_grad: float32 [3, 768], P(None, 'rows')
- position_bias_grad: float32 [32, 12], replicated
Inputs may be any that keep to these rules, and one draw needn't show every extreme that they name: `segments`: segment ids never fall along a row, every id of 0 to 3 is used, and a document spans 1 to 256 positions. buckets[d] = d for d < 16; the table never falls and buckets[511] = 31.
All inputs are finite; a program needn't handle non-finite values.
Results may differ from a plain program's by a relative error of at most 0.03.
Values may be sent and summed in bfloat16 or wider, within the bound.
A program may use at most 192 MiB of HBM per device.

v0:
```python
import jax
import jax.numpy as jnp
from jax import lax
from jax.sharding import PartitionSpec as P

D = 768
HEADS = 12
HEAD_DIM = 64
FF = 2048
BUCKETS = 32
MICRO = 2


EPS = 1e-06
NEG = -1e30
PRECISION_HIGH = lax.Precision.HIGHEST


def norm_apply(value, gain):
    return value * lax.rsqrt(jnp.mean(value * value, axis=-1, keepdims=True) + EPS) * gain


def gelu_tanh(value):
    return jax.nn.gelu(value, approximate=True)


def project(left, weight):
    return jnp.einsum("rsd,df->rsf", left, weight, preferred_element_type=jnp.float32)


def weight_grad(left, grad):
    return jnp.einsum("rsd,rsf->df", left, grad, preferred_element_type=jnp.float32)


def back_project(grad, weight):
    return jnp.einsum("rsf,df->rsd", grad, weight, preferred_element_type=jnp.float32)


def split_heads(value):
    return value.reshape(value.shape[0], value.shape[1], HEADS, HEAD_DIM)


def attend_scores(query, key_all, bias, allowed):
    scores = jnp.einsum(
        "rqhe,rkhe->rhqk",
        split_heads(query),
        split_heads(key_all),
        preferred_element_type=jnp.float32,
    )
    scores = scores * HEAD_DIM ** (-0.5) + bias
    return jnp.where(allowed, scores, NEG)


def attend_forward(query, key_all, value_all, bias, allowed):
    scores = attend_scores(query, key_all, bias, allowed)
    peak = jnp.max(scores, axis=-1, keepdims=True)
    log_total = peak + jnp.log(jnp.sum(jnp.exp(scores - peak), axis=-1, keepdims=True))
    soft_weights = jnp.exp(scores - log_total).astype(jnp.bfloat16)
    combined = jnp.einsum(
        "rhqk,rkhe->rqhe", soft_weights, split_heads(value_all), preferred_element_type=jnp.float32
    )
    return (combined.reshape(query.shape).astype(jnp.bfloat16), log_total)


def attend_backward(query, key_all, value_all, bias, allowed, log_total, grad_out):
    soft_weights = jnp.exp(attend_scores(query, key_all, bias, allowed) - log_total)
    grad_heads = split_heads(grad_out)
    grad_probs = jnp.einsum(
        "rqhe,rkhe->rhqk", grad_heads, split_heads(value_all), preferred_element_type=jnp.float32
    )
    rowdot = jnp.sum(soft_weights * grad_probs, axis=-1, keepdims=True)
    grad_scores = (soft_weights * (grad_probs - rowdot)).astype(jnp.bfloat16)
    score_scale = HEAD_DIM ** (-0.5)
    grad_query = (
        jnp.einsum(
            "rhqk,rkhe->rqhe", grad_scores, split_heads(key_all), preferred_element_type=jnp.float32
        )
        * score_scale
    )
    grad_key = (
        jnp.einsum(
            "rhqk,rqhe->rkhe", grad_scores, split_heads(query), preferred_element_type=jnp.float32
        )
        * score_scale
    )
    grad_value = jnp.einsum(
        "rhqk,rqhe->rkhe",
        soft_weights.astype(jnp.bfloat16),
        grad_heads,
        preferred_element_type=jnp.float32,
    )
    return (
        grad_query.reshape(query.shape).astype(jnp.bfloat16),
        grad_key.reshape(key_all.shape),
        grad_value.reshape(value_all.shape),
        grad_scores,
        rowdot,
    )


def seq_section(
    self_query,
    self_key,
    self_value,
    self_output,
    cross_query,
    cross_key,
    cross_value,
    cross_output,
    gate_weight,
    up_weight,
    down_weight,
):
    return (
        lax.all_gather(self_query, "seq", axis=1, tiled=True),
        lax.all_gather(self_key, "seq", axis=1, tiled=True),
        lax.all_gather(self_value, "seq", axis=1, tiled=True),
        lax.all_gather(self_output, "seq", axis=1, tiled=True),
        lax.all_gather(cross_query, "seq", axis=1, tiled=True),
        lax.all_gather(cross_key, "seq", axis=1, tiled=True),
        lax.all_gather(cross_value, "seq", axis=1, tiled=True),
        lax.all_gather(cross_output, "seq", axis=1, tiled=True),
        lax.all_gather(gate_weight, "seq", axis=1, tiled=True),
        lax.all_gather(up_weight, "seq", axis=1, tiled=True),
        lax.all_gather(down_weight, "seq", axis=1, tiled=True),
    )


def rows_section(
    self_query,
    self_key,
    self_value,
    self_output,
    cross_query,
    cross_key,
    cross_value,
    cross_output,
    gate_weight,
    up_weight,
    down_weight,
    norm_gains,
):
    return (
        lax.all_gather(self_query, "rows", axis=0, tiled=True),
        lax.all_gather(self_key, "rows", axis=0, tiled=True),
        lax.all_gather(self_value, "rows", axis=0, tiled=True),
        lax.all_gather(self_output, "rows", axis=0, tiled=True),
        lax.all_gather(cross_query, "rows", axis=0, tiled=True),
        lax.all_gather(cross_key, "rows", axis=0, tiled=True),
        lax.all_gather(cross_value, "rows", axis=0, tiled=True),
        lax.all_gather(cross_output, "rows", axis=0, tiled=True),
        lax.all_gather(gate_weight, "rows", axis=0, tiled=True),
        lax.all_gather(up_weight, "rows", axis=0, tiled=True),
        lax.all_gather(down_weight, "rows", axis=0, tiled=True),
        lax.all_gather(norm_gains, "rows", axis=1, tiled=True),
    )


def fetch_weights(weight_set, norm_gains):
    narrowed = seq_section(*weight_set)
    widened = rows_section(*narrowed, norm_gains)
    return (tuple(widened[:11]), widened[11])


def reduce_rows(
    grad_query,
    grad_key,
    grad_value,
    grad_output,
    grad_cquery,
    grad_ckey,
    grad_cvalue,
    grad_coutput,
    grad_gate,
    grad_up,
    grad_down,
):
    return (
        lax.psum_scatter(grad_query, "rows", scatter_dimension=0, tiled=True),
        lax.psum_scatter(grad_key, "rows", scatter_dimension=0, tiled=True),
        lax.psum_scatter(grad_value, "rows", scatter_dimension=0, tiled=True),
        lax.psum_scatter(grad_output, "rows", scatter_dimension=0, tiled=True),
        lax.psum_scatter(grad_cquery, "rows", scatter_dimension=0, tiled=True),
        lax.psum_scatter(grad_ckey, "rows", scatter_dimension=0, tiled=True),
        lax.psum_scatter(grad_cvalue, "rows", scatter_dimension=0, tiled=True),
        lax.psum_scatter(grad_coutput, "rows", scatter_dimension=0, tiled=True),
        lax.psum_scatter(grad_gate, "rows", scatter_dimension=0, tiled=True),
        lax.psum_scatter(grad_up, "rows", scatter_dimension=0, tiled=True),
        lax.psum_scatter(grad_down, "rows", scatter_dimension=0, tiled=True),
    )


def shards(
    layer_input,
    memory,
    output_grad,
    segments,
    buckets,
    self_query,
    self_key,
    self_value,
    self_output,
    cross_query,
    cross_key,
    cross_value,
    cross_output,
    gate_weight,
    up_weight,
    down_weight,
    norm_gains,
    position_bias,
):
    seq_place = lax.axis_index("seq")
    seq_count = lax.axis_size("seq")
    local_rows, seq_dev = (layer_input.shape[0], layer_input.shape[1])
    seq_total = segments.shape[1]
    row_dev = local_rows // MICRO
    query_pos = seq_place * seq_dev + jnp.arange(seq_dev, dtype=jnp.int32)
    key_pos = jnp.arange(seq_total, dtype=jnp.int32)
    causal = key_pos[None, :] <= query_pos[:, None]
    distance = jnp.maximum(query_pos[:, None] - key_pos[None, :], 0)
    bucket_ids = jnp.take(buckets, distance)
    bucket_onehot = (
        bucket_ids[None] == jnp.arange(BUCKETS, dtype=jnp.int32)[:, None, None]
    ).astype(jnp.float32)
    table_single_float = position_bias.astype(jnp.float32)
    bias_lattice = jnp.einsum(
        "wep,wv->vep", bucket_onehot, table_single_float, precision=PRECISION_HIGH
    )[None]
    weight_set = (
        self_query,
        self_key,
        self_value,
        self_output,
        cross_query,
        cross_key,
        cross_value,
        cross_output,
        gate_weight,
        up_weight,
        down_weight,
    )
    d_cols = D // seq_count
    ff_cols = FF // seq_count
    grad_acc = [jnp.zeros((D, d_cols), jnp.float32) for index_w in range(8)]
    grad_acc = grad_acc + [
        jnp.zeros((D, ff_cols), jnp.float32),
        jnp.zeros((D, ff_cols), jnp.float32),
        jnp.zeros((FF, d_cols), jnp.float32),
    ]
    bias_running_total = jnp.zeros((BUCKETS, HEADS), jnp.float32)
    gains_acc = jnp.zeros((3, D), jnp.float32)
    out_mixed, out_input, out_memory = ([], [], [])
    for micro_step in range(MICRO):
        full_mats, full_gains = fetch_weights(weight_set, norm_gains)
        (
            full_query,
            full_key,
            full_value,
            full_output,
            full_cquery,
            full_ckey,
            full_cvalue,
            full_coutput,
            full_gate,
            full_up,
            full_down,
        ) = full_mats
        gain_rows = full_gains.astype(jnp.float32)
        start_row = micro_step * row_dev
        x_block = layer_input[start_row : start_row + row_dev].astype(jnp.float32)
        mem_block = memory[start_row : start_row + row_dev]
        grad_block = output_grad[start_row : start_row + row_dev].astype(jnp.float32)
        seg_block = segments[start_row : start_row + row_dev]
        seg_query = lax.dynamic_slice_in_dim(seg_block, seq_place * seq_dev, seq_dev, 1)
        allowed = (causal[None] & (seg_query[:, :, None] == seg_block[:, None, :]))[:, None]
        normed_one, pull_first = jax.vjp(norm_apply, x_block, gain_rows[0])
        normed_a = normed_one.astype(jnp.bfloat16)
        query = project(normed_a, full_query).astype(jnp.bfloat16)
        key_self = project(normed_a, full_key).astype(jnp.bfloat16)
        value_self = project(normed_a, full_value).astype(jnp.bfloat16)
        mem_key = project(mem_block, full_ckey).astype(jnp.bfloat16)
        mem_value = project(mem_block, full_cvalue).astype(jnp.bfloat16)
        key_all, value_all, mem_key_all, mem_value_all = (
            lax.all_gather(key_self, "seq", axis=1, tiled=True),
            lax.all_gather(value_self, "seq", axis=1, tiled=True),
            lax.all_gather(mem_key, "seq", axis=1, tiled=True),
            lax.all_gather(mem_value, "seq", axis=1, tiled=True),
        )
        attended, total_self = attend_forward(query, key_all, value_all, bias_lattice, allowed)
        x_one = x_block + project(attended, full_output)
        normed_two, pull_second = jax.vjp(norm_apply, x_one, gain_rows[1])
        normed_b = normed_two.astype(jnp.bfloat16)
        cross_q = project(normed_b, full_cquery).astype(jnp.bfloat16)
        cross_att, total_cross = attend_forward(cross_q, mem_key_all, mem_value_all, 0.0, True)
        x_two = x_one + project(cross_att, full_coutput)
        normed_three, pull_third = jax.vjp(norm_apply, x_two, gain_rows[2])
        normed_c = normed_three.astype(jnp.bfloat16)
        gate_pre = project(normed_c, full_gate)
        up_pre = project(normed_c, full_up)
        gelu_out, gelu_pull = jax.vjp(gelu_tanh, gate_pre)
        hidden = (gelu_out * up_pre).astype(jnp.bfloat16)
        out_mixed.append((x_two + project(hidden, full_down)).astype(jnp.bfloat16))
        grad_ff = grad_block.astype(jnp.bfloat16)
        grad_hidden = back_project(grad_ff, full_down)
        grad_gate = gelu_pull(grad_hidden * up_pre)[0].astype(jnp.bfloat16)
        grad_up = (grad_hidden * gelu_out).astype(jnp.bfloat16)
        grad_c = back_project(grad_gate, full_gate) + back_project(grad_up, full_up)
        grad_x2n, gain_three = pull_third(grad_c)
        grad_x2 = grad_block + grad_x2n
        grad_co = grad_x2.astype(jnp.bfloat16)
        grad_catt = back_project(grad_co, full_coutput).astype(jnp.bfloat16)
        grad_cq, part_ckey, part_cvalue, unused_scores, rowdot_cross = attend_backward(
            cross_q, mem_key_all, mem_value_all, 0.0, True, total_cross, grad_catt
        )
        grad_x1n, gain_two = pull_second(back_project(grad_cq, full_cquery))
        grad_x1 = grad_x2 + grad_x1n
        grad_so = grad_x1.astype(jnp.bfloat16)
        grad_att = back_project(grad_so, full_output).astype(jnp.bfloat16)
        grad_query, part_key, part_value, grad_scores, rowdot_self = attend_backward(
            query, key_all, value_all, bias_lattice, allowed, total_self, grad_att
        )
        score_accumulated = jnp.sum(grad_scores.astype(jnp.float32), axis=0)
        bias_running_total = bias_running_total + jnp.einsum(
            "ugv,rgv->ru", score_accumulated, bucket_onehot, precision=PRECISION_HIGH
        )
        sum_key, sum_value, sum_ckey, sum_cvalue = (
            lax.psum_scatter(
                part_key.astype(jnp.bfloat16), "seq", scatter_dimension=1, tiled=True
            ).astype(jnp.float32),
            lax.psum_scatter(
                part_value.astype(jnp.bfloat16), "seq", scatter_dimension=1, tiled=True
            ).astype(jnp.float32),
            lax.psum_scatter(
                part_ckey.astype(jnp.bfloat16), "seq", scatter_dimension=1, tiled=True
            ).astype(jnp.float32),
            lax.psum_scatter(
                part_cvalue.astype(jnp.bfloat16), "seq", scatter_dimension=1, tiled=True
            ).astype(jnp.float32),
        )
        grad_key = sum_key.astype(jnp.bfloat16)
        grad_value = sum_value.astype(jnp.bfloat16)
        grad_ckey = sum_ckey.astype(jnp.bfloat16)
        grad_cvalue = sum_cvalue.astype(jnp.bfloat16)
        grad_a = (
            back_project(grad_query, full_query)
            + back_project(grad_key, full_key)
            + back_project(grad_value, full_value)
        )
        grad_x0n, gain_one = pull_first(grad_a)
        out_input.append(grad_x1 + grad_x0n)
        out_memory.append(
            back_project(grad_ckey, full_ckey) + back_project(grad_cvalue, full_cvalue)
        )
        gains_acc = gains_acc + jnp.stack([gain_one, gain_two, gain_three])
        left_a, left_att, left_b, left_catt, left_mem, left_c, left_hidden = (
            lax.all_gather(normed_a, "seq", axis=1, tiled=True),
            lax.all_gather(attended, "seq", axis=1, tiled=True),
            lax.all_gather(normed_b, "seq", axis=1, tiled=True),
            lax.all_gather(cross_att, "seq", axis=1, tiled=True),
            lax.all_gather(mem_block, "seq", axis=1, tiled=True),
            lax.all_gather(normed_c, "seq", axis=1, tiled=True),
            lax.all_gather(hidden, "seq", axis=1, tiled=True),
        )
        (
            cols_query,
            cols_key,
            cols_value,
            cols_so,
            cols_cq,
            cols_co,
            cols_ckey,
            cols_cvalue,
            cols_gate,
            cols_up,
            cols_ff,
        ) = (
            lax.all_to_all(grad_query, "seq", split_axis=2, concat_axis=1, tiled=True),
            lax.all_to_all(grad_key, "seq", split_axis=2, concat_axis=1, tiled=True),
            lax.all_to_all(grad_value, "seq", split_axis=2, concat_axis=1, tiled=True),
            lax.all_to_all(grad_so, "seq", split_axis=2, concat_axis=1, tiled=True),
            lax.all_to_all(grad_cq, "seq", split_axis=2, concat_axis=1, tiled=True),
            lax.all_to_all(grad_co, "seq", split_axis=2, concat_axis=1, tiled=True),
            lax.all_to_all(grad_ckey, "seq", split_axis=2, concat_axis=1, tiled=True),
            lax.all_to_all(grad_cvalue, "seq", split_axis=2, concat_axis=1, tiled=True),
            lax.all_to_all(grad_gate, "seq", split_axis=2, concat_axis=1, tiled=True),
            lax.all_to_all(grad_up, "seq", split_axis=2, concat_axis=1, tiled=True),
            lax.all_to_all(grad_ff, "seq", split_axis=2, concat_axis=1, tiled=True),
        )
        grad_acc[0] = grad_acc[0] + weight_grad(left_a, cols_query)
        grad_acc[1] = grad_acc[1] + weight_grad(left_a, cols_key)
        grad_acc[2] = grad_acc[2] + weight_grad(left_a, cols_value)
        grad_acc[3] = grad_acc[3] + weight_grad(left_att, cols_so)
        grad_acc[4] = grad_acc[4] + weight_grad(left_b, cols_cq)
        grad_acc[5] = grad_acc[5] + weight_grad(left_mem, cols_ckey)
        grad_acc[6] = grad_acc[6] + weight_grad(left_mem, cols_cvalue)
        grad_acc[7] = grad_acc[7] + weight_grad(left_catt, cols_co)
        grad_acc[8] = grad_acc[8] + weight_grad(left_c, cols_gate)
        grad_acc[9] = grad_acc[9] + weight_grad(left_c, cols_up)
        grad_acc[10] = grad_acc[10] + weight_grad(left_hidden, cols_ff)
    owned = reduce_rows(*grad_acc)
    bias_total, gains_total = lax.psum((bias_running_total, gains_acc), ("rows", "seq"))
    rows_width = D // lax.axis_size("rows")
    gains_own = lax.dynamic_slice_in_dim(
        gains_total, lax.axis_index("rows") * rows_width, rows_width, 1
    )
    mixed = jnp.concatenate(out_mixed, axis=0)
    input_grad = jnp.concatenate(out_input, axis=0)
    memory_grad = jnp.concatenate(out_memory, axis=0)
    return (
        mixed,
        input_grad,
        memory_grad,
        owned[0],
        owned[1],
        owned[2],
        owned[3],
        owned[4],
        owned[5],
        owned[6],
        owned[7],
        owned[8],
        owned[9],
        owned[10],
        gains_own,
        bias_total,
    )


def solution(mesh):
    return jax.shard_map(
        shards,
        mesh=mesh,
        in_specs=(
            P("rows", "seq", None),
            P("rows", "seq", None),
            P("rows", "seq", None),
            P("rows", None),
            P(),
            P("rows", "seq"),
            P("rows", "seq"),
            P("rows", "seq"),
            P("rows", "seq"),
            P("rows", "seq"),
            P("rows", "seq"),
            P("rows", "seq"),
            P("rows", "seq"),
            P("rows", "seq"),
            P("rows", "seq"),
            P("rows", "seq"),
            P(None, "rows"),
            P(),
        ),
        out_specs=(
            P("rows", "seq", None),
            P("rows", "seq", None),
            P("rows", "seq", None),
            P("rows", "seq"),
            P("rows", "seq"),
            P("rows", "seq"),
            P("rows", "seq"),
            P("rows", "seq"),
            P("rows", "seq"),
            P("rows", "seq"),
            P("rows", "seq"),
            P("rows", "seq"),
            P("rows", "seq"),
            P("rows", "seq"),
            P(None, "rows"),
            P(),
        ),
        check_vma=False,
    )
```

profile of v0, /device:TPU:0, one launch (start us, length us, event | category | flops | bytes accessed | tf_op | source)
XLA Modules:
  0.0 1715.2 jit_solution(15075525904597385584)
XLA Ops:
  85.6 21.0 %all-gather.10 = bf16[8,96,3]{1,2,0:T(4,128)(2,1)S(1)} all-gather(bf16[1,96,3]{1,2,0:T(4,128)(2,1)S(1)} %bitcast.966), channel_id=1, replica_groups=mesh['rows'=8,'seq'=4] {'rows'}, dimensions={0}, use_global_device_ids=true | all-gather | bytes 5184 | tf_op jit(solution)/shard_map/all_gather | solution.py:155
  108.1 407.7 %gather_fusion = s32[65536]{0:T(1024)S(1)} fusion(s32[512]{0:T(512)S(1)} %copy-done.2, s32[65536]{0:T(1024)S(1)} %broadcast_clamp_fusion), kind=kCustom, calls=%fused_computation | custom fusion | bytes 786432 | tf_op jit(solution)/shard_map/jit(_take)/gather | solution.py:222
  522.7 8.8 all-gather.1
  541.9 9.2 all-gather
  560.1 9.2 all-gather.3
  571.1 9.3 all-gather.2
  580.8 9.3 all-gather.5
  590.4 9.2 all-gather.4
  616.5 9.2 all-gather.7
  629.6 9.5 all-gather.6
  822.0 14.1 all_gather.197
  842.6 10.3 all_gather.198
  855.4 8.8 all_gather.189
  870.6 10.4 all_gather.193
  887.3 10.3 all_gather.194
  901.7 9.3 all_gather.190
  917.4 10.4 all_gather.191
  934.2 11.6 all_gather.192
  990.0 11.1 all_gather.195
  1012.6 10.9 all_gather.196
  1136.9 13.4 reduce.66
  1155.8 13.4 reduce.67
  1190.1 13.8 all_gather.199
  1203.9 9.1 all_gather.200
  1236.5 13.4 reduce.64
  1259.7 13.4 reduce.65
  1359.5 40.9 %all-reduce = (f32[3,768]{1,0:T(4,128)}, f32[32,12]{0,1:T(8,128)}) all-reduce(f32[3,768]{1,0:T(4,128)} %maximum_add_fusion, f32[32,12]{0,1:T(8,128)} %fusion.36), channel_id=1, replica_groups=mesh['rows'=8,'seq'=4] {'rows','seq'}, use_global_device_ids=true, to_apply=%region_49.50 | all-reduce | flops 2688 | bytes 21504 | tf_op jit(solution)/shard_map/psum | solution.py:402
  1408.1 28.0 %reduce-scatter.44.cloned.1.call-done = f32[96,192]{1,0:T(8,128)} async-done(((f32[768,192]{1,0:T(8,128)}), f32[96,192]{1,0:T(8,128)}) %reduce-scatter.44.cloned.1.call-update) | async-done | bytes 73744 | tf_op jit(solution)/shard_map/reduce_scatter | solution.py:181
  1436.1 66.2 %reduce-scatter.42.cloned.1.call-done = f32[96,192]{1,0:T(8,128)} async-done(((f32[768,192]{1,0:T(8,128)}), f32[96,192]{1,0:T(8,128)}) %reduce-scatter.42.cloned.1.call-update) | async-done | bytes 73744 | tf_op jit(solution)/shard_map/reduce_scatter | solution.py:180
  1502.3 68.4 %reduce-scatter.54.cloned.1.call-done = f32[96,512]{1,0:T(8,128)} async-done(((f32[768,512]{1,0:T(8,128)}), f32[96,512]{1,0:T(8,128)}) %reduce-scatter.54.cloned.1.call-update) | async-done | bytes 196624 | tf_op jit(solution)/shard_map/reduce_scatter | solution.py:188
  1570.7 68.4 %reduce-scatter.52.cloned.1.call-done = f32[96,512]{1,0:T(8,128)} async-done(((f32[768,512]{1,0:T(8,128)}), f32[96,512]{1,0:T(8,128)}) %reduce-scatter.52.cloned.1.call-update) | async-done | bytes 196624 | tf_op jit(solution)/shard_map/reduce_scatter | solution.py:187
  1639.1 69.1 %reduce-scatter.56.cloned.1.call-done = f32[256,192]{0,1:T(8,128)} async-done(((f32[2048,192]{0,1:T(8,128)}), f32[256,192]{0,1:T(8,128)}) %reduce-scatter.56.cloned.1.call-update) | async-done | bytes 196624 | tf_op jit(solution)/shard_map/reduce_scatter | solution.py:189
  (886 shorter events, 670.8 us)
Async XLA Ops:
  7.2 513.9 %all-gather.29.cloned.1.call-start = ((), (), s32[]{:S(2)}) async-start(), calls=%async_computation.43 | async-start | bytes 1327104 | tf_op jit(solution)/shard_map/all_gather | solution.py:145
  15.9 516.8 %all-gather.27.cloned.1.call-start = ((), (), s32[]{:S(2)}) async-start(), calls=%async_computation.42 | async-start | bytes 1327104 | tf_op jit(solution)/shard_map/all_gather | solution.py:144
  23.3 517.0 %all-gather.25.cloned.1.call-start = ((), (), s32[]{:S(2)}) async-start(), calls=%async_computation.41 | async-start | bytes 1327104 | tf_op jit(solution)/shard_map/all_gather | solution.py:146
  30.7 525.4 %all-gather.31.cloned.1.call-start = ((), (), s32[]{:S(2)}) async-start(), calls=%async_computation.44 | async-start | bytes 1327104 | tf_op jit(solution)/shard_map/all_gather | solution.py:147
  37.3 521.1 %all-gather.37.cloned.1.call-start = ((), (), s32[]{:S(2)}) async-start(), calls=%async_computation.47 | async-start | bytes 1327104 | tf_op jit(solution)/shard_map/all_gather | solution.py:149
  44.0 525.3 %all-gather.33.cloned.1.call-start = ((), (), s32[]{:S(2)}) async-start(), calls=%async_computation.45 | async-start | bytes 1327104 | tf_op jit(solution)/shard_map/all_gather | solution.py:150
  50.7 550.6 %all-gather.35.cloned.1.call-start = ((), (), s32[]{:S(2)}) async-start(), calls=%async_computation.46 | async-start | bytes 1327104 | tf_op jit(solution)/shard_map/all_gather | solution.py:148
  57.5 589.0 %all-gather.39.cloned.1.call-start = ((), (), s32[]{:S(2)}) async-start(), calls=%async_computation.48 | async-start | bytes 1327104 | tf_op jit(solution)/shard_map/all_gather | solution.py:151
  64.1 595.4 %all-gather.43.cloned.1.call-start = ((), (), s32[]{:S(2)}) async-start(), calls=%async_computation.50 | async-start | bytes 3538944 | tf_op jit(solution)/shard_map/all_gather | solution.py:153
  71.3 591.8 %all-gather.41.cloned.1.call-start = ((), (), s32[]{:S(2)}) async-start(), calls=%async_computation.49 | async-start | bytes 3538944 | tf_op jit(solution)/shard_map/all_gather | solution.py:152
  78.4 588.2 %all-gather.45.cloned.1.call-start = ((), (), s32[]{:S(2)}) async-start(), calls=%async_computation.51 | async-start | bytes 3538944 | tf_op jit(solution)/shard_map/all_gather | solution.py:154
  85.5 894.7 %reduce-scatter.68.cloned.1.call-start = ((), (), s32[]{:S(2)}) async-start(), calls=%async_computation.68 | async-start | bytes 983040
  708.4 292.7 %reduce-scatter.72.cloned.1.call-start = ((), (), s32[]{:S(2)}) async-start(), calls=%async_computation.70 | async-start | bytes 983040
  736.9 298.6 %reduce-scatter.70.cloned.1.call-start = ((), (), s32[]{:S(2)}) async-start(), calls=%async_computation.69 | async-start | bytes 983040
  751.4 295.5 %reduce-scatter.66.cloned.1.call-start = ((), (), s32[]{:S(2)}) async-start(), calls=%async_computation.67 | async-start | bytes 983040
  761.5 311.6 %reduce-scatter.60.cloned.1.call-start = ((), (), s32[]{:S(2)}) async-start(), calls=%async_computation.64 | async-start | bytes 983040
  775.8 308.8 %reduce-scatter.64.cloned.1.call-start = ((), (), s32[]{:S(2)}) async-start(), calls=%async_computation.66 | async-start | bytes 983040
  796.0 312.5 %reduce-scatter.58.cloned.1.call-start = ((), (), s32[]{:S(2)}) async-start(), calls=%async_computation.63 | async-start | bytes 983040
  806.4 313.6 %reduce-scatter.62.cloned.1.call-start = ((), (), s32[]{:S(2)}) async-start(), calls=%async_computation.65 | async-start | bytes 983040
  813.8 526.0 %all-gather.47.cloned.1.call-start = ((), (), s32[]{:S(2)}) async-start(), calls=%async_computation.61 | async-start | bytes 2621440 | tf_op jit(solution)/shard_map/all_gather | solution.py:363
  814.4 527.7 %all-gather.49.cloned.1.call-start = ((), (), s32[]{:S(2)}) async-start(), calls=%async_computation.62 | async-start | bytes 2621440 | tf_op jit(solution)/shard_map/all_gather | solution.py:363
  842.5 565.6 %reduce-scatter.50.cloned.1.call-start = ((), (), s32[]{:S(2)}) async-start(), calls=%async_computation.57 | async-start | bytes 884736 | tf_op jit(solution)/shard_map/reduce_scatter | solution.py:186
  887.2 520.9 %reduce-scatter.48.cloned.1.call-start = ((), (), s32[]{:S(2)}) async-start(), calls=%async_computation.56 | async-start | bytes 884736 | tf_op jit(solution)/shard_map/reduce_scatter | solution.py:183
  934.2 473.9 %reduce-scatter.46.cloned.1.call-start = ((), (), s32[]{:S(2)}) async-start(), calls=%async_computation.55 | async-start | bytes 884736 | tf_op jit(solution)/shard_map/reduce_scatter | solution.py:182
  970.1 438.0 %reduce-scatter.40.cloned.1.call-start = ((), (), s32[]{:S(2)}) async-start(), calls=%async_computation.52 | async-start | bytes 884736 | tf_op jit(solution)/shard_map/reduce_scatter | solution.py:179
  1012.5 395.6 %reduce-scatter.76.cloned.1.call-start = ((), (), s32[]{:S(2)}) async-start(), calls=%async_computation.72 | async-start | bytes 884736
  1059.9 348.2 %reduce-scatter.74.cloned.1.call-start = ((), (), s32[]{:S(2)}) async-start(), calls=%async_computation.71 | async-start | bytes 884736
  1097.5 338.6 %reduce-scatter.44.cloned.1.call-start = ((), (), s32[]{:S(2)}) async-start(), calls=%async_computation.54 | async-start | bytes 884736 | tf_op jit(solution)/shard_map/reduce_scatter | solution.py:181
  1177.1 325.2 %reduce-scatter.42.cloned.1.call-start = ((), (), s32[]{:S(2)}) async-start(), calls=%async_computation.53 | async-start | bytes 884736 | tf_op jit(solution)/shard_map/reduce_scatter | solution.py:180
  1190.1 380.6 %reduce-scatter.54.cloned.1.call-start = ((), (), s32[]{:S(2)}) async-start(), calls=%async_computation.59 | async-start | bytes 1769472 | tf_op jit(solution)/shard_map/reduce_scatter | solution.py:188
  1279.2 359.9 %reduce-scatter.52.cloned.1.call-start = ((), (), s32[]{:S(2)}) async-start(), calls=%async_computation.58 | async-start | bytes 1769472 | tf_op jit(solution)/shard_map/reduce_scatter | solution.py:187
  1316.8 391.4 %reduce-scatter.56.cloned.1.call-start = ((), (), s32[]{:S(2)}) async-start(), calls=%async_computation.60 | async-start | bytes 1769472 | tf_op jit(solution)/shard_map/reduce_scatter | solution.py:189
  (219 other events, 4330.2 us)
Sparse Core Ops, SparseCore 0:
  16.0 42.5 all-gather.28
  61.3 39.7 all-gather.26
  103.9 39.7 all-gather.24
  146.4 39.8 all-gather.30
  188.3 39.7 all-gather.36
  230.7 39.8 all-gather.32
  272.7 39.8 all-gather.34
  314.8 39.8 all-gather.38
  356.8 58.6 all-gather.42
  417.6 58.6 all-gather.40
  478.4 61.2 all-gather.44
  708.5 19.4 reduce-scatter.67
  737.0 19.5 reduce-scatter.71
  759.0 23.2 reduce-scatter.69
  784.7 23.2 reduce-scatter.65
  810.3 26.4 reduce-scatter.59
  839.2 20.0 reduce-scatter.63
  861.7 24.1 reduce-scatter.57
  889.0 26.6 reduce-scatter.61
  917.1 23.4 all-gather.46
  942.1 30.1 all-gather.48
  976.2 63.2 reduce-scatter.49
  1043.4 62.2 reduce-scatter.47
  1109.4 62.2 reduce-scatter.45
  1175.5 62.2 reduce-scatter.39
  1241.6 62.2 reduce-scatter.75
  1307.6 62.2 reduce-scatter.73
  1373.7 62.3 reduce-scatter.43
  1440.0 62.2 reduce-scatter.41
  1506.1 64.5 reduce-scatter.53
  1574.7 64.3 reduce-scatter.51
  1643.2 64.9 reduce-scatter.55
where the time goes:
time: 1730 us; the launch traced here: 1720 us
  local copies, waits for them, and re-layouts  668 us (39%)
  blocking collectives  333 us (19%)
  waiting for transfers between devices  317 us (18%)
  matrix products  173 us (10%)
  other arithmetic  120 us (7%)
  starting transfers between devices  86.8 us (5%)
  between operations  17.9 us (1%)
    gather x2, local copies, waits for them, and re-layouts, shards(): bucket_ids = jnp.take(buckets, distance)  408 us
    unnamed x504, local copies, waits for them, and re-layouts  175 us
    unnamed x23, other arithmetic  101 us
    reduce_scatter x1, waiting for transfers between devices, reduce_rows(): lax.psum_scatter(grad_down, 'rows', scatter_dimension=0, tiled=True)  69.1 us
    reduce_scatter x1, waiting for transfers between devices, reduce_rows(): lax.psum_scatter(grad_gate, 'rows', scatter_dimension=0, tiled=True)  68.4 us
    reduce_scatter x1, waiting for transfers between devices, reduce_rows(): lax.psum_scatter(grad_up, 'rows', scatter_dimension=0, tiled=True)  68.4 us
    reduce_scatter x1, waiting for transfers between devices, reduce_rows(): lax.psum_scatter(grad_key, 'rows', scatter_dimension=0, tiled=True)  66.2 us
    psum x1, blocking collectives, shards(): lax.psum((bias_running_total, gains_acc), ('rows', 'seq'))  40.9 us
  transfers between devices with their start and end apart: 54, of which 12 were waited for; matrix products, arithmetic and copies ran while one was open for 53% of the time, Pallas kernels for 0%

commit v1 on v0

v1 whole, which is shorter than its diff:
```python
import jax
import jax.numpy as jnp
from jax import lax
from jax.experimental import pallas as pl
from jax.experimental.pallas import tpu as pltpu
from jax.sharding import PartitionSpec as P

HEADS = 12
BUCKETS = 32
EPS = 1e-06
NEG = -1e30
F32 = jnp.float32
BF16 = jnp.bfloat16
MESH = pl.DeviceIdType.MESH
T = 512
D = 768
H = 384
FH = 1024
VMEM = pltpu.VMEM


def dotf(a, b):
    return jnp.dot(a, b, preferred_element_type=F32)


def dot_t(a, b):
    return lax.dot_general(a, b, (((1,), (1,)), ((), ())), preferred_element_type=F32)


def repeat(count, body):
    lax.fori_loop(0, count, lambda i, carry: (body(i), carry)[1], 0)


def tile(start, step, size):
    return pl.ds(pl.multiple_of(start * step, step), size)


def rms_scale(v):
    return lax.rsqrt(jnp.mean(v * v, axis=-1, keepdims=True) + EPS)


def norm_back(v, gain, upstream):
    r = rms_scale(v)
    scaled = gain * upstream
    gv = r * scaled - v * (r * r * r) * jnp.mean(scaled * v, axis=-1, keepdims=True)
    return gv, jnp.sum(upstream * v * r, axis=0, keepdims=True)


def layer_kernel(
    inp, segr, segc, table, gains,
    w_qkv, w_o, w_cq, w_ckv, w_co, w_g, w_u, w_d,
    mixed, input_grad, memory_grad, gains_grad, dist_grad,
    g_qkv, g_o, g_cq, g_ckv, g_co, g_g, g_u, g_d,
    full, na, nb, nc, qkv, att, x1, cq, mkv, catt, x2,
    bias, p_self, p_cross, hidden, gg, gu, gsend, grecv, gx2, gxb,
    gatt, gcq, gqkv, dk_t, dv_t, qt_s, gt_s, left_t, work,
    psend, precv, msend, late, gdsend,
    ssem, rsem,
):
    row = lax.axis_index("rows")
    seq = lax.axis_index("seq")
    x = lax.div(seq, 2)
    c = lax.rem(seq, 2)
    mate = (row, 2 * x + (1 - c))
    across = (row, lax.rem(seq + 2, 4))

    barrier = pltpu.get_barrier_semaphore()
    for peer in (mate, across):
        pl.semaphore_signal(barrier, inc=1, device_id=peer, device_id_type=MESH)
    pl.semaphore_wait(barrier, 2)

    started = []

    def remote(src, dst, slot, peer):
        copy = pltpu.make_async_remote_copy(
            src_ref=src, dst_ref=dst, send_sem=ssem.at[slot], recv_sem=rsem.at[slot],
            device_id=peer, device_id_type=MESH)
        copy.start()
        started.append(copy)
        return copy

    mine = tile(c, H, H)
    low = lax.broadcasted_iota(jnp.int32, (1, 128), 1) < 64
    masks = (low, jnp.logical_not(low))
    flip = (
        lax.broadcasted_iota(jnp.int32, (256, 256), 0)
        + lax.broadcasted_iota(jnp.int32, (256, 256), 1)
        == 255
    ).astype(BF16)

    own = tile(seq, 128, 128)
    other = tile(lax.rem(seq + 2, 4), 128, 128)
    to_across = remote(inp.at[:, 1 - x], full.at[:, own], 0, across)
    to_mate = remote(inp.at[:, x], full.at[:, own], 1, mate)
    for k in range(3):
        full[k, own] = inp[k, x]

    for qt in range(2):
        rows = slice(256 * qt, 256 * qt + 256)
        qpos = lax.broadcasted_iota(jnp.int32, (256, T), 0) + 256 * qt
        kpos = lax.broadcasted_iota(jnp.int32, (256, T), 1)
        allowed = (kpos <= qpos) & (segc[rows, :] == segr[...])
        work[0:256] = jnp.where(allowed, 0.0, NEG)

        def build(h):
            line = jnp.broadcast_to(table[pl.ds(h, 1), :], (256, T))
            line = pltpu.roll(line, 256 * qt, 1, stride=1, stride_axis=0)
            bias[h, rows] = (line + work[0:256]).astype(BF16)

        repeat(6, build)

    to_across.wait_recv()
    relay = remote(full.at[:, other], full.at[:, other], 2, mate)
    to_mate.wait_recv()
    relay.wait_recv()

    def norm(source, gain, dest):
        def part(i):
            chunk = tile(i, 128, 128)
            v = source(chunk)
            dest[chunk] = (v * rms_scale(v) * gains[gain : gain + 1]).astype(BF16)

        repeat(4, part)

    norm(lambda k: full[0, k].astype(F32), 0, na)

    def project_qkv(n):
        cols = tile(n, H, H)
        qkv[:, cols] = (dotf(na[...], w_qkv[:, cols]).astype(BF16) * jnp.where(n == 0, 0.125, 1.0)).astype(BF16)

    repeat(3, project_qkv)

    def attend(t, q, qo, k, ko, v, vo, bias_ref, probs, out):
        qc, kc, vc = tile(t + qo, 128, 128), tile(t + ko, 128, 128), tile(t + vo, 128, 128)
        oc = tile(t + 3 * c, 128, 128)
        for qt in range(2):
            rows = slice(256 * qt, 256 * qt + 256)
            nk = T if bias_ref is None else 256 * (qt + 1)
            q2, k2, v2 = q[rows, qc], k[0:nk, kc], v[0:nk, vc]
            outs = []
            for a in range(2):
                s = dot_t(jnp.where(masks[a], q2, jnp.zeros_like(q2)), k2)
                if bias_ref is not None:
                    s = s + bias_ref[2 * t + a, rows, 0:nk].astype(F32)
                e = jnp.exp(s - jnp.max(s, axis=-1, keepdims=True))
                prob = (e * (1.0 / jnp.sum(e, axis=-1, keepdims=True))).astype(BF16)
                probs[2 * t + a, rows, 0:nk] = prob
                outs.append(dotf(prob, v2))
            out[rows, oc] = jnp.where(low, outs[0], outs[1]).astype(BF16)

    def attend_back(t, q, qo, k, ko, v, vo, probs, out, causal, gq, gqo, gk, gko, gv, gvo):
        qc, kc, vc = tile(t + qo, 128, 128), tile(t + ko, 128, 128), tile(t + vo, 128, 128)
        oc, gc = tile(t + 3 * c, 128, 128), tile(t, 128, 128)
        qt_s[...] = q[:, qc].T
        gt_s[...] = gatt[:, gc].T
        for qt in (1, 0):
            rows = slice(256 * qt, 256 * qt + 256)
            nk = 256 * (qt + 1) if causal else T
            k2, v2 = k[0:nk, kc], v[0:nk, vc]
            g2 = gatt[rows, gc]
            both = g2.astype(F32) * out[rows, oc].astype(F32)
            outs = []
            for a in range(2):
                half = slice(64 * a, 64 * a + 64)
                delta = jnp.sum(jnp.where(masks[a], both, 0.0), axis=-1, keepdims=True)
                dp = dot_t(jnp.where(masks[a], g2, jnp.zeros_like(g2)), v2)
                prob = probs[2 * t + a, rows, 0:nk]
                ds = (prob.astype(F32) * (dp - delta)).astype(BF16)
                outs.append(dotf(ds, k2))
                dk = dotf(qt_s[half, rows], ds)
                dv = dotf(gt_s[half, rows], prob)
                if qt == 1:
                    dk_t[half, :] = dk
                    dv_t[half, :] = dv
                else:
                    dk_t[half, 0:nk] += dk
                    dv_t[half, 0:nk] += dv
                if causal:
                    band = slice(256 * a, 256 * a + 256)
                    if qt == 1:
                        work[band] = dotf(flip, ds)
                    else:
                        work[band, 256:T] += dotf(flip, ds)
                        turned = pltpu.roll(work[band], 0, 1, stride=1, stride_axis=0)
                        dist_grad[pl.ds(2 * t + a, 1), :] = jnp.sum(turned, axis=0, keepdims=True)
            gq[rows, tile(t + gqo, 128, 128)] = (jnp.where(low, outs[0], outs[1]) * 0.125).astype(BF16)
        gk[:, tile(t + gko, 128, 128)] = dk_t[...].T.astype(BF16)
        gv[:, tile(t + gvo, 128, 128)] = dv_t[...].T.astype(BF16)

    def send_head(ref, t, slot):
        cols = tile(t + 3 * c, 128, 128)
        return remote(ref.at[:, cols], ref.at[:, cols], slot + t, mate)

    def wait_all(copies):
        for copy in copies:
            copy.wait_recv()

    copies = []
    for t in range(3):
        attend(t, qkv, 0, qkv, 3, qkv, 6, bias, p_self, att)
        copies.append(send_head(att, t, 3))

    def project_memory(n):
        cols = tile(n, 256, 256)
        mkv[:, cols] = dotf(full[1], w_ckv[:, cols]).astype(BF16)

    repeat(3, project_memory)
    wait_all(copies)

    def first_residual(n):
        cols = tile(n, 256, 256)
        x1[:, cols] = full[0, :, cols].astype(F32) + dotf(att[...], w_o[:, cols])

    repeat(3, first_residual)
    norm(lambda k: x1[k], 1, nb)
    cq[...] = (dotf(nb[...], w_cq[:, mine]).astype(BF16) * 0.125).astype(BF16)

    copies = []
    for t in range(3):
        attend(t, cq, 0, mkv, 0, mkv, 3, None, p_cross, catt)
        copies.append(send_head(catt, t, 6))
    wait_all(copies)

    def second_residual(n):
        cols = tile(n, 256, 256)
        x2[:, cols] = x1[:, cols] + dotf(catt[...], w_co[:, cols])

    repeat(3, second_residual)
    norm(lambda k: x2[k], 2, nc)

    def feed(n):
        cols = tile(n, 256, 256)
        gate = dotf(nc[...], w_g[:, cols])
        up = dotf(nc[...], w_u[:, cols])
        back = dot_t(full[2], w_d[cols, :])
        square = gate * gate
        th = jnp.tanh(0.7978845608028654 * gate * (1.0 + 0.044715 * square))
        half = 0.5 * (1.0 + th)
        act = gate * half
        slope = half + 0.5 * gate * (1.0 - th * th) * (0.7978845608028654 * (1.0 + 0.134145 * square))
        hidden[:, cols] = (act * up).astype(BF16)
        gg[:, cols] = (back * up * slope).astype(BF16)
        gu[:, cols] = (back * act).astype(BF16)

    repeat(4, feed)

    gc_copies = []
    for n in range(3):
        cols = slice(256 * n, 256 * n + 256)
        gsend[:, cols] = (dot_t(gg[...], w_g[cols, :]) + dot_t(gu[...], w_u[cols, :])).astype(BF16)
        gc_copies.append(remote(gsend.at[:, cols], grecv.at[:, cols], 9 + n, mate))

    def pair_partial(product, buf_send, buf_recv, slot):
        def part(n):
            cols = tile(n, 256, 256)
            value = product(cols).astype(BF16)
            for b in range(4):
                buf_send[b, :, cols] = value[128 * b : 128 * b + 128]

        repeat(3, part)
        return [remote(buf_send.at[2 * k + (1 - c)], buf_recv.at[k], slot + k, mate) for k in range(2)]

    mix_copies = pair_partial(lambda k: dotf(hidden[...], w_d[:, k]), psend.at[0], precv.at[0], 12)

    def weight_grad(left, left_rows, grads):
        def turn(j):
            left_t[tile(j, 128, 128), :] = left(tile(j, 128, 128)).T

        repeat(left_rows // 128, turn)
        for grad, dest, count in grads:
            def part(n):
                dest(n, dotf(left_t[0:left_rows], grad(n)).astype(BF16))

            repeat(count, part)

    def into(ref):
        def put(n, value):
            ref[:, tile(n, 128, 128)] = value
        return put

    def cols_of(ref, first=0):
        return lambda n: ref[:, tile(n + first, 128, 128)]

    weight_grad(lambda j: nc[:, j], D, [(cols_of(gg), into(g_g), 8), (cols_of(gu), into(g_u), 8)])

    def put_own(n, value):
        g_d[tile(c, FH, FH), tile(n, 128, 128)] = value

    def put_mate(n, value):
        gdsend[:, tile(n, 128, 128)] = value

    weight_grad(lambda j: hidden[:, j], FH, [
        (lambda n: full[2, :, tile(n + 3 * (1 - c), 128, 128)], put_mate, 3),
        (lambda n: full[2, :, tile(n + 3 * c, 128, 128)], put_own, 3),
    ])
    gd_copy = remote(gdsend, g_d.at[tile(c, FH, FH)], 24, mate)

    wait_all(gc_copies)
    gains_grad[...] = jnp.zeros_like(gains_grad)

    def keep_gain(index, i, gain):
        gains_grad[index : index + 1] += jnp.where(lax.rem(i, 2) == c, gain, 0.0)

    def third(i):
        chunk = tile(i, 128, 128)
        upstream = gsend[chunk].astype(F32) + grecv[chunk].astype(F32)
        gv, gain = norm_back(x2[chunk], gains[2:3], upstream)
        total = full[2, chunk].astype(F32) + gv
        gx2[chunk] = total
        gxb[chunk] = total.astype(BF16)
        keep_gain(2, i, gain)

    repeat(4, third)
    gatt[...] = dot_t(gxb[...], w_co[mine, :]).astype(BF16)
    gmkv = grecv
    copies = []
    for t in range(3):
        attend_back(t, cq, 0, mkv, 0, mkv, 3, p_cross, catt, False, gcq, 3 * c, gmkv, 0, gmkv, 3)
        copies.append(send_head(gcq, t, 14))

    mem_copies = pair_partial(lambda k: dot_t(gmkv[...], w_ckv[k, :]), psend.at[1], precv.at[1], 17)

    wait_all(mix_copies)

    def mixed_block(k, chunk):
        return (x2[chunk] + psend[0, 2 * k + c].astype(F32) + precv[0, k].astype(F32)).astype(BF16)

    msend[0] = mixed_block(1 - x, other)
    mix_out = remote(msend.at[0], mixed.at[x], 19, across)
    mixed[x] = mixed_block(x, own)

    weight_grad(lambda j: catt[:, j], D, [(cols_of(gxb, 3 * c), into(g_co), 3)])
    wait_all(copies)

    def back_b(n):
        cols = tile(n, 256, 256)
        x2[:, cols] = dot_t(gcq[...], w_cq[cols, :])

    repeat(3, back_b)

    def second(i):
        chunk = tile(i, 128, 128)
        gv, gain = norm_back(x1[chunk], gains[1:2], x2[chunk])
        total = gx2[chunk] + gv
        gx2[chunk] = total
        gxb[chunk] = total.astype(BF16)
        keep_gain(1, i, gain)

    repeat(4, second)
    gatt[...] = dot_t(gxb[...], w_o[mine, :]).astype(BF16)
    for t in range(3):
        attend_back(t, qkv, 0, qkv, 3, qkv, 6, p_self, att, True, gqkv, 0, gqkv, 3, gqkv, 6)

    ig_copies = pair_partial(lambda k: dot_t(gqkv[...], w_qkv[k, :]), psend.at[2], precv.at[2], 21)

    weight_grad(lambda j: full[1, :, j], D, [(cols_of(gmkv), into(g_ckv), 6)])
    weight_grad(lambda j: nb[:, j], D, [(cols_of(gcq, 3 * c), into(g_cq), 3)])
    weight_grad(lambda j: att[:, j], D, [(cols_of(gxb, 3 * c), into(g_o), 3)])
    weight_grad(lambda j: na[:, j], D, [(cols_of(gqkv), into(g_qkv), 9)])

    wait_all(mem_copies)
    msend[1] = (psend[1, 2 * (1 - x) + c].astype(F32) + precv[1, 1 - x].astype(F32)).astype(BF16)
    mem_out = remote(msend.at[1], late.at[0], 20, across)
    memory_grad[x] = psend[1, 2 * x + c].astype(F32) + precv[1, x].astype(F32)

    wait_all(ig_copies)

    def first_block(k, chunk):
        upstream = psend[2, 2 * k + c].astype(F32) + precv[2, k].astype(F32)
        gv, gain = norm_back(full[0, chunk].astype(F32), gains[0:1], upstream)
        gains_grad[0:1] += gain
        return gx2[chunk] + gv

    msend[2] = first_block(1 - x, other).astype(BF16)
    ig_out = remote(msend.at[2], late.at[1], 23, across)
    input_grad[x] = first_block(x, own)

    mem_out.wait_recv()
    memory_grad[1 - x] = late[0].astype(F32)
    ig_out.wait_recv()
    input_grad[1 - x] = late[1].astype(F32)
    mix_out.wait_recv()
    gd_copy.wait_recv()
    for copy in started:
        copy.wait_send()


def layer(inp, segr, segc, table, gains, weights):
    def bf(*shape):
        return VMEM(shape, BF16)

    def fl(*shape):
        return VMEM(shape, F32)

    outs = [
        ((2, 128, D), BF16), ((2, 128, D), F32), ((2, 128, D), F32), ((8, D), F32), ((8, T), F32),
        ((D, 3 * H), BF16), ((D, H), BF16), ((D, H), BF16), ((D, D), BF16), ((D, H), BF16),
        ((D, FH), BF16), ((D, FH), BF16), ((2 * FH, H), BF16),
    ]
    whole = pl.BlockSpec(memory_space=pltpu.VMEM)
    return pl.pallas_call(
        layer_kernel,
        out_shape=[jax.ShapeDtypeStruct(s, d) for s, d in outs],
        in_specs=[whole] * (5 + len(weights)),
        out_specs=[whole] * len(outs),
        scratch_shapes=[
            bf(3, T, D), bf(T, D), bf(T, D), bf(T, D), bf(T, 3 * H), bf(T, D), fl(T, D), bf(T, H), bf(T, D),
            bf(T, D), fl(T, D),
            bf(6, T, T), bf(6, T, T), bf(6, T, T), bf(T, FH), bf(T, FH), bf(T, FH), bf(T, D), bf(T, D),
            fl(T, D), bf(T, D),
            bf(T, H), bf(T, D), bf(T, 3 * H), fl(128, T), fl(128, T), bf(128, T), bf(128, T),
            bf(FH, T), fl(T, T),
            bf(3, 4, 128, D), bf(3, 2, 128, D), bf(3, 128, D), bf(2, 128, D), bf(FH, H),
            pltpu.SemaphoreType.DMA((25,)), pltpu.SemaphoreType.DMA((25,)),
        ],
        compiler_params=pltpu.CompilerParams(
            collective_id=0, has_side_effects=True, vmem_limit_bytes=67043328),
        name="layer",
    )(inp, segr, segc, table, gains, *weights)


def to_plane(v, axis):
    axis = axis % v.ndim
    s = v.shape
    v = v.reshape(s[:axis] + (2, 2, 3, 64) + s[axis + 1 :])
    order = list(range(axis)) + [axis + 1, axis + 2, axis, axis + 3] + list(range(axis + 4, v.ndim))
    return v.transpose(order).reshape(s)


def from_plane(v, axis):
    axis = axis % v.ndim
    s = v.shape
    v = v.reshape(s[:axis] + (2, 3, 2, 64) + s[axis + 1 :])
    order = list(range(axis)) + [axis + 2, axis, axis + 1, axis + 3] + list(range(axis + 4, v.ndim))
    return v.transpose(order).reshape(s)


def ff_plane(v, axis):
    axis = axis % v.ndim
    s = v.shape
    v = v.reshape(s[:axis] + (2, 2, 512) + s[axis + 1 :])
    return jnp.swapaxes(v, axis, axis + 1).reshape(s)


def shards(
    layer_input, memory, output_grad, segments, buckets,
    self_query, self_key, self_value, self_output,
    cross_query, cross_key, cross_value, cross_output,
    gate_weight, up_weight, down_weight, norm_gains, position_bias,
):
    seq = lax.axis_index("seq")
    x, c = seq // 2, seq % 2
    mates = [[0, 2], [1, 3]]

    def whole(w):
        return lax.all_gather(lax.all_gather(w, "rows", axis=0, tiled=True), "seq", axis=1, tiled=True)

    def my_cols(w, width):
        return lax.dynamic_slice_in_dim(w, c * width, width, 1)

    square = jnp.stack([self_query, self_key, self_value, self_output, cross_query, cross_key, cross_value, cross_output])
    square = lax.all_gather(lax.all_gather(square, "rows", axis=1, tiled=True), "seq", axis=2, tiled=True)
    square = to_plane(to_plane(square, 1), 2)
    mine = lax.dynamic_slice_in_dim(square, c * H, H, 2)
    w_qkv = jnp.concatenate([mine[0], mine[1], mine[2]], axis=1)
    w_ckv = jnp.concatenate([mine[5], mine[6]], axis=1)
    w_g = my_cols(ff_plane(to_plane(whole(gate_weight), 0), 1), FH)
    w_u = my_cols(ff_plane(to_plane(whole(up_weight), 0), 1), FH)
    w_d = lax.dynamic_slice_in_dim(to_plane(ff_plane(whole(down_weight), 0), 1), c * FH, FH, 0)
    gains = to_plane(lax.all_gather(norm_gains, "rows", axis=1, tiled=True).astype(F32), 1)
    gains = jnp.pad(gains, ((0, 5), (0, 0)))

    inp = to_plane(jnp.stack([layer_input, memory, output_grad]), 3)
    seg = lax.dynamic_slice_in_dim(segments, x, 1, 0)
    turned = jnp.concatenate([buckets[:1], jnp.flip(buckets[1:])])
    ids = jnp.arange(BUCKETS, dtype=jnp.int32)
    onehot = (turned[None] == ids[:, None]).astype(BF16)
    table = lax.dot_general(position_bias, onehot, (((0,), (0,)), ((), ())), preferred_element_type=F32)
    table = lax.dynamic_index_in_dim(table.reshape(2, 2, 3, T), c, 1, keepdims=False)
    table = jnp.pad(table.transpose(1, 0, 2).reshape(6, T), ((0, 2), (0, 0)))

    (mixed, input_grad, memory_grad, gains_grad, dist_grad,
     g_qkv, g_o, g_cq, g_ckv, g_co, g_g, g_u, g_d) = layer(
        inp, seg, seg.reshape(T, 1), table, gains,
        (w_qkv, square[3], square[4], w_ckv, square[7], w_g, w_u, w_d))

    def own_part(grad):
        grad = lax.psum_scatter(grad, "rows", scatter_dimension=0, tiled=True)
        parts = grad.reshape(grad.shape[0], 2, grad.shape[1] // 2).astype(F32)
        kept = lax.dynamic_index_in_dim(parts, x, 1, keepdims=False)
        sent = lax.dynamic_index_in_dim(parts, 1 - x, 1, keepdims=False).astype(BF16)
        back = lax.ppermute(sent, "seq", [(0, 2), (2, 0), (1, 3), (3, 1)])
        return kept + back.astype(F32)

    def square_grad(grad):
        grad = from_plane(grad, 0)
        return own_part(grad.reshape(D, 3, 2, 64).transpose(0, 2, 1, 3).reshape(D, H))

    def wide_grad(grad):
        return own_part(from_plane(grad, 0))

    def down_grad(grad):
        grad = ff_plane(grad, 0)
        return own_part(grad.reshape(2048, 3, 2, 64).transpose(0, 2, 1, 3).reshape(2048, H))

    gains_grad = from_plane(gains_grad[:3], 1)
    rev = (jnp.flip(buckets)[:, None] == ids[None]).astype(F32)
    per_head = jnp.dot(dist_grad[:6], rev, precision=lax.Precision.HIGHEST)
    bias_grad = jnp.zeros((2, 2, 3, BUCKETS), F32)
    mine_grad = per_head.reshape(3, 2, BUCKETS).transpose(1, 0, 2)[:, None]
    bias_grad = lax.dynamic_update_slice_in_dim(bias_grad, mine_grad, c, 1).reshape(HEADS, BUCKETS).T
    bias_grad, gains_grad = lax.psum((bias_grad, gains_grad), ("rows", "seq"))
    width = D // lax.axis_size("rows")
    gains_own = lax.dynamic_slice_in_dim(gains_grad, lax.axis_index("rows") * width, width, 1)
    return (
        from_plane(mixed, 2), from_plane(input_grad, 2), from_plane(memory_grad, 2),
        square_grad(g_qkv[:, :H]), square_grad(g_qkv[:, H : 2 * H]), square_grad(g_qkv[:, 2 * H :]),
        square_grad(g_o), square_grad(g_cq), square_grad(g_ckv[:, :H]), square_grad(g_ckv[:, H:]),
        square_grad(g_co), wide_grad(g_g), wide_grad(g_u), down_grad(g_d),
        gains_own, bias_grad,
    )


def solution(mesh):
    tokens = P("rows", "seq", None)
    weight = P("rows", "seq")
    return jax.shard_map(
        shards,
        mesh=mesh,
        in_specs=(tokens, tokens, tokens, P("rows", None), P()) + (weight,) * 11 + (P(None, "rows"), P()),
        out_specs=(tokens,) * 3 + (weight,) * 11 + (P(None, "rows"), P()),
        check_vma=False,
    )
```

time: 1730 us -> 1230 us (0.71)
  local copies, waits for them, and re-layouts: 668 us -> 254 us
  waiting for transfers between devices: 317 us -> 652 us
  matrix products: 173 us -> 0.4 us
  blocking collectives: 333 us -> 169 us
  other arithmetic: 120 us -> 12.3 us
  Pallas kernels: 0 us -> 101 us
  starting transfers between devices: 86.8 us -> 14.8 us
    gather x2 -> x0, local copies, waits for them, and re-layouts: 408 us -> none  [shards(): bucket_ids = jnp.take(buckets, distance)]
    reduce_scatter x9 -> x11, waiting for transfers between devices: 300 us -> 610 us  [own_part(): grad = lax.psum_scatter(grad, 'rows', scatter_dimension=0, tiled=True)]
    dot_general x93 -> x2, matrix products: 173 us -> 0.4 us  [the longest x1 0.27 us: shards(): per_head = jnp.dot(dist_grad[:6], rev, precision=lax.Precision.HIGHEST)]
    all_gather x32 -> x4, blocking collectives: 292 us -> 129 us  [the longest x3 109 us: whole(): lax.all_gather(w, 'rows', axis=0, tiled=True)]
    unnamed x504 -> x96, local copies, waits for them, and re-layouts: 175 us -> 35.8 us
    pallas_call x0 -> x1, Pallas kernels: none -> 101 us  [layer(): pl.pallas_call(layer_kernel, out_shape=[jax.ShapeDtypeStruct(s, d) for s,...]
    unnamed x23 -> x0, other arithmetic: 101 us -> none
    all_to_all x22 -> x0, starting transfers between devices: 84.7 us -> none  [the longest x2 8.47 us: shards(): lax.all_to_all(grad_gate, 'seq', split_axis=2, concat_axis=1, tiled=True)]
  transfers between devices with their start and end apart: 54 -> 27, of which waited for: 12 -> 12; matrix products, arithmetic and copies ran while one was open for 53% -> 10% of each run, Pallas kernels for 0% -> 0%
where the time goes in v1:
time: 1230 us; the launch traced here: 1220 us
  waiting for transfers between devices  652 us (53%)
  local copies, waits for them, and re-layouts  254 us (21%)
  blocking collectives  169 us (14%)
  Pallas kernels  101 us (8%)
  between operations  15.2 us (1%)
  starting transfers between devices  14.8 us (1%)
  other arithmetic  12.3 us (1%)
    reduce_scatter x11, waiting for transfers between devices, own_part(): grad = lax.psum_scatter(grad, 'rows', scatter_dimension=0, tiled=True)  610 us
    all_gather x3, blocking collectives, whole(): lax.all_gather(w, 'rows', axis=0, tiled=True)  109 us
    pallas_call x1, Pallas kernels, layer(): pl.pallas_call(layer_kernel, out_shape=[jax.ShapeDtypeStruct(s, d) for s,...  101 us
    transpose x5, local copies, waits for them, and re-layouts, to_plane(): return v.transpose(order).reshape(s)  54 us
    psum x1, blocking collectives, shards(): bias_grad, gains_grad = lax.psum((bias_grad, gains_grad), ('rows', 'seq'))  40.7 us
    all_gather x1, waiting for transfers between devices, shards(): lax.all_gather(lax.all_gather(square, 'rows', axis=1, tiled=True), 'seq',...  40.5 us
    another operation x2, local copies, waits for them, and re-layouts, to_plane(): v = v.reshape(s[:axis] + (2, 2, 3, 64) + s[axis + 1:])  38.1 us
    unnamed x96, local copies, waits for them, and re-layouts  35.8 us
  transfers between devices with their start and end apart: 27, of which 12 were waited for; matrix products, arithmetic and copies ran while one was open for 10% of the time, Pallas kernels for 0%

profile of v1, /device:TPU:0, one launch (start us, length us, event | category | flops | bytes accessed | tf_op | source)
XLA Modules:
  0.0 1219.1 jit_solution(10918279219258359508)
XLA Ops:
  14.5 37.1 %all_gather.30 = bf16[768,512]{1,0:T(8,128)(2,1)} all-gather(bf16[96,512]{1,0:T(8,128)(2,1)} %param.31), channel_id=1, replica_groups=mesh['rows'=8,'seq'=4] {'rows'}, dimensions={0}, use_global_device_ids=true | all-gather | bytes 884736 | tf_op jit(solution)/shard_map/all_gather | solution.py:456
  51.7 36.5 %all_gather.32 = bf16[768,512]{1,0:T(8,128)(2,1)} all-gather(bf16[96,512]{1,0:T(8,128)(2,1)S(1)} %copy-done.19), channel_id=1, replica_groups=mesh['rows'=8,'seq'=4] {'rows'}, dimensions={0}, use_global_device_ids=true | all-gather | bytes 884736 | tf_op jit(solution)/shard_map/all_gather | solution.py:456
  88.3 34.9 %all_gather.34 = bf16[2048,192]{0,1:T(8,128)(2,1)} all-gather(bf16[256,192]{0,1:T(8,128)(2,1)S(1)} %copy-done.20), channel_id=1, replica_groups=mesh['rows'=8,'seq'=4] {'rows'}, dimensions={0}, use_global_device_ids=true | all-gather | bytes 884736 | tf_op jit(solution)/shard_map/all_gather | solution.py:456
  123.3 5.0 copy.314
  133.9 20.2 %all-gather = bf16[8,96,3]{1,2,0:T(4,128)(2,1)S(1)} all-gather(bf16[1,96,3]{1,2,0:T(4,128)(2,1)S(1)} %bitcast.328), channel_id=1, replica_groups=mesh['rows'=8,'seq'=4] {'rows'}, dimensions={0}, use_global_device_ids=true | all-gather | bytes 5184 | tf_op jit(solution)/shard_map/all_gather | solution.py:470
  158.3 4.0 reshape_reshape.40
  162.2 5.4 copy.323
  167.6 4.0 reshape.240
  173.8 4.0 reshape_reshape.41
  177.8 5.1 copy.325
  182.9 4.0 reshape.242
  186.9 5.3 reshape.243
  192.2 5.0 copy.450
  197.2 5.0 reshape_reshape.42
  206.5 3.5 constant_dynamic-slice_fusion.16
  210.0 40.5 %all-gather.9.cloned.1.call-done = bf16[8,768,768]{1,0,2:T(8,128)(2,1)} async-done(((bf16[8,768,192]{1,0,2:T(8,128)(2,1)}), bf16[8,768,768]{1,0,2:T(8,128)(2,1)}) %all-gather.9.cloned.1.call-update) | async-done | bytes 9437200 | tf_op jit(solution)/shard_map/all_gather | solution.py:462
  250.5 13.0 %copy.315 = bf16[8,768,768]{2,1,0:T(8,128)(2,1)} copy(bf16[8,768,768]{1,0,2:T(8,128)(2,1)} %all-gather.9.cloned.1.call-done) | data formatting | bytes 18874368 | tf_op jit(solution)/shard_map/all_gather | solution.py:462
  263.5 45.1 %copy.316 = bf16[8,2,3,2,64,768]{4,3,2,1,5,0:T(2,128)(2,1)} copy(bf16[8,2,3,2,64,768]{5,4,2,1,3,0:T(8,128)(2,1)} %bitcast.242) | data formatting | bytes 18874368 | tf_op jit(solution)/shard_map/transpose | solution.py:427
  308.6 33.1 %reshape_reshape.39 = bf16[8,768,2,2,3,64]{1,5,4,3,2,0:T(8,128)(2,1)} reshape(bf16[8,2,3,2,64,768]{4,3,2,1,5,0:T(2,128)(2,1)} %copy.316) | data formatting | bytes 18874368 | tf_op jit(solution)/shard_map/reshape;reshape | solution.py:425
  341.7 8.6 copy.317
  376.4 101.3 %layer.1 = (bf16[2,128,768]{2,1,0:T(8,128)(2,1)}, f32[2,128,768]{2,1,0:T(8,128)}, f32[2,128,768]{2,1,0:T(8,128)}, f32[8,768]{1,0:T(8,128)}, f32[8,512]{1,0:T(8,1...) custom-call(bf16[3,2,128,768]{3,2,1,0:T(8,128)(2,1)} %copy.329.inp, ...), custom_call_target="tpu_custom_call" | custom-call | tf_op jit(solution)/shard_map/layer/pallas_call | solution.py:401
  523.5 40.7 %all-reduce.2 = (f32[3,768]{1,0:T(4,128)S(1)}, f32[32,12]{0,1:T(8,128)}) all-reduce(f32[3,768]{1,0:T(4,128)S(1)} %reshape.274, f32[32,12]{0,1:T(8,128)S(1)} %bitcast.325), channel_id=1, replica_groups=mesh['rows'=8,'seq'=4] {'rows','seq'}, use_global_device_ids=true, to_apply=%region_11.12 | all-reduce | flops 2688 | bytes 21504 | tf_op jit(solution)/shard_map/psum | solution.py:512
  566.2 45.0 %reduce-scatter.46.cloned.1.call-done = bf16[96,384]{1,0:T(8,128)(2,1)} async-done(((bf16[768,384]{1,0:T(8,128)(2,1)}), bf16[96,384]{1,0:T(8,128)(2,1)}) %reduce-scatter.46.cloned.1.call-update) | async-done | bytes 73744 | tf_op jit(solution)/shard_map/reduce_scatter | solution.py:488
  612.6 63.8 %reduce-scatter.44.cloned.1.call-done = bf16[96,384]{1,0:T(8,128)(2,1)} async-done(((bf16[768,384]{1,0:T(8,128)(2,1)}), bf16[96,384]{1,0:T(8,128)(2,1)}) %reduce-scatter.44.cloned.1.call-update) | async-done | bytes 73744 | tf_op jit(solution)/shard_map/reduce_scatter | solution.py:488
  677.6 63.8 %reduce-scatter.42.cloned.1.call-done = bf16[96,384]{1,0:T(8,128)(2,1)} async-done(((bf16[768,384]{1,0:T(8,128)(2,1)}), bf16[96,384]{1,0:T(8,128)(2,1)}) %reduce-scatter.42.cloned.1.call-update) | async-done | bytes 73744 | tf_op jit(solution)/shard_map/reduce_scatter | solution.py:488
  744.3 62.0 %reduce-scatter.40.cloned.1.call-done = bf16[96,384]{1,0:T(8,128)(2,1)} async-done(((bf16[768,384]{1,0:T(8,128)(2,1)}), bf16[96,384]{1,0:T(8,128)(2,1)}) %reduce-scatter.40.cloned.1.call-update) | async-done | bytes 73744 | tf_op jit(solution)/shard_map/reduce_scatter | solution.py:488
  807.4 64.0 %reduce-scatter.38.cloned.1.call-done = bf16[96,384]{1,0:T(8,128)(2,1)} async-done(((bf16[768,384]{1,0:T(8,128)(2,1)}), bf16[96,384]{1,0:T(8,128)(2,1)}) %reduce-scatter.38.cloned.1.call-update) | async-done | bytes 73744 | tf_op jit(solution)/shard_map/reduce_scatter | solution.py:488
  872.5 63.8 %reduce-scatter.36.cloned.1.call-done = bf16[96,384]{1,0:T(8,128)(2,1)} async-done(((bf16[768,384]{1,0:T(8,128)(2,1)}), bf16[96,384]{1,0:T(8,128)(2,1)}) %reduce-scatter.36.cloned.1.call-update) | async-done | bytes 73744 | tf_op jit(solution)/shard_map/reduce_scatter | solution.py:488
  937.4 64.0 %reduce-scatter.34.cloned.1.call-done = bf16[96,384]{1,0:T(8,128)(2,1)} async-done(((bf16[768,384]{1,0:T(8,128)(2,1)}), bf16[96,384]{1,0:T(8,128)(2,1)}) %reduce-scatter.34.cloned.1.call-update) | async-done | bytes 73744 | tf_op jit(solution)/shard_map/reduce_scatter | solution.py:488
  1016.5 53.7 %reduce-scatter.32.cloned.1.call-done = bf16[256,384]{0,1:T(8,128)(2,1)} async-done(((bf16[2048,384]{0,1:T(8,128)(2,1)}), bf16[256,384]{0,1:T(8,128)(2,1)}) %reduce-scatter.32.cloned.1.call-update) | async-done | bytes 196624 | tf_op jit(solution)/shard_map/reduce_scatter | solution.py:488
  1072.7 65.1 %reduce-scatter.30.cloned.1.call-done = bf16[96,1024]{1,0:T(8,128)(2,1)} async-done(((bf16[768,1024]{1,0:T(8,128)(2,1)}), bf16[96,1024]{1,0:T(8,128)(2,1)}) %reduce-scatter.30.cloned.1.call-update) | async-done | bytes 196624 | tf_op jit(solution)/shard_map/reduce_scatter | solution.py:488
  1141.1 64.4 %reduce-scatter.28.cloned.1.call-done = bf16[96,1024]{1,0:T(8,128)(2,1)} async-done(((bf16[768,1024]{1,0:T(8,128)(2,1)}), bf16[96,1024]{1,0:T(8,128)(2,1)}) %reduce-scatter.28.cloned.1.call-update) | async-done | bytes 196624 | tf_op jit(solution)/shard_map/reduce_scatter | solution.py:488
  (281 shorter events, 133.0 us)
Async XLA Ops:
  7.2 44.5 %copy-start.19 = (bf16[96,512]{1,0:T(8,128)(2,1)S(1)}, bf16[96,512]{1,0:T(8,128)(2,1)}, u32[]{:S(2)}) copy-start(bf16[96,512]{1,0:T(8,128)(2,1)} %param.32) | copy-start | bytes 294916
  7.2 116.1 %all-gather.7.cloned.1.call-start = ((), (), s32[]{:S(2)}) async-start(), calls=%async_computation.11 | async-start | bytes 3538944 | tf_op jit(solution)/shard_map/all_gather | solution.py:462
  14.4 73.9 %copy-start.20 = (bf16[256,192]{0,1:T(8,128)(2,1)S(1)}, bf16[256,192]{0,1:T(8,128)(2,1)}, u32[]{:S(2)}) copy-start(bf16[256,192]{0,1:T(8,128)(2,1)} %param.33) | copy-start | bytes 294916
  14.4 141.7 %all-gather.11.cloned.1.call-start = ((), (), s32[]{:S(2)}) async-start(), calls=%async_computation.13 | async-start | bytes 3932160 | tf_op jit(solution)/shard_map/all_gather | solution.py:456
  51.7 120.0 %all-gather.13.cloned.1.call-start = ((), (), s32[]{:S(2)}) async-start(), calls=%async_computation.14 | async-start | bytes 3932160 | tf_op jit(solution)/shard_map/all_gather | solution.py:456
  88.3 98.7 %all-gather.15.cloned.1.call-start = ((), (), s32[]{:S(2)}) async-start(), calls=%async_computation.15 | async-start | bytes 3932160 | tf_op jit(solution)/shard_map/all_gather | solution.py:456
  123.2 127.3 %all-gather.9.cloned.1.call-start = ((), (), s32[]{:S(2)}) async-start(), calls=%async_computation.12 | async-start | bytes 11796480 | tf_op jit(solution)/shard_map/all_gather | solution.py:462
  128.3 3.3 copy-start.15
  128.3 3.5 copy-start.16
  128.3 3.7 copy-start.17
  128.3 436.6 %reduce-scatter.48.cloned.1.call-start = ((), (), s32[]{:S(2)}) async-start(), calls=%async_computation.26 | async-start | bytes 663552 | tf_op jit(solution)/shard_map/reduce_scatter | solution.py:488
  482.4 128.9 %reduce-scatter.46.cloned.1.call-start = ((), (), s32[]{:S(2)}) async-start(), calls=%async_computation.25 | async-start | bytes 663552 | tf_op jit(solution)/shard_map/reduce_scatter | solution.py:488
  486.1 190.2 %reduce-scatter.44.cloned.1.call-start = ((), (), s32[]{:S(2)}) async-start(), calls=%async_computation.24 | async-start | bytes 663552 | tf_op jit(solution)/shard_map/reduce_scatter | solution.py:488
  489.8 251.7 %reduce-scatter.42.cloned.1.call-start = ((), (), s32[]{:S(2)}) async-start(), calls=%async_computation.23 | async-start | bytes 663552 | tf_op jit(solution)/shard_map/reduce_scatter | solution.py:488
  493.4 312.9 %reduce-scatter.40.cloned.1.call-start = ((), (), s32[]{:S(2)}) async-start(), calls=%async_computation.22 | async-start | bytes 663552 | tf_op jit(solution)/shard_map/reduce_scatter | solution.py:488
  497.0 374.4 %reduce-scatter.38.cloned.1.call-start = ((), (), s32[]{:S(2)}) async-start(), calls=%async_computation.21 | async-start | bytes 663552 | tf_op jit(solution)/shard_map/reduce_scatter | solution.py:488
  502.2 434.1 %reduce-scatter.36.cloned.1.call-start = ((), (), s32[]{:S(2)}) async-start(), calls=%async_computation.20 | async-start | bytes 663552 | tf_op jit(solution)/shard_map/reduce_scatter | solution.py:488
  505.9 495.5 %reduce-scatter.34.cloned.1.call-start = ((), (), s32[]{:S(2)}) async-start(), calls=%async_computation.19 | async-start | bytes 663552 | tf_op jit(solution)/shard_map/reduce_scatter | solution.py:488
  509.5 560.7 %reduce-scatter.32.cloned.1.call-start = ((), (), s32[]{:S(2)}) async-start(), calls=%async_computation.18 | async-start | bytes 1769472 | tf_op jit(solution)/shard_map/reduce_scatter | solution.py:488
  513.7 624.1 %reduce-scatter.30.cloned.1.call-start = ((), (), s32[]{:S(2)}) async-start(), calls=%async_computation.17 | async-start | bytes 1769472 | tf_op jit(solution)/shard_map/reduce_scatter | solution.py:488
  516.5 689.0 %reduce-scatter.28.cloned.1.call-start = ((), (), s32[]{:S(2)}) async-start(), calls=%async_computation.16 | async-start | bytes 1769472 | tf_op jit(solution)/shard_map/reduce_scatter | solution.py:488
  742.7 264.9 %collective-permute-start.7 = (bf16[96,192]{1,0:T(8,128)(2,1)S(1)}, bf16[96,192]{1,0:T(8,128)(2,1)S(1)}, u32[]{:S(2)}, u32[]{:S(2)}) collective-permute-start(bf16[96,192]{1,0:T(8,128)(2,1)S(1)} %bitcast.317), channel_id=1, source_target_pairs={{0,2},{2,0},{1,3},{3,1},{4,6},{6,4},{5,7},{7,5},{8,10},{10,8},{9,1... | collective-permute-start | bytes 110600 | tf_op jit(solution)/shard_map/ppermute | solution.py:492
  1003.3 6.6 collective-permute-start.6
  1004.8 6.2 collective-permute-start.5
  1005.5 7.8 collective-permute-start.4
  1007.0 6.9 collective-permute-start.3
  1007.7 6.9 collective-permute-start.2
  1009.9 5.3 collective-permute-start.1
  1011.1 4.8 collective-permute-start
  1071.2 138.2 %collective-permute-start.10 = (bf16[256,192]{0,1:T(8,128)(2,1)S(1)}, bf16[256,192]{0,1:T(8,128)(2,1)S(1)}, u32[]{:S(2)}, u32[]{:S(2)}) collective-permute-start(bf16[256,192]{0,1:T(8,128)(2,1)S(1)} %fusion.2), channel_id=1, source_target_pairs={{0,2},{2,0},{1,3},{3,1},{4,6},{6,4},{5,7},{7,5},{8,10},{10,8},{9,1... | collective-permute-start | bytes 294920 | tf_op jit(solution)/shard_map/ppermute | solution.py:492
  1139.4 69.3 %collective-permute-start.9 = (bf16[96,512]{1,0:T(8,128)(2,1)S(1)}, bf16[96,512]{1,0:T(8,128)(2,1)S(1)}, u32[]{:S(2)}, u32[]{:S(2)}) collective-permute-start(bf16[96,512]{1,0:T(8,128)(2,1)S(1)} %bitcast.313), channel_id=1, source_target_pairs={{0,2},{2,0},{1,3},{3,1},{4,6},{6,4},{5,7},{7,5},{8,10},{10,8},{9,1... | collective-permute-start | bytes 294920 | tf_op jit(solution)/shard_map/ppermute | solution.py:492
  1207.0 4.7 collective-permute-start.8
  (23 other events, 40.3 us)
Sparse Core Ops, SparseCore 0:
  14.5 82.3 all-gather.6
  98.5 26.2 all-gather.10
  126.4 28.4 all-gather.12
  156.3 28.4 all-gather.14
  186.3 64.2 all-gather.8
  482.5 63.7 reduce-scatter.47
  549.6 61.6 reduce-scatter.45
  614.5 61.7 reduce-scatter.43
  679.6 61.7 reduce-scatter.41
  744.6 61.7 reduce-scatter.39
  809.6 61.7 reduce-scatter.37
  874.5 61.7 reduce-scatter.35
  939.6 61.7 reduce-scatter.33
  1004.7 65.4 reduce-scatter.31
  1073.5 64.3 reduce-scatter.29
  1141.1 64.3 reduce-scatter.27

commit v2 on v1

v2 whole, which is shorter than its diff:
```python
import jax
import jax.numpy as jnp
from jax import lax
from jax.experimental import pallas as pl
from jax.experimental.pallas import tpu as pltpu
from jax.sharding import PartitionSpec as P

HEADS = 12
BUCKETS = 32
EPS = 1e-06
NEG = -1e30
F32 = jnp.float32
BF16 = jnp.bfloat16
MESH = pl.DeviceIdType.MESH
T = 512
D = 768
H = 384
FH = 1024
VMEM = pltpu.VMEM


def dotf(a, b):
    return jnp.dot(a, b, preferred_element_type=F32)


def dot_t(a, b):
    return lax.dot_general(a, b, (((1,), (1,)), ((), ())), preferred_element_type=F32)


def repeat(count, body):
    lax.fori_loop(0, count, lambda i, carry: (body(i), carry)[1], 0)


def tile(start, step, size):
    return pl.ds(pl.multiple_of(start * step, step), size)


def rms_scale(v):
    return lax.rsqrt(jnp.mean(v * v, axis=-1, keepdims=True) + EPS)


def norm_back(v, gain, upstream):
    r = rms_scale(v)
    scaled = gain * upstream
    gv = r * scaled - v * (r * r * r) * jnp.mean(scaled * v, axis=-1, keepdims=True)
    return gv, jnp.sum(upstream * v * r, axis=0, keepdims=True)


def roll_half(v):
    return pltpu.roll(v, 64, 1)


def low_lanes():
    return lax.broadcasted_iota(jnp.int32, (1, 128), 1) < 64


def sliced_order(tiles):
    low = low_lanes()
    out = []
    for n in range(6):
        a, b = tiles[n // 2], tiles[n // 2 + 3]
        out.append(jnp.where(low, a, roll_half(b)) if n % 2 == 0 else jnp.where(low, roll_half(a), b))
    return out


def natural_order(tiles):
    low = low_lanes()
    out = [jnp.where(low, tiles[2 * k], roll_half(tiles[2 * k + 1])) for k in range(3)]
    return out + [jnp.where(low, roll_half(tiles[2 * k]), tiles[2 * k + 1]) for k in range(3)]


def lane_tiles(v):
    return [v[:, 128 * n : 128 * n + 128] for n in range(v.shape[1] // 128)]


def layer_kernel(
    in_x, in_m, in_g, segments, buckets, pos_bias, w_in, wd_in,
    mixed, input_grad, memory_grad, small, gw, gwd,
    w, wd,    w_o, w_cq, w_co, w_d, gains, table, dist_grad, full, ffb, na, qkv, att, attn, x1, cq, mkv, catt, cattn, x2,
    bias, p_self, hidden, gg, gu, gsend, grecv, gx2, gxb,
    gcq, dk_t, dv_t, qt_s, gt_s, left_t, work,
    psend, precv, msend, late, gdsend,
    ssem, rsem,
):
    p_cross = bias
    nb = nc = na
    gatt = hidden
    row = lax.axis_index("rows")
    seq = lax.axis_index("seq")
    x = lax.div(seq, 2)
    c = lax.rem(seq, 2)
    mate = (row, 2 * x + (1 - c))
    across = (row, lax.rem(seq + 2, 4))

    barrier = pltpu.get_barrier_semaphore()
    for peer in (mate, across):
        pl.semaphore_signal(barrier, inc=1, device_id=peer, device_id_type=MESH)
    pl.semaphore_wait(barrier, 2)

    started = []

    def remote(src, dst, slot, peer):
        copy = pltpu.make_async_remote_copy(
            src_ref=src, dst_ref=dst, send_sem=ssem.at[slot], recv_sem=rsem.at[slot],
            device_id=peer, device_id_type=MESH)
        copy.start()
        started.append(copy)
        return copy

    mine = tile(c, H, H)
    low = lax.broadcasted_iota(jnp.int32, (1, 128), 1) < 64
    masks = (low, jnp.logical_not(low))
    flip = (
        lax.broadcasted_iota(jnp.int32, (256, 256), 0)
        + lax.broadcasted_iota(jnp.int32, (256, 256), 1)
        == 255
    ).astype(BF16)

    own = tile(seq, 128, 128)
    other = tile(lax.rem(seq + 2, 4), 128, 128)
    dist_grad[...] = jnp.zeros_like(dist_grad)
    to_across, to_mate = [], []
    for k, block in enumerate((in_x, in_m, in_g)):
        to_across.append(remote(block.at[1 - x], full.at[k, own], 25 + k, across))
        to_mate.append(remote(block.at[x], full.at[k, own], 28 + k, mate))
        full[k, own] = block[x]

    loads = [
        pltpu.make_async_copy(w_in, w, ssem.at[40]), pltpu.make_async_copy(wd_in, wd, ssem.at[41])]
    for copy in loads:
        copy.start()
    for copy in loads:
        copy.wait()

    def separate(first, second, ref, lanes, rows_at, count):
        def part(i):
            at = tile(i, 128, 128) if rows_at is None else rows_at(i)
            a, b = ref[0, at, lanes].astype(F32), ref[1, at, lanes].astype(F32)
            first(at, jnp.where(low, a, b).astype(BF16))
            second(at, roll_half(jnp.where(low, b, a)).astype(BF16))

        repeat(count, part)

    def store(ref, lead, lanes):
        def put(at, value):
            ref[lead, at, lanes] = value
        return put

    for t in range(12):
        lanes = slice(128 * t, 128 * t + 128)
        inside = slice(128 * (t % 3), 128 * (t % 3) + 128)
        first, second = store(w, 0, lanes), store(w, 1, lanes)
        if t // 3 == 1:
            second = store(w_cq, c, inside)
        if t // 3 == 3:
            first, second = store(w_o, c, inside), store(w_co, c, inside)
        separate(first, second, w, lanes, None, 6)

    halves = []
    for k, ref in enumerate((w_o, w_cq, w_co)):
        halves.append(remote(ref.at[c], ref.at[c], 31 + k, mate))

    for t in range(3):
        lanes = slice(128 * t, 128 * t + 128)

        def part(i):
            at = tile(i, 128, 128)
            a, b = wd[0, at, lanes].astype(F32), wd[1, at, lanes].astype(F32)
            wd[0, at, lanes] = jnp.where(low, a, b).astype(BF16)
            wd[1, at, lanes] = roll_half(jnp.where(low, b, a)).astype(BF16)

        repeat(8, part)
    for xs in range(2):
        for b in range(2):
            piece = wd.at[b, tile((1 - c) + 2 * xs, 256, 256)]
            halves.append(remote(piece, w_d.at[c, 2 * xs + b], 34 + 2 * xs + b, mate))
            w_d[c, 2 * xs + b] = wd[b, tile(c + 2 * xs, 256, 256)]

    gains[...] = w[0, :, 2560:2688].astype(F32).T[0:8]
    hot = (lax.broadcasted_iota(jnp.int32, (BUCKETS, T), 0) == buckets[...]).astype(BF16)
    by_distance = lax.dot_general(pos_bias[...], hot, (((0,), (0,)), ((), ())), preferred_element_type=F32)
    total = lax.broadcasted_iota(jnp.int32, (T, T), 0) + lax.broadcasted_iota(jnp.int32, (T, T), 1)
    mirror = ((total == 0) | (total == T)).astype(BF16)
    work[0:HEADS] = dotf(by_distance.astype(BF16), mirror)
    for t in range(3):
        for a in range(2):
            table[2 * t + a : 2 * t + a + 1] = work[pl.ds(3 * (2 * a + c) + t, 1), :]
    seg_row = segments[pl.ds(x, 1), :]
    seg_col = jnp.broadcast_to(seg_row.astype(F32), (128, T)).T[:, 0:1].astype(jnp.int32)

    for qt in range(2):
        rows = slice(256 * qt, 256 * qt + 256)
        qpos = lax.broadcasted_iota(jnp.int32, (256, T), 0) + 256 * qt
        kpos = lax.broadcasted_iota(jnp.int32, (256, T), 1)
        allowed = (kpos <= qpos) & (seg_col[rows, :] == seg_row)
        work[0:256] = jnp.where(allowed, 0.0, NEG)

        def build(h):
            line = jnp.broadcast_to(table[pl.ds(h, 1), :], (256, T))
            line = pltpu.roll(line, 256 * qt, 1, stride=1, stride_axis=0)
            bias[h, rows] = (line + work[0:256]).astype(BF16)

        repeat(6, build)

    relays = []
    for k in range(3):
        to_across[k].wait_recv()
        relays.append(remote(full.at[k, other], full.at[k, other], k, mate))
    for k in range(3):
        to_mate[k].wait_recv()
        relays[k].wait_recv()

    def order_grad(i):
        chunk = tile(i, 128, 128)
        for n, value in enumerate(sliced_order(lane_tiles(full[2, chunk].astype(F32)))):
            ffb[chunk, 128 * n : 128 * n + 128] = value.astype(BF16)

    repeat(4, order_grad)

    def norm(source, gain, dest):
        def part(i):
            chunk = tile(i, 128, 128)
            v = source(chunk)
            dest[chunk] = (v * rms_scale(v) * gains[gain : gain + 1]).astype(BF16)

        repeat(4, part)

    norm(lambda k: full[0, k].astype(F32), 0, na)

    qkv[:, 0:H] = (dotf(na[...], w[0, :, 0:H]).astype(BF16) * 0.125).astype(BF16)
    qkv[:, H : 2 * H] = dotf(na[...], w[1, :, 0:H]).astype(BF16)
    qkv[:, 2 * H :] = dotf(na[...], w[0, :, H : 2 * H]).astype(BF16)

    def attend(t, q, qo, k, ko, v, vo, bias_ref, probs, out):
        qc, kc, vc = tile(t + qo, 128, 128), tile(t + ko, 128, 128), tile(t + vo, 128, 128)
        oc = tile(t + 3 * c, 128, 128)
        for qt in range(2):
            rows = slice(256 * qt, 256 * qt + 256)
            nk = T if bias_ref is None else 256 * (qt + 1)
            q2, k2, v2 = q[rows, qc], k[0:nk, kc], v[0:nk, vc]
            outs = []
            for a in range(2):
                s = dot_t(jnp.where(masks[a], q2, jnp.zeros_like(q2)), k2)
                if bias_ref is not None:
                    s = s + bias_ref[2 * t + a, rows, 0:nk].astype(F32)
                e = jnp.exp(s - jnp.max(s, axis=-1, keepdims=True))
                prob = (e * (1.0 / jnp.sum(e, axis=-1, keepdims=True))).astype(BF16)
                probs[2 * t + a, rows, 0:nk] = prob
                outs.append(dotf(prob, v2))
            out[rows, oc] = jnp.where(low, outs[0], outs[1]).astype(BF16)

    def attend_back(t, q, qo, k, ko, v, vo, probs, out, causal, gq, gqo, gk, gko, gv, gvo):
        qc, kc, vc = tile(t + qo, 128, 128), tile(t + ko, 128, 128), tile(t + vo, 128, 128)
        oc, gc = tile(t + 3 * c, 128, 128), tile(t, 128, 128)
        qt_s[...] = q[:, qc].T
        gt_s[...] = gatt[:, gc].T
        for qt in (1, 0):
            rows = slice(256 * qt, 256 * qt + 256)
            nk = 256 * (qt + 1) if causal else T
            k2, v2 = k[0:nk, kc], v[0:nk, vc]
            g2 = gatt[rows, gc]
            both = g2.astype(F32) * out[rows, oc].astype(F32)
            outs = []
            for a in range(2):
                half = slice(64 * a, 64 * a + 64)
                delta = jnp.sum(jnp.where(masks[a], both, 0.0), axis=-1, keepdims=True)
                dp = dot_t(jnp.where(masks[a], g2, jnp.zeros_like(g2)), v2)
                prob = probs[2 * t + a, rows, 0:nk]
                ds = (prob.astype(F32) * (dp - delta)).astype(BF16)
                outs.append(dotf(ds, k2))
                dk = dotf(qt_s[half, rows], ds)
                dv = dotf(gt_s[half, rows], prob)
                if qt == 1:
                    dk_t[half, :] = dk
                    dv_t[half, :] = dv
                else:
                    dk_t[half, 0:nk] += dk
                    dv_t[half, 0:nk] += dv
                if causal:
                    band = slice(256 * a, 256 * a + 256)
                    if qt == 1:
                        work[band] = dotf(flip, ds)
                    else:
                        work[band, 256:T] += dotf(flip, ds)
                        turned = pltpu.roll(work[band], 0, 1, stride=1, stride_axis=0)
                        dist_grad[pl.ds(2 * t + a, 1), :] = jnp.sum(turned, axis=0, keepdims=True)
            gq[rows, tile(t + gqo, 128, 128)] = (jnp.where(low, outs[0], outs[1]) * 0.125).astype(BF16)
        gk[:, tile(t + gko, 128, 128)] = dk_t[...].T.astype(BF16)
        gv[:, tile(t + gvo, 128, 128)] = dv_t[...].T.astype(BF16)

    def send_head(ref, t, slot):
        cols = tile(t + 3 * c, 128, 128)
        return remote(ref.at[:, cols], ref.at[:, cols], slot + t, mate)

    def wait_all(copies):
        for copy in copies:
            copy.wait_recv()

    copies = []
    for t in range(3):
        attend(t, qkv, 0, qkv, 3, qkv, 6, bias, p_self, att)
        copies.append(send_head(att, t, 3))

    for k in range(2):
        mkv[:, H * k : H * k + H] = dotf(full[1], w[k, :, 2 * H : 3 * H]).astype(BF16)
    wait_all(halves)
    wait_all(copies)

    def natural_heads(source, dest):
        def part(i):
            chunk = tile(i, 128, 128)
            for n, value in enumerate(natural_order(lane_tiles(source[chunk].astype(F32)))):
                dest[chunk, 128 * n : 128 * n + 128] = value.astype(BF16)

        repeat(4, part)

    def residual(before, heads, weight, dest):
        def part(i):
            chunk = tile(i, 256, 256)
            parts = lane_tiles(dotf(heads[chunk], weight[0])) + lane_tiles(dotf(heads[chunk], weight[1]))
            for n, value in enumerate(natural_order(parts)):
                cols = slice(128 * n, 128 * n + 128)
                dest[chunk, cols] = before(chunk, cols) + value

        repeat(2, part)

    natural_heads(att, attn)
    residual(lambda r, k: full[0, r, k].astype(F32), attn, w_o, x1)
    norm(lambda k: x1[k], 1, nb)
    cq[...] = (dotf(nb[...], w_cq[c]).astype(BF16) * 0.125).astype(BF16)

    copies = []
    for t in range(3):
        attend(t, cq, 0, mkv, 0, mkv, 3, None, p_cross, catt)
        copies.append(send_head(catt, t, 6))
    wait_all(copies)

    natural_heads(catt, cattn)
    residual(lambda r, k: x1[r, k], cattn, w_co, x2)
    norm(lambda k: x2[k], 2, nc)

    def feed(n):
        cols = tile(n, 256, 256)
        xs, b = lax.div(n, 2), lax.rem(n, 2)
        gate = dotf(nc[...], w[xs, :, tile(6 + b, 256, 256)])
        up = dotf(nc[...], w[xs, :, tile(8 + b, 256, 256)])
        back = dot_t(ffb[:, 0:H], w_d[0, n]) + dot_t(ffb[:, H:], w_d[1, n])
        square = gate * gate
        th = jnp.tanh(0.7978845608028654 * gate * (1.0 + 0.044715 * square))
        half = 0.5 * (1.0 + th)
        act = gate * half
        slope = half + 0.5 * gate * (1.0 - th * th) * (0.7978845608028654 * (1.0 + 0.134145 * square))
        hidden[:, cols] = (act * up).astype(BF16)
        gg[:, cols] = (back * up * slope).astype(BF16)
        gu[:, cols] = (back * act).astype(BF16)

    repeat(4, feed)

    gc_copies = []
    for n in range(3):
        cols = slice(256 * n, 256 * n + 256)
        part = dot_t(gg[:, 0:512], w[0, cols, 1536:2048]) + dot_t(gu[:, 0:512], w[0, cols, 2048:2560])
        part = part + dot_t(gg[:, 512:], w[1, cols, 1536:2048]) + dot_t(gu[:, 512:], w[1, cols, 2048:2560])
        gsend[:, cols] = part.astype(BF16)
        gc_copies.append(remote(gsend.at[:, cols], grecv.at[:, cols], 9 + n, mate))

    def pair_partial(product, buf_send, buf_recv, slot):
        def part(n):
            cols = tile(n, 256, 256)
            value = product(cols).astype(BF16)
            for b in range(4):
                buf_send[b, :, cols] = value[128 * b : 128 * b + 128]

        if product is not None:
            repeat(3, part)
        return [remote(buf_send.at[2 * k + (1 - c)], buf_recv.at[k], slot + k, mate) for k in range(2)]

    def down(b):
        chunk = tile(b, 128, 128)
        parts = []
        for p in range(2):
            total = dotf(hidden[chunk, 0:256], w_d[p, 0])
            for n in range(1, 4):
                total = total + dotf(hidden[chunk, 256 * n : 256 * n + 256], w_d[p, n])
            parts = parts + lane_tiles(total)
        for n, value in enumerate(natural_order(parts)):
            psend[0, b, :, 128 * n : 128 * n + 128] = value.astype(BF16)

    repeat(4, down)
    mix_copies = pair_partial(None, psend.at[0], precv.at[0], 12)

    def weight_grad(left, left_rows, grads):
        def turn(j):
            left_t[tile(j, 128, 128), :] = left(tile(j, 128, 128)).T

        repeat(left_rows // 128, turn)
        for grad, dest, count in grads:
            def part(n):
                dest(n, dotf(left_t[0:left_rows], grad(n)))

            repeat(count, part)

    def into(lead_of, first):
        def put(n, value):
            gw[lead_of(n), :, tile(first(n), 128, 128)] = value.astype(BF16)
        return put

    def pack_first(value, a, b):
        return jnp.where(low, value, a.astype(F32)).astype(BF16), jnp.where(low, b.astype(F32), value).astype(BF16)

    def pack_second(value, a, b):
        value = roll_half(value)
        return jnp.where(low, a.astype(F32), value).astype(BF16), jnp.where(low, value, b.astype(F32)).astype(BF16)

    def into_pair(group, pack):
        def put(n, value):
            cols = tile(n + 3 * group, 128, 128)
            gw[0, :, cols], gw[1, :, cols] = pack(value, gw[0, :, cols], gw[1, :, cols])
        return put

    def cols_of(ref, first=0):
        return lambda n: ref[:, tile(n + first, 128, 128)]

    weight_grad(lambda j: nc[:, j], D, [
        (cols_of(gg), into(lambda n: lax.div(n, 4), lambda n: 12 + lax.rem(n, 4)), 8),
        (cols_of(gu), into(lambda n: lax.div(n, 4), lambda n: 16 + lax.rem(n, 4)), 8),
    ])

    def put_down(half):
        def put(n, value):
            cols = tile(n, 128, 128)
            for xs in range(2):
                top = value[512 * xs : 512 * xs + 256]
                bottom = roll_half(value[512 * xs + 256 : 512 * xs + 512])
                a, b = jnp.where(low, top, bottom).astype(BF16), jnp.where(low, bottom, top).astype(BF16)
                if half:
                    rows = tile(c + 2 * xs, 256, 256)
                    gwd[0, rows, cols] = a
                    gwd[1, rows, cols] = b
                else:
                    gdsend[xs, 0, :, cols] = a
                    gdsend[xs, 1, :, cols] = b
        return put

    weight_grad(lambda j: hidden[:, j], FH, [
        (lambda n: ffb[:, tile(n + 3 * (1 - c), 128, 128)], put_down(False), 3),
        (lambda n: ffb[:, tile(n + 3 * c, 128, 128)], put_down(True), 3),
    ])
    gd_copies = [
        remote(gdsend.at[xs], gwd.at[:, tile(c + 2 * xs, 256, 256)], 38 + xs, mate) for xs in range(2)
    ]

    wait_all(gc_copies)
    small[...] = jnp.zeros_like(small)

    def keep_gain(index, i, gain):
        small[index : index + 1, 0:D] += jnp.where(lax.rem(i, 2) == c, gain, 0.0)

    def keep_sliced(chunk, total):
        for n, value in enumerate(sliced_order(lane_tiles(total))):
            gxb[chunk, 128 * n : 128 * n + 128] = value.astype(BF16)

    def back_heads(weight):
        for t in range(3):
            first, second = tile(3 * c + t, 64, 64), tile(3 * c + t + 6, 64, 64)
            part = None
            for p in range(2):
                rows = jnp.concatenate([weight[p, first], weight[p, second]], axis=0)
                term = dot_t(gxb[:, H * p : H * p + H], rows)
                part = term if part is None else part + term
            gatt[:, 128 * t : 128 * t + 128] = part.astype(BF16)

    def third(i):
        chunk = tile(i, 128, 128)
        upstream = gsend[chunk].astype(F32) + grecv[chunk].astype(F32)
        gv, gain = norm_back(x2[chunk], gains[2:3], upstream)
        total = full[2, chunk].astype(F32) + gv
        gx2[chunk] = total
        keep_sliced(chunk, total)
        keep_gain(2, i, gain)

    repeat(4, third)
    back_heads(w_co)
    gmkv = grecv
    copies = []
    for t in range(3):
        attend_back(t, cq, 0, mkv, 0, mkv, 3, p_cross, catt, False, gcq, 3 * c, gmkv, 0, gmkv, 3)
        copies.append(send_head(gcq, t, 14))

    mem_copies = pair_partial(lambda k: dot_t(gmkv[:, 0:H], w[0, k, 2 * H : 3 * H]) + dot_t(gmkv[:, H:], w[1, k, 2 * H : 3 * H]), psend.at[1], precv.at[1], 17)

    wait_all(mix_copies)

    def mixed_block(k, chunk):
        return (x2[chunk] + psend[0, 2 * k + c].astype(F32) + precv[0, k].astype(F32)).astype(BF16)

    msend[0] = mixed_block(1 - x, other)
    mix_out = remote(msend.at[0], mixed.at[x], 19, across)
    mixed[x] = mixed_block(x, own)

    weight_grad(lambda j: cattn[:, j], D, [(cols_of(gxb, 3 * c), into_pair(3, pack_second), 3)])
    wait_all(copies)

    def back_b(n):
        cols = tile(n, 256, 256)
        x2[:, cols] = dot_t(gcq[:, 0:H], w_cq[0, cols]) + dot_t(gcq[:, H:], w_cq[1, cols])

    repeat(3, back_b)

    def second(i):
        chunk = tile(i, 128, 128)
        gv, gain = norm_back(x1[chunk], gains[1:2], x2[chunk])
        total = gx2[chunk] + gv
        gx2[chunk] = total
        keep_sliced(chunk, total)
        keep_gain(1, i, gain)

    repeat(4, second)
    back_heads(w_o)
    for t in range(3):
        attend_back(t, qkv, 0, qkv, 3, qkv, 6, p_self, att, True, gg, 0, gg, 3, gu, 0)

    def back_a(k):
        part = dot_t(gg[:, 0:H], w[0, k, 0:H]) + dot_t(gg[:, H : 2 * H], w[1, k, 0:H])
        return part + dot_t(gu[:, 0:H], w[0, k, H : 2 * H])

    ig_copies = pair_partial(back_a, psend.at[2], precv.at[2], 21)

    weight_grad(lambda j: full[1, :, j], D, [
        (cols_of(gmkv), into_pair(2, pack_first), 3), (cols_of(gmkv, 3), into_pair(2, pack_second), 3)])
    norm(lambda k: x1[k], 1, nb)
    weight_grad(lambda j: nb[:, j], D, [(cols_of(gcq, 3 * c), into_pair(1, pack_second), 3)])
    weight_grad(lambda j: attn[:, j], D, [(cols_of(gxb, 3 * c), into_pair(3, pack_first), 3)])
    norm(lambda k: full[0, k].astype(F32), 0, na)
    weight_grad(lambda j: na[:, j], D, [
        (cols_of(gg), into_pair(0, pack_first), 3), (cols_of(gg, 3), into_pair(0, pack_second), 3),
        (cols_of(gu), into_pair(1, pack_first), 3)])

    flipped = (
        lax.broadcasted_iota(jnp.int32, (T, T), 0) + lax.broadcasted_iota(jnp.int32, (T, T), 1) == T - 1
    ).astype(F32)
    by_bucket = (
        jnp.broadcast_to(buckets[...], (128, T)) == lax.broadcasted_iota(jnp.int32, (128, T), 0)
    ).astype(F32)
    high = lax.Precision.HIGHEST
    distances = jnp.dot(dist_grad[...], flipped, precision=high, preferred_element_type=F32)
    per_head = lax.dot_general(
        distances, by_bucket, (((1,), (1,)), ((), ())), precision=high, preferred_element_type=F32)
    for t in range(3):
        for a in range(2):
            here = lax.broadcasted_iota(jnp.int32, (16, 128), 0) == 3 * (2 * a + c) + t
            small[:, D:] += jnp.where(here, per_head[2 * t + a : 2 * t + a + 1], 0.0)

    wait_all(mem_copies)
    msend[1] = (psend[1, 2 * (1 - x) + c].astype(F32) + precv[1, 1 - x].astype(F32)).astype(BF16)
    mem_out = remote(msend.at[1], late.at[0], 20, across)
    memory_grad[x] = psend[1, 2 * x + c].astype(F32) + precv[1, x].astype(F32)

    wait_all(ig_copies)

    def first_block(k, chunk):
        upstream = psend[2, 2 * k + c].astype(F32) + precv[2, k].astype(F32)
        gv, gain = norm_back(full[0, chunk].astype(F32), gains[0:1], upstream)
        small[0:1, 0:D] += gain
        return gx2[chunk] + gv

    msend[2] = first_block(1 - x, other).astype(BF16)
    ig_out = remote(msend.at[2], late.at[1], 23, across)
    input_grad[x] = first_block(x, own)

    mem_out.wait_recv()
    memory_grad[1 - x] = late[0].astype(F32)
    ig_out.wait_recv()
    input_grad[1 - x] = late[1].astype(F32)
    mix_out.wait_recv()
    wait_all(gd_copies)
    for copy in started:
        copy.wait_send()


def layer(blocks, segments, buckets, pos_bias, w, wd):
    def bf(*shape):
        return VMEM(shape, BF16)

    def fl(*shape):
        return VMEM(shape, F32)

    outs = [
        ((2, 128, D), BF16), ((2, 128, D), F32), ((2, 128, D), F32), ((16, D + 128), F32),
        ((2, D, 2560), BF16), ((2, FH, H), BF16),
    ]
    whole = pl.BlockSpec(memory_space=pltpu.VMEM)
    return pl.pallas_call(
        layer_kernel,
        out_shape=[jax.ShapeDtypeStruct(s, d) for s, d in outs],
        in_specs=[whole] * 6 + [pl.BlockSpec(memory_space=pl.ANY)] * 2,
        out_specs=[whole] * len(outs),
        scratch_shapes=[
            bf(2, D, 2688), bf(2, FH, H),
            bf(2, D, H), bf(2, D, H), bf(2, D, H), bf(2, 4, 256, H), fl(8, D), fl(8, T), fl(8, T),
            bf(3, T, D), bf(T, D), bf(T, D), bf(T, 3 * H), bf(T, D), bf(T, D), fl(T, D),
            bf(T, H), bf(T, D), bf(T, D), bf(T, D), fl(T, D),
            bf(6, T, T), bf(6, T, T), bf(T, FH), bf(T, FH), bf(T, FH), bf(T, D), bf(T, D),
            fl(T, D), bf(T, D),
            bf(T, D), fl(128, T), fl(128, T), bf(128, T), bf(128, T),
            bf(FH, T), fl(T, T),
            bf(3, 4, 128, D), bf(3, 2, 128, D), bf(3, 128, D), bf(2, 128, D), bf(2, 2, 256, H),
            pltpu.SemaphoreType.DMA((42,)), pltpu.SemaphoreType.DMA((40,)),
        ],
        input_output_aliases={},
        compiler_params=pltpu.CompilerParams(
            collective_id=0, has_side_effects=True, vmem_limit_bytes=67043328),
        name="layer",
    )(*blocks, segments, buckets.reshape(1, T), pos_bias, w, wd)


PAIRS = ((0, 1), (2, 4), (5, 6), (3, 7))


def pack_pair(a, b, x):
    n = a.shape[0]
    both = jnp.stack([a.reshape(n, 3, 64), b.reshape(n, 3, 64)], axis=2)
    return jnp.where(x == 0, both, both[:, :, ::-1]).reshape(n, H)


def unpack_pair(v, x):
    both = v.reshape(v.shape[0], 3, 2, 64)
    both = jnp.where(x == 0, both, both[:, :, ::-1])
    return both[:, :, 0].reshape(-1, 192), both[:, :, 1].reshape(-1, 192)


def hidden_order(v, half, forward=True):
    n = v.shape[0]
    outer = v.shape[1] // (2 * half)
    v = v.reshape((n, outer, 2, half) if forward else (n, 2, outer, half))
    return v.transpose(0, 2, 1, 3).reshape(n, -1)


def gather_plain(squares, gate, up, down, gains, x):
    half = down.shape[0] // 2
    parts = [pack_pair(squares[a], squares[b], x) for a, b in PAIRS]
    parts += [hidden_order(gate, half), hidden_order(up, half)]
    parts.append(jnp.pad(gains.T, ((0, 0), (0, 125))))
    groups = [[0, 2], [1, 3]]

    def both(v):
        v = lax.all_gather(v, "rows", axis=0, tiled=True)
        return lax.all_gather(v, "seq", axis=0, axis_index_groups=groups)

    return both(jnp.concatenate(parts, axis=1)), both(pack_pair(down[:half], down[half:], x))


def scatter_plain(gw, gwd, small, x):
    def reduced(v):
        v = lax.psum_scatter(v, "rows", scatter_dimension=1, tiled=True)
        kept = lax.dynamic_index_in_dim(v, x, 0, keepdims=False).astype(F32)
        sent = lax.dynamic_index_in_dim(v, 1 - x, 0, keepdims=False)
        return kept + lax.ppermute(sent, "seq", [(0, 2), (2, 0), (1, 3), (3, 1)]).astype(F32)

    total, down = reduced(gw), reduced(gwd)
    half = down.shape[0]
    squares = [None] * 8
    for k, (a, b) in enumerate(PAIRS):
        squares[a], squares[b] = unpack_pair(total[:, H * k : H * k + H], x)
    gate = hidden_order(total[:, 1536:2048], half, False)
    up = hidden_order(total[:, 2048:], half, False)
    down = jnp.concatenate(unpack_pair(down, x), axis=0)
    return squares, gate, up, down, lax.psum(small, ("rows", "seq"))


def shards(
    layer_input, memory, output_grad, segments, buckets,
    self_query, self_key, self_value, self_output,
    cross_query, cross_key, cross_value, cross_output,
    gate_weight, up_weight, down_weight, norm_gains, position_bias,
):
    x = lax.axis_index("seq") // 2
    squares = (self_query, self_key, self_value, self_output, cross_query, cross_key, cross_value, cross_output)
    w, wd = gather_plain(squares, gate_weight, up_weight, down_weight, norm_gains, x)
    mixed, input_grad, memory_grad, small, gw, gwd = layer(
        (layer_input, memory, output_grad), segments, buckets, position_bias, w, wd)
    squares, gate, up, down, small = scatter_plain(gw, gwd, small, x)
    width = D // lax.axis_size("rows")
    gains = lax.dynamic_slice(small, (0, lax.axis_index("rows") * width), (3, width))
    return (mixed, input_grad, memory_grad, *squares, gate, up, down, gains, small[:HEADS, D : D + BUCKETS].T)


def solution(mesh):
    tokens = P("rows", "seq", None)
    weight = P("rows", "seq")
    return jax.shard_map(
        shards,
        mesh=mesh,
        in_specs=(tokens, tokens, tokens, P("rows", None), P()) + (weight,) * 11 + (P(None, "rows"), P()),
        out_specs=(tokens,) * 3 + (weight,) * 11 + (P(None, "rows"), P()),
        check_vma=False,
    )
```

time: 1230 us -> 590 us (0.48)
  waiting for transfers between devices: 652 us -> 344 us
  local copies, waits for them, and re-layouts: 254 us -> 28 us
  blocking collectives: 169 us -> 81.2 us
    reduce_scatter x11 -> x2, waiting for transfers between devices: 610 us -> 160 us  [reduced(): v = lax.psum_scatter(v, 'rows', scatter_dimension=1, tiled=True)]
    all_gather x5 -> x3, waiting for transfers between devices: 40.5 us -> 171 us  [the longest x2 128 us: both(): return lax.all_gather(v, 'seq', axis=0, axis_index_groups=groups)]
    all_gather x4 -> x1, blocking collectives: 129 us -> 40.7 us  [both(): v = lax.all_gather(v, 'rows', axis=0, tiled=True)]
    transpose x19 -> x5, local copies, waits for them, and re-layouts: 80.3 us -> 0.94 us  [the longest x1 0.6 us: shards(): small[:HEADS, D:D + BUCKETS]]
    another operation x14 -> x0, local copies, waits for them, and re-layouts: 52.9 us -> none  [the longest x2 38.1 us: to_plane(): v = v.reshape(s[:axis] + (2, 2, 3, 64) + s[axis + 1:])]
    reshape x29 -> x16, local copies, waits for them, and re-layouts: 31.2 us -> 3.47 us  [the longest x4 1.76 us: hidden_order(): return v.transpose(0, 2, 1, 3).reshape(n, -1)]
    unnamed x96 -> x45, local copies, waits for them, and re-layouts: 35.8 us -> 17.6 us
    all_gather x3 -> x1, local copies, waits for them, and re-layouts: 18 us -> 2.59 us  [both(): return lax.all_gather(v, 'seq', axis=0, axis_index_groups=groups)]
  transfers between devices with their start and end apart: 27 -> 7, of which waited for: 12 -> 7; matrix products, arithmetic and copies ran while one was open for 10% -> 1% of each run, Pallas kernels for 0% -> 0%
where the time goes in v2:
time: 590 us; the launch traced here: 579 us
  waiting for transfers between devices  344 us (58%)
  Pallas kernels  105 us (18%)
  blocking collectives  81.2 us (14%)
  local copies, waits for them, and re-layouts  28 us (5%)
  between operations  14.8 us (3%)
    reduce_scatter x2, waiting for transfers between devices, reduced(): v = lax.psum_scatter(v, 'rows', scatter_dimension=1, tiled=True)  160 us
    all_gather x2, waiting for transfers between devices, both(): return lax.all_gather(v, 'seq', axis=0, axis_index_groups=groups)  128 us
    pallas_call x1, Pallas kernels, layer(): pl.pallas_call(layer_kernel, out_shape=[jax.ShapeDtypeStruct(s, d) for s,...  105 us
    all_gather x1, waiting for transfers between devices, both(): v = lax.all_gather(v, 'rows', axis=0, tiled=True)  43 us
    all_gather x1, blocking collectives, both(): v = lax.all_gather(v, 'rows', axis=0, tiled=True)  40.7 us
    psum x1, blocking collectives, scatter_plain(): return (squares, gate, up, down, lax.psum(small, ('rows', 'seq')))  40.5 us
    unnamed x45, local copies, waits for them, and re-layouts  17.6 us
    ppermute x2, waiting for transfers between devices, reduced(): lax.ppermute(sent, 'seq', [(0, 2), (2, 0), (1, 3), (3, 1)]).astype(F32)  12.1 us
  transfers between devices with their start and end apart: 7, of which 7 were waited for; matrix products, arithmetic and copies ran while one was open for 1% of the time, Pallas kernels for 0%

profile of v2, /device:TPU:0, one launch (start us, length us, event | category | flops | bytes accessed | tf_op | source)
XLA Modules:
  0.0 578.9 jit_solution(3504949547315443081)
XLA Ops:
  7.3 0.9 copy.52
  8.2 0.9 copy.53
  9.3 0.9 copy.55
  10.3 0.9 copy.56
  11.4 0.9 copy.58
  12.3 0.9 copy.59
  13.4 0.9 copy.61
  14.3 0.9 copy.62
  15.4 0.9 reshape.98
  16.9 0.8 copy-done.2
  17.9 40.7 %all_gather.21 = bf16[1024,384]{0,1:T(8,128)(2,1)} all-gather(bf16[128,384]{0,1:T(8,128)(2,1)S(1)} %bitcast.59), channel_id=1, replica_groups=mesh['rows'=8,'seq'=4] {'rows'}, dimensions={0}, use_global_device_ids=true | all-gather | bytes 884736 | tf_op jit(solution)/shard_map/all_gather | solution.py:647
  58.7 43.0 %all-gather.6.cloned.1.call-done = bf16[768,2688]{1,0:T(8,128)(2,1)} async-done(((bf16[96,2688]{1,0:T(8,128)(2,1)}), bf16[768,2688]{1,0:T(8,128)(2,1)}) %all-gather.6.cloned.1.call-update) | async-done | bytes 4128784 | tf_op jit(solution)/shard_map/all_gather | solution.py:647
  102.4 26.5 %all-gather.10.cloned.1.call-done = bf16[2048,384]{0,1:T(8,128)(2,1)} async-done(((bf16[1024,384]{0,1:T(8,128)(2,1)}), bf16[2048,384]{0,1:T(8,128)(2,1)}) %all-gather.10.cloned.1.call-update) | async-done | bytes 1572880 | tf_op jit(solution)/shard_map/all_gather | solution.py:648
  128.9 2.6 copy.71
  131.5 101.5 %all-gather.8.cloned.1.call-done = bf16[1536,2688]{1,0:T(8,128)(2,1)} async-done(((bf16[768,2688]{1,0:T(8,128)(2,1)}), bf16[1536,2688]{1,0:T(8,128)(2,1)}) %all-gather.8.cloned.1.call-update) | async-done | bytes 8257552 | tf_op jit(solution)/shard_map/all_gather | solution.py:648
  233.0 104.7 %layer.1 = (bf16[2,128,768]{2,1,0:T(8,128)(2,1)}, f32[2,128,768]{2,1,0:T(8,128)}, f32[2,128,768]{2,1,0:T(8,128)}, f32[16,896]{1,0:T(8,128)}, bf16[2,768,2560]{2,...) custom-call(bf16[2,128,768]{2,1,0:T(8,128)(2,1)} %in_x.1, bf16[2,128,768]{2,1,0:T(8,128)(2,1)} %in_m.1, ...), custom_call_target="tpu_custom_call" | custom-call | tf_op jit(solution)/shard_map/layer/pallas_call | solution.py:593
  338.5 40.5 %psum.7 = f32[16,896]{1,0:T(8,128)S(1)} all-reduce(f32[16,896]{1,0:T(8,128)S(1)} %copy-done.6), channel_id=1, replica_groups=mesh['rows'=8,'seq'=4] {'rows','seq'}, use_global_device_ids=true, to_apply=%region_2.3 | all-reduce | flops 14336 | bytes 114688 | tf_op jit(solution)/shard_map/psum | solution.py:668
  379.6 24.1 %reduce-scatter.5.cloned.1.call-done = bf16[2,128,384]{2,1,0:T(8,128)(2,1)} async-done(((bf16[2,1024,384]{2,1,0:T(8,128)(2,1)}), bf16[2,128,384]{2,1,0:T(8,128)(2,1)}) %reduce-scatter.5.cloned.1.call-update) | async-done | bytes 196624 | tf_op jit(solution)/shard_map/reduce_scatter | solution.py:655
  403.7 0.9 dynamic-slice_bitcast_fusion.1
  404.6 1.7 collective-permute-start.1
  406.9 2.4 collective-permute-done.1
  409.3 0.9 convert_add_fusion.1
  410.3 136.0 %reduce-scatter.3.cloned.1.call-done = bf16[2,96,2560]{2,1,0:T(8,128)(2,1)} async-done(((bf16[2,768,2560]{2,1,0:T(8,128)(2,1)}), bf16[2,96,2560]{2,1,0:T(8,128)(2,1)}) %reduce-scatter.3.cloned.1.call-update) | async-done | bytes 983056 | tf_op jit(solution)/shard_map/reduce_scatter | solution.py:655
  546.3 1.1 dynamic-slice_bitcast_fusion
  547.4 1.5 collective-permute-start
  549.7 9.7 %collective-permute-done = bf16[96,2560]{1,0:T(8,128)(2,1)S(1)} collective-permute-done((bf16[96,2560]{1,0:T(8,128)(2,1)S(1)}, bf16[96,2560]{1,0:T(8,128)(2,1)S(1)}, u32[]{:S(2)}, u32[]{:S(2)}) %collective-permute-start) | collective-permute-done | bytes 491552 | tf_op jit(solution)/shard_map/ppermute | solution.py:658
  559.4 1.1 convert_add_fusion
  567.5 0.8 reshape.108
  568.6 0.8 reshape.110
  569.4 0.7 copy.106
  570.2 0.9 copy.107
  571.1 0.9 copy.108
  (94 shorter events, 12.1 us)
Async XLA Ops:
  7.2 9.3 %copy-start.4 = (bf16[96,512]{1,0:T(8,128)(2,1)S(1)}, bf16[96,512]{1,0:T(8,128)(2,1)}, u32[]{:S(2)}) copy-start(bf16[96,512]{1,0:T(8,128)(2,1)} %param.32) | copy-start | bytes 294916
  7.2 9.5 %copy-start.8 = (bf16[3,96]{1,0:T(4,128)(2,1)S(1)}, bf16[3,96]{1,0:T(4,128)(2,1)}, u32[]{:S(2)}) copy-start(bf16[3,96]{1,0:T(4,128)(2,1)} %param.34) | copy-start | bytes 1732
  7.2 10.6 %copy-start.5 = (bf16[256,192]{0,1:T(8,128)(2,1)S(1)}, bf16[256,192]{0,1:T(8,128)(2,1)}, u32[]{:S(2)}) copy-start(bf16[256,192]{0,1:T(8,128)(2,1)} %param.33) | copy-start | bytes 294916
  7.2 94.4 %all-gather.6.cloned.1.call-start = ((), (), s32[]{:S(2)}) async-start(), calls=%async_computation.2 | async-start | bytes 4644864 | tf_op jit(solution)/shard_map/all_gather | solution.py:647
  16.5 85.2 %copy-start.7 = (bf16[32,12]{0,1:T(8,128)(2,1)S(1)}, bf16[32,12]{0,1:T(8,128)(2,1)}, u32[]{:S(2)}) copy-start(bf16[32,12]{0,1:T(8,128)(2,1)} %param.35) | copy-start | bytes 2308
  16.9 0.8 copy-start.2
  17.7 111.2 %all-gather.10.cloned.1.call-start = ((), (), s32[]{:S(2)}) async-start(), calls=%async_computation.6 | async-start | bytes 2359296 | tf_op jit(solution)/shard_map/all_gather | solution.py:648
  58.6 174.4 %all-gather.8.cloned.1.call-start = ((), (), s32[]{:S(2)}) async-start(), calls=%async_computation.5 | async-start | bytes 12386304 | tf_op jit(solution)/shard_map/all_gather | solution.py:648
  101.6 302.0 %reduce-scatter.5.cloned.1.call-start = ((), (), s32[]{:S(2)}) async-start(), calls=%async_computation.4 | async-start | bytes 1769472 | tf_op jit(solution)/shard_map/reduce_scatter | solution.py:655
  337.7 0.8 copy-start.6
  337.7 208.6 %reduce-scatter.3.cloned.1.call-start = ((), (), s32[]{:S(2)}) async-start(), calls=%async_computation.3 | async-start | bytes 8847360 | tf_op jit(solution)/shard_map/reduce_scatter | solution.py:655
  404.6 4.7 collective-permute-start.1
  547.4 12.0 %collective-permute-start = (bf16[96,2560]{1,0:T(8,128)(2,1)S(1)}, bf16[96,2560]{1,0:T(8,128)(2,1)S(1)}, u32[]{:S(2)}, u32[]{:S(2)}) collective-permute-start(bf16[96,2560]{1,0:T(8,128)(2,1)S(1)} %dynamic-slice_bitcast_fusion), channel_id=1, source_target_pairs={{0,2},{2,0},{1,3},{3,1},{4,6},{6,4},{5,7},{7,5},{8,10},{10,8},{9,1... | collective-permute-start | bytes 1474568 | tf_op jit(solution)/shard_map/ppermute | solution.py:658
  560.9 8.5 %copy-start.3 = (bf16[2,128,768]{2,1,0:T(8,128)(2,1)S(1)}, bf16[2,128,768]{2,1,0:T(8,128)(2,1)}, u32[]{:S(2)}) copy-start(bf16[2,128,768]{2,1,0:T(8,128)(2,1)} %get-tuple-element.82) | copy-start | bytes 1179652
  561.0 9.2 %copy-start.1 = (f32[2,128,768]{2,1,0:T(8,128)S(1)}, f32[2,128,768]{2,1,0:T(8,128)}, u32[]{:S(2)}) copy-start(f32[2,128,768]{2,1,0:T(8,128)} %get-tuple-element.83) | copy-start | bytes 2359300
  564.1 7.0 %copy-start = (f32[2,128,768]{2,1,0:T(8,128)S(1)}, f32[2,128,768]{2,1,0:T(8,128)}, u32[]{:S(2)}) copy-start(f32[2,128,768]{2,1,0:T(8,128)} %get-tuple-element.84) | copy-start | bytes 2359300
Sparse Core Ops, SparseCore 0:
  17.9 83.7 all-gather.5
  103.2 25.7 all-gather.9
  130.5 102.4 all-gather.7
  337.8 65.7 reduce-scatter.4
  407.2 139.1 reduce-scatter.2

commit v3 on v2

--- a/solution.py
+++ b/solution.py
@@ -1,3 +1,5 @@
+import functools
+
 import jax
 import jax.numpy as jnp
 from jax import lax
@@ -73,16 +75,157 @@
     return [v[:, 128 * n : 128 * n + 128] for n in range(v.shape[1] // 128)]
 
 
+GATHER = (
+    ("w", 2560, 128, 0), ("w", 0, H, 0), ("w", H, H, 1), ("w", 2 * H, H, 0), ("w", 3 * H, H, 1),
+    ("w", 1536, 512, 0), ("w", 2048, 512, 1), ("d", 0, 64, 0), ("d", 64, 64, 1),
+)
+SCATTER = (
+    ("w", 1536, 512, 0), ("w", 2048, 512, 1), ("d", 0, 64, 0), ("d", 64, 64, 1),
+    ("w", 2 * H, H, 0), ("w", 3 * H, H, 1), ("w", 0, H, 0), ("w", H, H, 1),
+)
+
+
+def place():
+    row, seq = lax.axis_index("rows"), lax.axis_index("seq")
+    return lax.div(row, 2), lax.rem(row, 2), lax.div(seq, 2), lax.rem(seq, 2)
+
+
+def device(z, y, x, c):
+    return (2 * z + y, 2 * x + c)
+
+
+class Gather:
+    def __init__(self, own_w, own_d, w, wd, ssem, rsem):
+        self.refs = (own_w, own_d, w, wd, ssem, rsem)
+        self.z, self.y, self.x, self.c = place()
+        self.sent = []
+        self.open = {}
+        self.todo = []
+        count = len(GATHER)
+        for k in range(min(3, count)):
+            self.todo.append((self.begin, k))
+        for k in range(count):
+            self.todo.append((self.after_z, k))
+            if k + 3 < count:
+                self.todo.append((self.begin, k + 3))
+            if k >= 1:
+                self.todo.append((self.after_p, k - 1))
+            if k >= 2:
+                self.todo.append((self.finish, k - 2))
+        self.todo += [(self.after_p, count - 1), (self.finish, count - 2), (self.finish, count - 1)]
+        self.done = -1
+
+    def view(self, k, x, z, y):
+        kind, first, size, _ = GATHER[k]
+        _, _, w, wd, _, _ = self.refs
+        r = 2 * z + y
+        if kind == "w":
+            return w.at[x, pl.ds(pl.multiple_of(96 * r, 96), 96), first : first + size]
+        return wd.at[x, pl.ds(pl.multiple_of(128 * r + first, 64), size), :]
+
+    def own(self, k):
+        kind, first, size, _ = GATHER[k]
+        own_w, own_d, _, _, _, _ = self.refs
+        return own_w.at[:, first : first + size] if kind == "w" else own_d.at[first : first + size, :]
+
+    def peers(self, k):
+        y_peer, x_peer = device(self.z, 1 - self.y, self.x, self.c), device(self.z, self.y, 1 - self.x, self.c)
+        return (x_peer, y_peer) if GATHER[k][3] else (y_peer, x_peer)
+
+    def across_p(self, k):
+        return (1 - self.x, self.y) if GATHER[k][3] else (self.x, 1 - self.y)
+
+    def copy(self, k, slot, src, dst, peer):
+        _, _, _, _, ssem, rsem = self.refs
+        return pltpu.make_async_remote_copy(
+            src_ref=src, dst_ref=dst, send_sem=ssem.at[k, slot], recv_sem=rsem.at[k, slot],
+            device_id=peer, device_id_type=MESH)
+
+    def send(self, k, *args):
+        copy = self.copy(k, *args)
+        copy.start()
+        self.open[k].append(copy)
+
+    def behind(self, j):
+        return lax.rem(self.z + 4 - j, 4)
+
+    def begin(self, k):
+        here = self.view(k, self.x, self.z, self.y)
+        p, q = self.peers(k)
+        own = self.own(k)
+        self.open[k] = []
+        self.send(k, 3, own, here, p)
+        self.send(k, 7, own, here, q)
+        for j in range(1, 4):
+            self.send(k, j - 1, own, here, device(lax.rem(self.z + j, 4), self.y, self.x, self.c))
+        here[...] = own[...]
+
+    def after_z(self, k):
+        p, q = self.peers(k)
+        for j in range(1, 4):
+            block = self.view(k, self.x, self.behind(j), self.y)
+            self.copy(k, j - 1, block, block, p).wait_recv()
+            self.send(k, 3 + j, block, block, p)
+            self.send(k, 7 + j, block, block, q)
+
+    def after_p(self, k):
+        p, q = self.peers(k)
+        x, y = self.across_p(k)
+        for j in range(4):
+            block = self.view(k, x, self.behind(j), y)
+            self.copy(k, 3 + j, block, block, p).wait_recv()
+            self.send(k, 11 + j, block, block, q)
+
+    def finish(self, k):
+        p, q = self.peers(k)
+        x, y = (self.x, 1 - self.y) if GATHER[k][3] else (1 - self.x, self.y)
+        for j in range(4):
+            block = self.view(k, x, self.behind(j), y)
+            self.copy(k, 7 + j, block, block, q).wait_recv()
+        for j in range(4):
+            block = self.view(k, 1 - self.x, self.behind(j), 1 - self.y)
+            self.copy(k, 11 + j, block, block, q).wait_recv()
+        for copy in self.open[k]:
+            copy.wait_send()
+        self.done = k
+
+    def pump(self, count):
+        for _ in range(min(count, len(self.todo))):
+            action, k = self.todo.pop(0)
+            action(k)
+
+    def need(self, k):
+        while self.done < k:
+            self.pump(1)
+
+
+class Loaded:
+    def __init__(self, w_in, wd_in, w, wd, sems):
+        self.copies = [pltpu.make_async_copy(w_in, w, sems.at[0]), pltpu.make_async_copy(wd_in, wd, sems.at[1])]
+        for copy in self.copies:
+            copy.start()
+        self.sent = []
+
+    def pump(self, count):
+        pass
+
+    def need(self, k):
+        for copy in self.copies:
+            copy.wait()
+        self.copies = []
+
+
 def layer_kernel(
-    in_x, in_m, in_g, segments, buckets, pos_bias, w_in, wd_in,
-    mixed, input_grad, memory_grad, small, gw, gwd,
-    w, wd,    w_o, w_cq, w_co, w_d, gains, table, dist_grad, full, ffb, na, qkv, att, attn, x1, cq, mkv, catt, cattn, x2,
+    inside, in_x, in_m, in_g, segments, buckets, pos_bias, w_in, wd_in,
+    mixed, input_grad, memory_grad, small, w, wd,
+    w_o, w_cq, w_co, w_d, gains, table, dist_grad, full, ffb, na, qkv, att, attn, x1, cq, mkv, catt, cattn, x2,
     bias, p_self, hidden, gg, gu, gsend, grecv, gx2, gxb,
     gcq, dk_t, dv_t, qt_s, gt_s, left_t, work,
     psend, precv, msend, late, gdsend,
-    ssem, rsem,
+    ssem, rsem, gather_ssem, gather_rsem,
 ):
     p_cross = bias
+    gw, gwd = w, wd
     nb = nc = na
     gatt = hidden
     row = lax.axis_index("rows")
@@ -93,18 +236,24 @@
     across = (row, lax.rem(seq + 2, 4))
 
     barrier = pltpu.get_barrier_semaphore()
-    for peer in (mate, across):
+    peers = [mate, across]
+    if inside:
+        pz, py, px, pc = place()
+        peers.append(device(pz, 1 - py, px, pc))
+        peers += [device(lax.rem(pz + j, 4), py, px, pc) for j in range(1, 4)]
+    for peer in peers:
         pl.semaphore_signal(barrier, inc=1, device_id=peer, device_id_type=MESH)
-    pl.semaphore_wait(barrier, 2)
+    pl.semaphore_wait(barrier, len(peers))
 
     started = []
 
-    def remote(src, dst, slot, peer):
+    def remote(src, dst, slot, peer, keep=True):
         copy = pltpu.make_async_remote_copy(
             src_ref=src, dst_ref=dst, send_sem=ssem.at[slot], recv_sem=rsem.at[slot],
             device_id=peer, device_id_type=MESH)
         copy.start()
-        started.append(copy)
+        if keep:
+            started.append(copy)
         return copy
 
     mine = tile(c, H, H)
@@ -125,12 +274,11 @@
         to_mate.append(remote(block.at[x], full.at[k, own], 28 + k, mate))
         full[k, own] = block[x]
 
-    loads = [
-        pltpu.make_async_copy(w_in, w, ssem.at[40]), pltpu.make_async_copy(wd_in, wd, ssem.at[41])]
-    for copy in loads:
-        copy.start()
-    for copy in loads:
-        copy.wait()
+    if inside:
+        weights = Gather(w_in, wd_in, w, wd, gather_ssem, gather_rsem)
+    else:
+        weights = Loaded(w_in, wd_in, w, wd, gather_ssem)
+    weights.need(8)
 
     def separate(first, second, ref, lanes, rows_at, count):
         def part(i):
@@ -158,7 +306,7 @@
 
     halves = []
     for k, ref in enumerate((w_o, w_cq, w_co)):
-        halves.append(remote(ref.at[c], ref.at[c], 31 + k, mate))
+        halves.append(remote(ref.at[c], ref.at[c], 31 + k, mate, False))
 
     for t in range(3):
         lanes = slice(128 * t, 128 * t + 128)
@@ -173,8 +321,11 @@
     for xs in range(2):
         for b in range(2):
             piece = wd.at[b, tile((1 - c) + 2 * xs, 256, 256)]
-            halves.append(remote(piece, w_d.at[c, 2 * xs + b], 34 + 2 * xs + b, mate))
+            halves.append(remote(piece, w_d.at[c, 2 * xs + b], 34 + 2 * xs + b, mate, False))
             w_d[c, 2 * xs + b] = wd[b, tile(c + 2 * xs, 256, 256)]
+
+    for copy in halves:
+        copy.wait_send()
 
     gains[...] = w[0, :, 2560:2688].astype(F32).T[0:8]
     hot = (lax.broadcasted_iota(jnp.int32, (BUCKETS, T), 0) == buckets[...]).astype(BF16)
@@ -426,29 +577,27 @@
         (cols_of(gu), into(lambda n: lax.div(n, 4), lambda n: 16 + lax.rem(n, 4)), 8),
     ])
 
-    def put_down(half):
+    def put_down(xs, own_half):
         def put(n, value):
             cols = tile(n, 128, 128)
-            for xs in range(2):
-                top = value[512 * xs : 512 * xs + 256]
-                bottom = roll_half(value[512 * xs + 256 : 512 * xs + 512])
-                a, b = jnp.where(low, top, bottom).astype(BF16), jnp.where(low, bottom, top).astype(BF16)
-                if half:
-                    rows = tile(c + 2 * xs, 256, 256)
-                    gwd[0, rows, cols] = a
-                    gwd[1, rows, cols] = b
-                else:
-                    gdsend[xs, 0, :, cols] = a
-                    gdsend[xs, 1, :, cols] = b
+            top, bottom = value[0:256], roll_half(value[256:512])
+            a, b = jnp.where(low, top, bottom).astype(BF16), jnp.where(low, bottom, top).astype(BF16)
+            if own_half:
+                rows = tile(c + 2 * xs, 256, 256)
+                gwd[0, rows, cols] = a
+                gwd[1, rows, cols] = b
+            else:
+                gdsend[xs, 0, :, cols] = a
+                gdsend[xs, 1, :, cols] = b
         return put
 
-    weight_grad(lambda j: hidden[:, j], FH, [
-        (lambda n: ffb[:, tile(n + 3 * (1 - c), 128, 128)], put_down(False), 3),
-        (lambda n: ffb[:, tile(n + 3 * c, 128, 128)], put_down(True), 3),
-    ])
-    gd_copies = [
-        remote(gdsend.at[xs], gwd.at[:, tile(c + 2 * xs, 256, 256)], 38 + xs, mate) for xs in range(2)
-    ]
+    gd_copies = []
+    for xs in range(2):
+        weight_grad(lambda j: hidden[:, pl.ds(pl.multiple_of(j.start + 512 * xs, 128), 128)], 512, [
+            (lambda n: ffb[:, tile(n + 3 * (1 - c), 128, 128)], put_down(xs, False), 3),
+            (lambda n: ffb[:, tile(n + 3 * c, 128, 128)], put_down(xs, True), 3),
+        ])
+        gd_copies.append(remote(gdsend.at[xs], gwd.at[:, tile(c + 2 * xs, 256, 256)], 38 + xs, mate))
 
     wait_all(gc_copies)
     small[...] = jnp.zeros_like(small)
@@ -574,11 +723,11 @@
     input_grad[1 - x] = late[1].astype(F32)
     mix_out.wait_recv()
     wait_all(gd_copies)
-    for copy in started:
+    for copy in started + weights.sent:
         copy.wait_send()
 
 
-def layer(blocks, segments, buckets, pos_bias, w, wd):
+def layer(blocks, segments, buckets, pos_bias, w, wd, inside):
     def bf(*shape):
         return VMEM(shape, BF16)
 
@@ -587,25 +736,26 @@
 
     outs = [
         ((2, 128, D), BF16), ((2, 128, D), F32), ((2, 128, D), F32), ((16, D + 128), F32),
-        ((2, D, 2560), BF16), ((2, FH, H), BF16),
+        ((2, D, 2688), BF16), ((2, FH, H), BF16),
     ]
     whole = pl.BlockSpec(memory_space=pltpu.VMEM)
+    dma = pltpu.SemaphoreType.DMA
+    gather_sems = [dma((len(GATHER), 15)), dma((len(GATHER), 15))] if inside else [dma((2,)), dma((2,))]
     return pl.pallas_call(
-        layer_kernel,
+        functools.partial(layer_kernel, inside),
         out_shape=[jax.ShapeDtypeStruct(s, d) for s, d in outs],
-        in_specs=[whole] * 6 + [pl.BlockSpec(memory_space=pl.ANY)] * 2,
+        in_specs=[whole] * 6 + [whole if inside else pl.BlockSpec(memory_space=pl.ANY)] * 2,
         out_specs=[whole] * len(outs),
         scratch_shapes=[
-            bf(2, D, 2688), bf(2, FH, H),
             bf(2, D, H), bf(2, D, H), bf(2, D, H), bf(2, 4, 256, H), fl(8, D), fl(8, T), fl(8, T),
             bf(3, T, D), bf(T, D), bf(T, D), bf(T, 3 * H), bf(T, D), bf(T, D), fl(T, D),
             bf(T, H), bf(T, D), bf(T, D), bf(T, D), fl(T, D),
             bf(6, T, T), bf(6, T, T), bf(T, FH), bf(T, FH), bf(T, FH), bf(T, D), bf(T, D),
             fl(T, D), bf(T, D),
             bf(T, D), fl(128, T), fl(128, T), bf(128, T), bf(128, T),
-            bf(FH, T), fl(T, T),
+            bf(D, T), fl(T, T),
             bf(3, 4, 128, D), bf(3, 2, 128, D), bf(3, 128, D), bf(2, 128, D), bf(2, 2, 256, H),
-            pltpu.SemaphoreType.DMA((42,)), pltpu.SemaphoreType.DMA((40,)),
+            pltpu.SemaphoreType.DMA((40,)), pltpu.SemaphoreType.DMA((40,)), *gather_sems,
         ],
         input_output_aliases={},
         compiler_params=pltpu.CompilerParams(
@@ -636,21 +786,185 @@
     return v.transpose(0, 2, 1, 3).reshape(n, -1)
 
 
-def gather_plain(squares, gate, up, down, gains, x):
+def payload(squares, gate, up, down, gains, x):
     half = down.shape[0] // 2
     parts = [pack_pair(squares[a], squares[b], x) for a, b in PAIRS]
     parts += [hidden_order(gate, half), hidden_order(up, half)]
     parts.append(jnp.pad(gains.T, ((0, 0), (0, 125))))
-    groups = [[0, 2], [1, 3]]
-
-    def both(v):
-        v = lax.all_gather(v, "rows", axis=0, tiled=True)
-        return lax.all_gather(v, "seq", axis=0, axis_index_groups=groups)
-
-    return both(jnp.concatenate(parts, axis=1)), both(pack_pair(down[:half], down[half:], x))
+    return jnp.concatenate(parts, axis=1), pack_pair(down[:half], down[half:], x)
+
+
+def gather_plain(v):
+    v = lax.all_gather(v, "rows", axis=0, tiled=True)
+    return lax.all_gather(v, "seq", axis=0, axis_index_groups=[[0, 2], [1, 3]])
+
+
+def reduce_kernel(
+    gw, gwd, small_in, *refs,
+):
+    squares, (gate, up, down, total), refs = refs[:8], refs[8:12], refs[12:]
+    r1, r1d, r2, r2d, r3, r3d, acc, got, ssem, rsem, small_ssem, small_rsem = refs
+    z, y, x, c = place()
+    mate = device(z, y, x, 1 - c)
+    y_peer, x_peer = device(z, 1 - y, x, c), device(z, y, 1 - x, c)
+    z_peers = [device(lax.rem(z + j, 4), y, x, c) for j in range(1, 4)]
+    low = low_lanes()
+
+    barrier = pltpu.get_barrier_semaphore()
+    for peer in [mate, y_peer, x_peer] + z_peers:
+        pl.semaphore_signal(barrier, inc=1, device_id=peer, device_id_type=MESH)
+    pl.semaphore_wait(barrier, 6)
+    sent = []
+
+    def copy(k, slot, src, dst, peer):
+        return pltpu.make_async_remote_copy(
+            src_ref=src, dst_ref=dst, send_sem=ssem.at[k, slot], recv_sem=rsem.at[k, slot],
+            device_id=peer, device_id_type=MESH)
+
+    def send(*args):
+        out = copy(*args)
+        out.start()
+        sent.append(out)
+        return out
+
+    def part(k, w_ref, d_ref, *lead):
+        kind, first, size, _ = SCATTER[k]
+        if kind == "w":
+            return w_ref.at[(*lead, slice(None), slice(first, first + size))]
+        return d_ref.at[(*lead, slice(first, first + size), slice(None))]
+
+    def grads(k, a, mine):
+        if SCATTER[k][3]:
+            return part(k, gw, gwd, a, slice(None), y if mine else 1 - y)
+        return part(k, gw, gwd, x if mine else 1 - x, slice(None), a)
+
+    def second_place(k):
+        return x if SCATTER[k][3] else y
+
+    def sides(k):
+        m = second_place(k)
+        return (1 - m, m)
+
+    def first_send(k):
+        peer = y_peer if SCATTER[k][3] else x_peer
+        for i, a in enumerate(sides(k)):
+            send(k, i, grads(k, a, False), part(k, r1, r1d, a, slice(None)), peer)
+
+    def add_blocks(dest, other):
+        def one(i):
+            dest[i] = (dest[i].astype(F32) + other[i].astype(F32)).astype(BF16)
+
+        repeat(4, one)
+
+    def after_first(k):
+        peer = y_peer if SCATTER[k][3] else x_peer
+        onward = x_peer if SCATTER[k][3] else y_peer
+        for i, a in enumerate(sides(k)):
+            block = part(k, r1, r1d, a, slice(None))
+            copy(k, i, block, block, peer).wait_recv()
+            add_blocks(block, grads(k, a, True))
+            if i == 0:
+                send(k, 2, block, part(k, r2, r2d, slice(None)), onward)
+
+    def after_second(k):
+        onward = x_peer if SCATTER[k][3] else y_peer
+        block = part(k, r2, r2d, slice(None))
+        copy(k, 2, block, block, onward).wait_recv()
+        add_blocks(block, part(k, r1, r1d, second_place(k), slice(None)))
+        for j in range(1, 4):
+            send(k, 2 + j, part(k, r2, r2d, lax.rem(z + j, 4)), part(k, r3, r3d, j - 1), z_peers[j - 1])
+
+    def after_third(k):
+        value = part(k, r2, r2d, z)[...].astype(F32)
+        for j in range(1, 4):
+            block = part(k, r3, r3d, j - 1)
+            copy(k, 2 + j, block, block, z_peers[j - 1]).wait_recv()
+            value = value + block[...].astype(F32)
+        kind, first, size, _ = SCATTER[k]
+        if kind == "w" and first >= 1536:
+            dest = gate if first == 1536 else up
+            for n, m in enumerate((0, 2, 1, 3)):
+                dest[:, 128 * m : 128 * m + 128] = value[:, 128 * n : 128 * n + 128]
+            return
+        tiles = [jnp.where(x == 0, v, roll_half(v)) for v in lane_tiles(value)]
+        turned = [roll_half(v) for v in tiles]
+        if kind == "w":
+            one, two = PAIRS[first // H]
+            targets = ((squares[one], slice(0, 96)), (squares[two], slice(0, 96)))
+        else:
+            targets = ((down, slice(first, first + size)), (down, slice(128 + first, 128 + first + size)))
+        ref, rows = targets[0]
+        ref[rows, 0:128] = jnp.where(low, tiles[0], turned[1])
+        ref[rows, 128:192] = tiles[2][:, 0:64]
+        ref, rows = targets[1]
+        ref[rows, 0:128] = jnp.where(low, turned[0], tiles[1])
+        ref[rows, 128:192] = turned[2][:, 0:64]
+
+    def small_send(slot, src, peer):
+        out = pltpu.make_async_remote_copy(
+            src_ref=src, dst_ref=got.at[slot], send_sem=small_ssem.at[slot], recv_sem=small_rsem.at[slot],
+            device_id=peer, device_id_type=MESH)
+        out.start()
+        sent.append(out)
+        return out
+
+    count = len(SCATTER)
+    first = small_send(0, small_in, mate)
+    for k in range(count):
+        first_send(k)
+    first.wait_recv()
+    acc[0] = small_in[...] + got[0]
+    first = small_send(1, acc.at[0], x_peer)
+    after_first(0)
+    first.wait_recv()
+    acc[1] = acc[0] + got[1]
+    first = small_send(2, acc.at[1], y_peer)
+    after_first(1)
+    after_second(0)
+    first.wait_recv()
+    acc[2] = acc[1] + got[2]
+    last = [small_send(2 + j, acc.at[2], z_peers[j - 1]) for j in range(1, 4)]
+    for k in range(2, count):
+        after_first(k)
+        after_second(k - 1)
+        after_third(k - 2)
+    after_second(count - 1)
+    after_third(count - 2)
+    after_third(count - 1)
+    for out in last:
+        out.wait_recv()
+    total[...] = acc[2] + got[3] + got[4] + got[5]
+    for out in sent:
+        out.wait_send()
+
+
+def scatter_lines(gw, gwd, small, x):
+    def bf(*shape):
+        return VMEM(shape, BF16)
+
+    whole = pl.BlockSpec(memory_space=pltpu.VMEM)
+    dma = pltpu.SemaphoreType.DMA
+    outs = [(96, 192)] * 8 + [(96, 512), (96, 512), (256, 192), small.shape]
+    out = pl.pallas_call(
+        reduce_kernel,
+        out_shape=[jax.ShapeDtypeStruct(s, F32) for s in outs],
+        in_specs=[whole] * 3,
+        out_specs=[whole] * len(outs),
+        scratch_shapes=[
+            bf(2, 4, 96, 2560), bf(2, 4, 128, H), bf(4, 96, 2560), bf(4, 128, H), bf(3, 96, 2560), bf(3, 128, H),
+            VMEM((3,) + small.shape, F32), VMEM((6,) + small.shape, F32),
+            dma((len(SCATTER), 6)), dma((len(SCATTER), 6)), dma((6,)), dma((6,)),
+        ],
+        compiler_params=pltpu.CompilerParams(
+            collective_id=1, has_side_effects=True, vmem_limit_bytes=60000000),
+        name="reduce",
+    )(gw.reshape(2, 4, 2, 96, 2688), gwd.reshape(2, 4, 2, 128, H), small)
+    return list(out[:8]), *out[8:]
 
 
 def scatter_plain(gw, gwd, small, x):
+    gw = gw[:, :, :2560]
+
     def reduced(v):
         v = lax.psum_scatter(v, "rows", scatter_dimension=1, tiled=True)
         kept = lax.dynamic_index_in_dim(v, x, 0, keepdims=False).astype(F32)
@@ -676,10 +990,14 @@
 ):
     x = lax.axis_index("seq") // 2
     squares = (self_query, self_key, self_value, self_output, cross_query, cross_key, cross_value, cross_output)
-    w, wd = gather_plain(squares, gate_weight, up_weight, down_weight, norm_gains, x)
+    w, wd = payload(squares, gate_weight, up_weight, down_weight, norm_gains, x)
+    inside = lax.axis_size("rows") == 8
+    if not inside:
+        w, wd = gather_plain(w), gather_plain(wd)
     mixed, input_grad, memory_grad, small, gw, gwd = layer(
-        (layer_input, memory, output_grad), segments, buckets, position_bias, w, wd)
-    squares, gate, up, down, small = scatter_plain(gw, gwd, small, x)
+        (layer_input, memory, output_grad), segments, buckets, position_bias, w, wd, inside)
+    scatter = scatter_lines if inside else scatter_plain
+    squares, gate, up, down, small = scatter(gw, gwd, small, x)
     width = D // lax.axis_size("rows")
     gains = lax.dynamic_slice(small, (0, lax.axis_index("rows") * width), (3, width))
     return (mixed, input_grad, memory_grad, *squares, gate, up, down, gains, small[:HEADS, D : D + BUCKETS].T)

time: 590 us -> 376 us (0.64); the launches traced: 579 us -> 373 us
  waiting for transfers between devices: 344 us -> 0 us
  Pallas kernels: 105 us -> 331 us
  blocking collectives: 81.2 us -> 0 us
  between operations: 14.8 us -> 1.12 us
  local copies, waits for them, and re-layouts: 28 us -> 40.5 us
    pallas_call x1 -> x2, Pallas kernels: 105 us -> 331 us  [the longest x1 207 us: layer(): pl.pallas_call(functools.partial(layer_kernel, inside), out_shape=[jax.Sh...]
    all_gather x3 -> x0, waiting for transfers between devices: 171 us -> none  [the longest x2 128 us: both(): return lax.all_gather(v, 'seq', axis=0, axis_index_groups=groups)]
    reduce_scatter x2 -> x0, waiting for transfers between devices: 160 us -> none  [reduced(): v = lax.psum_scatter(v, 'rows', scatter_dimension=1, tiled=True)]
    all_gather x1 -> x0, blocking collectives: 40.7 us -> none  [both(): v = lax.all_gather(v, 'rows', axis=0, tiled=True)]
    psum x1 -> x0, blocking collectives: 40.5 us -> none  [scatter_plain(): return (squares, gate, up, down, lax.psum(small, ('rows', 'seq')))]
    unnamed x45 -> x36, local copies, waits for them, and re-layouts: 17.6 us -> 33.1 us
    ppermute x2 -> x0, waiting for transfers between devices: 12.1 us -> none  [reduced(): lax.ppermute(sent, 'seq', [(0, 2), (2, 0), (1, 3), (3, 1)]).astype(F32)]
  transfers between devices with their start and end apart: 7 -> 0, of which waited for: 7 -> 0; matrix products, arithmetic and copies ran while one was open for 1% -> 0% of each run, Pallas kernels for 0% -> 0%
where the time goes in v3:
time: 376 us; the launch traced here: 373 us
  Pallas kernels  331 us (88%)
  local copies, waits for them, and re-layouts  40.5 us (11%)
    pallas_call x1, Pallas kernels, layer(): pl.pallas_call(functools.partial(layer_kernel, inside), out_shape=[jax.Sh...  207 us
    pallas_call x1, Pallas kernels, scatter_lines(): pl.pallas_call(reduce_kernel, out_shape=[jax.ShapeDtypeStruct(s, F32) for...  124 us
    unnamed x36, local copies, waits for them, and re-layouts  33.1 us

profile of v3, /device:TPU:0, one launch (start us, length us, event | category | flops | bytes accessed | tf_op | source)
XLA Modules:
  0.0 372.8 jit_solution(11710504020093015298)
XLA Ops:
  0.7 1.4 copy.68.pos_bias
  2.0 0.8 copy.63
  2.8 0.9 copy.49
  3.7 0.9 copy.50
  4.7 0.9 copy.52
  5.6 0.9 copy.58
  6.5 0.9 copy.53
  7.7 0.9 copy.55
  8.6 0.9 copy.56
  9.5 0.9 copy.59
  10.9 0.9 reshape.73
  12.0 0.9 reshape.75
  13.0 0.8 fusion
  13.9 0.8 copy.69.wd_in
  19.1 206.7 %layer.1 = (bf16[2,128,768]{2,1,0:T(8,128)(2,1)}, f32[2,128,768]{2,1,0:T(8,128)}, f32[2,128,768]{2,1,0:T(8,128)}, f32[16,896]{1,0:T(8,128)}, bf16[2,768,2688]{2,...) custom-call(bf16[2,128,768]{2,1,0:T(8,128)(2,1)} %in_x.1, bf16[2,128,768]{2,1,0:T(8,128)(2,1)} %in_m.1, ...), custom_call_target="tpu_custom_call" | custom-call | tf_op jit(solution)/shard_map/layer/pallas_call | solution.py:744
  225.8 124.3 %reduce.1 = (f32[96,192]{1,0:T(8,128)}, f32[96,192]{1,0:T(8,128)}, f32[96,192]{1,0:T(8,128)}, f32[96,192]{1,0:T(8,128)}, f32[96,192]{1,0:T(8,128)}, /*index=5*/f...) custom-call(bf16[2,4,2,96,2688]{4,3,2,1,0:T(8,128)(2,1)} %bitcast.27, ...), custom_call_target="tpu_custom_call" | custom-call | tf_op jit(solution)/shard_map/reduce/pallas_call | solution.py:948
  350.2 1.4 constant_dynamic-slice_fusion
  351.5 1.3 slice_bitcast_fusion
  352.8 1.7 copy.70
  354.6 0.7 copy.94
  355.3 0.9 copy.95
  356.2 0.9 copy.96
  357.1 1.5 copy.97
  358.6 1.5 copy.98
  360.1 1.5 copy.99
  361.7 1.5 copy.100
  363.2 1.5 copy.101
  364.8 1.5 copy.102
  366.3 1.5 copy.103
  367.8 1.5 copy.104
  369.4 1.6 copy.105
  371.0 1.6 copy.106
  (33 shorter events, 5.4 us)
Async XLA Ops:
  225.8 128.8 %copy-start.2 = (bf16[2,128,768]{2,1,0:T(8,128)(2,1)S(1)}, bf16[2,128,768]{2,1,0:T(8,128)(2,1)}, u32[]{:S(2)}) copy-start(bf16[2,128,768]{2,1,0:T(8,128)(2,1)} %get-tuple-element.106) | copy-start | bytes 1179652
  225.8 129.5 %copy-start.1 = (f32[2,128,768]{2,1,0:T(8,128)S(1)}, f32[2,128,768]{2,1,0:T(8,128)}, u32[]{:S(2)}) copy-start(f32[2,128,768]{2,1,0:T(8,128)} %get-tuple-element.107) | copy-start | bytes 2359300
  225.8 130.4 %copy-start = (f32[2,128,768]{2,1,0:T(8,128)S(1)}, f32[2,128,768]{2,1,0:T(8,128)}, u32[]{:S(2)}) copy-start(f32[2,128,768]{2,1,0:T(8,128)} %get-tuple-element.108) | copy-start | bytes 2359300

commit v4 on v3

--- a/solution.py
+++ b/solution.py
@@ -77,7 +77,7 @@
 
 GATHER = (
     ("w", 2560, 128, 0), ("w", 0, H, 0), ("w", H, H, 1), ("w", 2 * H, H, 0), ("w", 3 * H, H, 1),
-    ("w", 1536, 512, 0), ("w", 2048, 512, 1), ("d", 0, 64, 0), ("d", 64, 64, 1),
+    ("d", 0, 64, 0), ("d", 64, 64, 1), ("w", 1536, 512, 0), ("w", 2048, 512, 1),
 )
 SCATTER = (
     ("w", 1536, 512, 0), ("w", 2048, 512, 1), ("d", 0, 64, 0), ("d", 64, 64, 1),
@@ -85,6 +85,12 @@
 )
 
 
+OWN = {
+    ("w", 0): (0, 0), ("w", H): (0, H), ("w", 2560): (0, 2 * H), ("w", 2 * H): (96, 0), ("w", 3 * H): (96, H),
+    ("w", 1536): (192, 0), ("w", 2048): (192, 512), ("d", 0): (288, 0), ("d", 64): (352, 0),
+}
+
+
 def place():
     row, seq = lax.axis_index("rows"), lax.axis_index("seq")
     return lax.div(row, 2), lax.rem(row, 2), lax.div(seq, 2), lax.rem(seq, 2)
@@ -95,8 +101,8 @@
 
 
 class Gather:
-    def __init__(self, own_w, own_d, w, wd, ssem, rsem):
-        self.refs = (own_w, own_d, w, wd, ssem, rsem)
+    def __init__(self, room, w, wd, ssem, rsem):
+        self.refs = (room, w, wd, ssem, rsem)
         self.z, self.y, self.x, self.c = place()
         self.sent = []
         self.open = {}
@@ -117,7 +123,7 @@
 
     def view(self, k, x, z, y):
         kind, first, size, _ = GATHER[k]
-        _, _, w, wd, _, _ = self.refs
+        _, w, wd, _, _ = self.refs
         r = 2 * z + y
         if kind == "w":
             return w.at[x, pl.ds(pl.multiple_of(96 * r, 96), 96), first : first + size]
@@ -125,8 +131,9 @@
 
     def own(self, k):
         kind, first, size, _ = GATHER[k]
-        own_w, own_d, _, _, _, _ = self.refs
-        return own_w.at[:, first : first + size] if kind == "w" else own_d.at[first : first + size, :]
+        row, lane = OWN[kind, first]
+        height, width = (96, size) if kind == "w" else (size, H)
+        return self.refs[0].at[row : row + height, lane : lane + width]
 
     def peers(self, k):
         y_peer, x_peer = device(self.z, 1 - self.y, self.x, self.c), device(self.z, self.y, 1 - self.x, self.c)
@@ -136,7 +143,7 @@
         return (1 - self.x, self.y) if GATHER[k][3] else (self.x, 1 - self.y)
 
     def copy(self, k, slot, src, dst, peer):
-        _, _, _, _, ssem, rsem = self.refs
+        _, _, _, ssem, rsem = self.refs
         return pltpu.make_async_remote_copy(
             src_ref=src, dst_ref=dst, send_sem=ssem.at[k, slot], recv_sem=rsem.at[k, slot],
             device_id=peer, device_id_type=MESH)
@@ -199,6 +206,135 @@
             self.pump(1)
 
 
+class Scatter:
+    def __init__(self, w, wd, sums, buffers, ssem, rsem):
+        self.grads, self.sums = (w, wd), sums
+        self.buffers = (buffers[0:2], buffers[2:4], buffers[4:6])
+        self.sems = (ssem, rsem)
+        self.z, self.y, self.x, self.c = place()
+        self.y_peer = device(self.z, 1 - self.y, self.x, self.c)
+        self.x_peer = device(self.z, self.y, 1 - self.x, self.c)
+        self.z_peers = [device(lax.rem(self.z + j, 4), self.y, self.x, self.c) for j in range(1, 4)]
+        self.sent = []
+        self.ready = set()
+        count = len(SCATTER)
+        self.todo = [(self.first, n) for n in range(4)]
+        for n in range(count):
+            self.todo.append((self.after_first, n))
+            if n + 4 < count:
+                self.todo.append((self.first, n + 4))
+            if n >= 1:
+                self.todo.append((self.after_second, n - 1))
+            if n >= 2:
+                self.todo.append((self.after_third, n - 2))
+        self.todo += [(self.after_second, count - 1), (self.after_third, count - 2), (self.after_third, count - 1)]
+
+    def copy(self, n, slot, src, dst, peer):
+        ssem, rsem = self.sems
+        return pltpu.make_async_remote_copy(
+            src_ref=src, dst_ref=dst, send_sem=ssem.at[n, slot], recv_sem=rsem.at[n, slot],
+            device_id=peer, device_id_type=MESH)
+
+    def send(self, *args):
+        copy = self.copy(*args)
+        copy.start()
+        self.sent.append(copy)
+
+    def part(self, n, refs, *lead):
+        kind, first, size, _ = SCATTER[n]
+        if kind == "w":
+            return refs[0].at[(*lead, slice(None), slice(first, first + size))]
+        return refs[1].at[(*lead, slice(first, first + size), slice(None))]
+
+    def grad(self, n, a, z, mine):
+        kind, first, size, order = SCATTER[n]
+        x, y = (a, self.y if mine else 1 - self.y) if order else (self.x if mine else 1 - self.x, a)
+        r = 2 * z + y
+        if kind == "w":
+            return self.grads[0].at[x, pl.ds(pl.multiple_of(96 * r, 96), 96), first : first + size]
+        return self.grads[1].at[x, pl.ds(pl.multiple_of(128 * r + first, 64), size), :]
+
+    def second_place(self, n):
+        return self.x if SCATTER[n][3] else self.y
+
+    def first(self, n):
+        peer = self.y_peer if SCATTER[n][3] else self.x_peer
+        m = self.second_place(n)
+        for i, a in enumerate((1 - m, m)):
+            for z in range(4):
+                self.send(n, 4 * i + z, self.grad(n, a, z, False), self.part(n, self.buffers[0], a, z), peer)
+
+    def add(self, dest, other):
+        dest[...] = (dest[...].astype(F32) + other[...].astype(F32)).astype(BF16)
+
+    def after_first(self, n):
+        peer, onward = (self.y_peer, self.x_peer) if SCATTER[n][3] else (self.x_peer, self.y_peer)
+        m = self.second_place(n)
+        for i, a in enumerate((1 - m, m)):
+            for z in range(4):
+                block = self.part(n, self.buffers[0], a, z)
+                self.copy(n, 4 * i + z, block, block, peer).wait_recv()
+
+            def one(z):
+                self.add(self.part(n, self.buffers[0], a, z), self.grad(n, a, z, True))
+
+            repeat(4, one)
+            if i == 0:
+                block = self.part(n, self.buffers[0], a, slice(None))
+                self.send(n, 8, block, self.part(n, self.buffers[1], slice(None)), onward)
+
+    def after_second(self, n):
+        onward = self.x_peer if SCATTER[n][3] else self.y_peer
+        block = self.part(n, self.buffers[1], slice(None))
+        self.copy(n, 8, block, block, onward).wait_recv()
+        m = self.second_place(n)
+
+        def one(z):
+            self.add(self.part(n, self.buffers[1], z), self.part(n, self.buffers[0], m, z))
+
+        repeat(4, one)
+        for j in range(1, 4):
+            self.send(
+                n, 8 + j, self.part(n, self.buffers[1], lax.rem(self.z + j, 4)),
+                self.part(n, self.buffers[2], j - 1), self.z_peers[j - 1])
+
+    def after_third(self, n):
+        value = self.part(n, self.buffers[1], self.z)[...].astype(F32)
+        for j in range(1, 4):
+            block = self.part(n, self.buffers[2], j - 1)
+            self.copy(n, 8 + j, block, block, self.z_peers[j - 1]).wait_recv()
+            value = value + block[...].astype(F32)
+        self.part(n, self.sums)[...] = value
+
+    def made(self, *pieces):
+        self.ready.update(pieces)
+        self.pump(0)
+
+    def pump(self, count):
+        while self.todo:
+            action, n = self.todo[0]
+            if action == self.first:
+                if n not in self.ready:
+                    return
+            elif count <= 0:
+                return
+            else:
+                count -= 1
+            self.todo.pop(0)
+            action(n)
+
+
+class Idle:
+    def __init__(self):
+        self.sent = []
+
+    def made(self, *pieces):
+        pass
+
+    def pump(self, count):
+        pass
+
+
 class Loaded:
     def __init__(self, w_in, wd_in, w, wd, sems):
         self.copies = [pltpu.make_async_copy(w_in, w, sems.at[0]), pltpu.make_async_copy(wd_in, wd, sems.at[1])]
@@ -215,18 +351,59 @@
         self.copies = []
 
 
+def pair_tiles(a, b, x):
+    low = low_lanes()
+    tiles = []
+    for t in range(3):
+        u, v = [m[:, 64 * t : 64 * t + 64].astype(F32) for m in (a, b)]
+        tiles.append(jnp.where(x == 0, jnp.concatenate([u, v], axis=1), jnp.concatenate([v, u], axis=1)))
+    return tiles
+
+
+def fill_payload(packed, room, x):
+    squares, gate, up, down, gains = packed[:8], packed[8], packed[9], packed[10], packed[11]
+    for n, (a, b) in enumerate(PAIRS):
+        for t, value in enumerate(pair_tiles(squares[a][...], squares[b][...], x)):
+            rows, lanes = OWN["w", H * n]
+            room[rows : rows + 96, lanes + 128 * t : lanes + 128 * t + 128] = value.astype(BF16)
+    for ref, first in ((gate, 1536), (up, 2048)):
+        rows, lanes = OWN["w", first]
+        for n, m in enumerate((0, 2, 1, 3)):
+            room[rows : rows + 96, lanes + 128 * n : lanes + 128 * n + 128] = ref[:, 128 * m : 128 * m + 128]
+    rows, lanes = OWN["d", 0]
+    for t, value in enumerate(pair_tiles(down[0:128], down[128:256], x)):
+        room[rows : rows + 128, lanes + 128 * t : lanes + 128 * t + 128] = value.astype(BF16)
+    spread = lax.broadcasted_iota(jnp.int32, (3, 128), 0) == lax.broadcasted_iota(jnp.int32, (3, 128), 1)
+    columns = lax.dot_general(
+        gains[...], spread.astype(BF16), (((0,), (0,)), ((), ())), preferred_element_type=F32)
+    rows, lanes = OWN["w", 2560]
+    room[rows : rows + 96, lanes : lanes + 128] = columns.astype(BF16)
+
+
 def layer_kernel(
-    inside, in_x, in_m, in_g, segments, buckets, pos_bias, w_in, wd_in,
-    mixed, input_grad, memory_grad, small, w, wd,
-    w_o, w_cq, w_co, w_d, gains, table, dist_grad, full, ffb, na, qkv, att, attn, x1, cq, mkv, catt, cattn, x2,
+    inside, in_x, in_m, in_g, segments, buckets, pos_bias, *refs,
+):
+    count = 12 if inside else 2
+    packed, refs = refs[:count], refs[count:]
+    mixed, input_grad, memory_grad, *refs = refs
+    if inside:
+        sums, sums_d, total, *refs = refs
+    else:
+        small, w, wd, *refs = refs
+    (
+    w_o, w_cq, w_co, w_d, gains, table, dist_grad, full, ffb, na, qkv, att, attn, x1, cq, mkv, catt, x2,
     bias, p_self, hidden, gg, gu, gsend, grecv, gx2, gxb,
     gcq, dk_t, dv_t, qt_s, gt_s, left_t, work,
     psend, precv, msend, late, gdsend,
     ssem, rsem, gather_ssem, gather_rsem,
-):
+    ) = refs[:43]
+    if inside:
+        small, w, wd, acc, got, *refs = refs[43:]
+        buffers, (scatter_ssem, scatter_rsem, small_ssem, small_rsem) = refs[:6], refs[6:]
     p_cross = bias
     gw, gwd = w, wd
     nb = nc = na
+    cattn = attn
     gatt = hidden
     row = lax.axis_index("rows")
     seq = lax.axis_index("seq")
@@ -234,6 +411,9 @@
     c = lax.rem(seq, 2)
     mate = (row, 2 * x + (1 - c))
     across = (row, lax.rem(seq + 2, 4))
+
+    if inside:
+        fill_payload(packed, gg, x)
 
     barrier = pltpu.get_barrier_semaphore()
     peers = [mate, across]
@@ -245,6 +425,14 @@
         pl.semaphore_signal(barrier, inc=1, device_id=peer, device_id_type=MESH)
     pl.semaphore_wait(barrier, len(peers))
 
+    if inside:
+        weights = Gather(gg, w, wd, gather_ssem, gather_rsem)
+    else:
+        weights = Loaded(packed[0], packed[1], w, wd, gather_ssem)
+    weights.pump(3)
+    scatter = Idle()
+    if inside:
+        scatter = Scatter(w, wd, (sums, sums_d), buffers, scatter_ssem, scatter_rsem)
     started = []
 
     def remote(src, dst, slot, peer, keep=True):
@@ -274,12 +462,6 @@
         to_mate.append(remote(block.at[x], full.at[k, own], 28 + k, mate))
         full[k, own] = block[x]
 
-    if inside:
-        weights = Gather(w_in, wd_in, w, wd, gather_ssem, gather_rsem)
-    else:
-        weights = Loaded(w_in, wd_in, w, wd, gather_ssem)
-    weights.need(8)
-
     def separate(first, second, ref, lanes, rows_at, count):
         def part(i):
             at = tile(i, 128, 128) if rows_at is None else rows_at(i)
@@ -294,44 +476,38 @@
             ref[lead, at, lanes] = value
         return put
 
-    for t in range(12):
-        lanes = slice(128 * t, 128 * t + 128)
-        inside = slice(128 * (t % 3), 128 * (t % 3) + 128)
-        first, second = store(w, 0, lanes), store(w, 1, lanes)
-        if t // 3 == 1:
-            second = store(w_cq, c, inside)
-        if t // 3 == 3:
-            first, second = store(w_o, c, inside), store(w_co, c, inside)
-        separate(first, second, w, lanes, None, 6)
+    def separate_group(group):
+        for t in range(3):
+            lanes = slice(128 * (3 * group + t), 128 * (3 * group + t) + 128)
+            inner = slice(128 * t, 128 * t + 128)
+            first, second = store(w, 0, lanes), store(w, 1, lanes)
+            if group == 1:
+                second = store(w_cq, c, inner)
+            if group == 3:
+                first, second = store(w_o, c, inner), store(w_co, c, inner)
+            separate(first, second, w, lanes, None, 6)
 
     halves = []
-    for k, ref in enumerate((w_o, w_cq, w_co)):
-        halves.append(remote(ref.at[c], ref.at[c], 31 + k, mate, False))
-
-    for t in range(3):
-        lanes = slice(128 * t, 128 * t + 128)
-
-        def part(i):
-            at = tile(i, 128, 128)
-            a, b = wd[0, at, lanes].astype(F32), wd[1, at, lanes].astype(F32)
-            wd[0, at, lanes] = jnp.where(low, a, b).astype(BF16)
-            wd[1, at, lanes] = roll_half(jnp.where(low, b, a)).astype(BF16)
-
-        repeat(8, part)
-    for xs in range(2):
-        for b in range(2):
-            piece = wd.at[b, tile((1 - c) + 2 * xs, 256, 256)]
-            halves.append(remote(piece, w_d.at[c, 2 * xs + b], 34 + 2 * xs + b, mate, False))
-            w_d[c, 2 * xs + b] = wd[b, tile(c + 2 * xs, 256, 256)]
-
-    for copy in halves:
-        copy.wait_send()
-
-    gains[...] = w[0, :, 2560:2688].astype(F32).T[0:8]
+
+    def share(ref, slot):
+        halves.append(remote(ref.at[c], ref.at[c], slot, mate))
+
+    def separate_down():
+        for t in range(3):
+            lanes = slice(128 * t, 128 * t + 128)
+            separate(store(wd, 0, lanes), store(wd, 1, lanes), wd, lanes, None, 8)
+        copies = []
+        for xs in range(2):
+            for b in range(2):
+                w_d[c, 2 * xs + b] = wd[b, tile(c + 2 * xs, 256, 256)]
+                piece = wd.at[b, tile((1 - c) + 2 * xs, 256, 256)]
+                copies.append(remote(piece, w_d.at[c, 2 * xs + b], 34 + 2 * xs + b, mate, False))
+        return copies
+
     hot = (lax.broadcasted_iota(jnp.int32, (BUCKETS, T), 0) == buckets[...]).astype(BF16)
     by_distance = lax.dot_general(pos_bias[...], hot, (((0,), (0,)), ((), ())), preferred_element_type=F32)
-    total = lax.broadcasted_iota(jnp.int32, (T, T), 0) + lax.broadcasted_iota(jnp.int32, (T, T), 1)
-    mirror = ((total == 0) | (total == T)).astype(BF16)
+    both = lax.broadcasted_iota(jnp.int32, (T, T), 0) + lax.broadcasted_iota(jnp.int32, (T, T), 1)
+    mirror = ((both == 0) | (both == T)).astype(BF16)
     work[0:HEADS] = dotf(by_distance.astype(BF16), mirror)
     for t in range(3):
         for a in range(2):
@@ -376,11 +552,22 @@
 
         repeat(4, part)
 
+    weights.need(0)
+    gains[...] = w[0, :, 2560:2688].astype(F32).T[0:8]
     norm(lambda k: full[0, k].astype(F32), 0, na)
-
+    weights.need(1)
+    separate_group(0)
     qkv[:, 0:H] = (dotf(na[...], w[0, :, 0:H]).astype(BF16) * 0.125).astype(BF16)
     qkv[:, H : 2 * H] = dotf(na[...], w[1, :, 0:H]).astype(BF16)
+    weights.need(2)
+    separate_group(1)
+    share(w_cq, 31)
     qkv[:, 2 * H :] = dotf(na[...], w[0, :, H : 2 * H]).astype(BF16)
+
+    def prob_place(qt, causal):
+        if causal:
+            return slice(0, 256), slice(256 * qt, 256 + 512 * qt)
+        return slice(256 * qt, 256 * qt + 256), slice(0, T)
 
     def attend(t, q, qo, k, ko, v, vo, bias_ref, probs, out):
         qc, kc, vc = tile(t + qo, 128, 128), tile(t + ko, 128, 128), tile(t + vo, 128, 128)
@@ -396,7 +583,8 @@
                     s = s + bias_ref[2 * t + a, rows, 0:nk].astype(F32)
                 e = jnp.exp(s - jnp.max(s, axis=-1, keepdims=True))
                 prob = (e * (1.0 / jnp.sum(e, axis=-1, keepdims=True))).astype(BF16)
-                probs[2 * t + a, rows, 0:nk] = prob
+                at, keys = prob_place(qt, bias_ref is not None)
+                probs[2 * t + a, at, keys] = prob
                 outs.append(dotf(prob, v2))
             out[rows, oc] = jnp.where(low, outs[0], outs[1]).astype(BF16)
 
@@ -416,7 +604,8 @@
                 half = slice(64 * a, 64 * a + 64)
                 delta = jnp.sum(jnp.where(masks[a], both, 0.0), axis=-1, keepdims=True)
                 dp = dot_t(jnp.where(masks[a], g2, jnp.zeros_like(g2)), v2)
-                prob = probs[2 * t + a, rows, 0:nk]
+                at, keys = prob_place(qt, causal)
+                prob = probs[2 * t + a, at, keys]
                 ds = (prob.astype(F32) * (dp - delta)).astype(BF16)
                 outs.append(dotf(ds, k2))
                 dk = dotf(qt_s[half, rows], ds)
@@ -451,10 +640,16 @@
     for t in range(3):
         attend(t, qkv, 0, qkv, 3, qkv, 6, bias, p_self, att)
         copies.append(send_head(att, t, 3))
-
+        weights.pump(3)
+
+    weights.need(3)
+    separate_group(2)
     for k in range(2):
         mkv[:, H * k : H * k + H] = dotf(full[1], w[k, :, 2 * H : 3 * H]).astype(BF16)
-    wait_all(halves)
+    weights.need(4)
+    separate_group(3)
+    share(w_o, 32)
+    share(w_co, 33)
     wait_all(copies)
 
     def natural_heads(source, dest):
@@ -476,6 +671,7 @@
         repeat(2, part)
 
     natural_heads(att, attn)
+    wait_all(halves)
     residual(lambda r, k: full[0, r, k].astype(F32), attn, w_o, x1)
     norm(lambda k: x1[k], 1, nb)
     cq[...] = (dotf(nb[...], w_cq[c]).astype(BF16) * 0.125).astype(BF16)
@@ -484,11 +680,18 @@
     for t in range(3):
         attend(t, cq, 0, mkv, 0, mkv, 3, None, p_cross, catt)
         copies.append(send_head(catt, t, 6))
+        weights.pump(2)
     wait_all(copies)
 
+    weights.need(6)
+    down_copies = separate_down()
     natural_heads(catt, cattn)
     residual(lambda r, k: x1[r, k], cattn, w_co, x2)
     norm(lambda k: x2[k], 2, nc)
+
+    weights.need(8)
+    for copy in down_copies:
+        copy.wait()
 
     def feed(n):
         cols = tile(n, 256, 256)
@@ -576,6 +779,7 @@
         (cols_of(gg), into(lambda n: lax.div(n, 4), lambda n: 12 + lax.rem(n, 4)), 8),
         (cols_of(gu), into(lambda n: lax.div(n, 4), lambda n: 16 + lax.rem(n, 4)), 8),
     ])
+    scatter.made(0, 1)
 
     def put_down(xs, own_half):
         def put(n, value):
@@ -591,6 +795,7 @@
                 gdsend[xs, 1, :, cols] = b
         return put
 
+    wait_all(gc_copies)
     gd_copies = []
     for xs in range(2):
         weight_grad(lambda j: hidden[:, pl.ds(pl.multiple_of(j.start + 512 * xs, 128), 128)], 512, [
@@ -599,7 +804,6 @@
         ])
         gd_copies.append(remote(gdsend.at[xs], gwd.at[:, tile(c + 2 * xs, 256, 256)], 38 + xs, mate))
 
-    wait_all(gc_copies)
     small[...] = jnp.zeros_like(small)
 
     def keep_gain(index, i, gain):
@@ -629,14 +833,22 @@
         keep_gain(2, i, gain)
 
     repeat(4, third)
+    wait_all(gd_copies)
+    scatter.made(2, 3)
     back_heads(w_co)
     gmkv = grecv
     copies = []
     for t in range(3):
         attend_back(t, cq, 0, mkv, 0, mkv, 3, p_cross, catt, False, gcq, 3 * c, gmkv, 0, gmkv, 3)
         copies.append(send_head(gcq, t, 14))
+        scatter.pump(1 if t else 0)
 
     mem_copies = pair_partial(lambda k: dot_t(gmkv[:, 0:H], w[0, k, 2 * H : 3 * H]) + dot_t(gmkv[:, H:], w[1, k, 2 * H : 3 * H]), psend.at[1], precv.at[1], 17)
+
+    weight_grad(lambda j: full[1, :, j], D, [
+        (cols_of(gmkv), into_pair(2, pack_first), 3), (cols_of(gmkv, 3), into_pair(2, pack_second), 3)])
+    scatter.made(4)
+    scatter.pump(1)
 
     wait_all(mix_copies)
 
@@ -665,25 +877,36 @@
         keep_gain(1, i, gain)
 
     repeat(4, second)
+    natural_heads(att, attn)
+    weight_grad(lambda j: attn[:, j], D, [(cols_of(gxb, 3 * c), into_pair(3, pack_first), 3)])
+    scatter.made(5)
+    scatter.pump(2)
     back_heads(w_o)
     for t in range(3):
         attend_back(t, qkv, 0, qkv, 3, qkv, 6, p_self, att, True, gg, 0, gg, 3, gu, 0)
+        scatter.pump(2)
+
+    for copy in mix_copies:
+        copy.wait_send()
+    started[:] = [copy for copy in started if not any(copy is done for done in mix_copies)]
 
     def back_a(k):
         part = dot_t(gg[:, 0:H], w[0, k, 0:H]) + dot_t(gg[:, H : 2 * H], w[1, k, 0:H])
         return part + dot_t(gu[:, 0:H], w[0, k, H : 2 * H])
 
-    ig_copies = pair_partial(back_a, psend.at[2], precv.at[2], 21)
-
-    weight_grad(lambda j: full[1, :, j], D, [
-        (cols_of(gmkv), into_pair(2, pack_first), 3), (cols_of(gmkv, 3), into_pair(2, pack_second), 3)])
-    norm(lambda k: x1[k], 1, nb)
-    weight_grad(lambda j: nb[:, j], D, [(cols_of(gcq, 3 * c), into_pair(1, pack_second), 3)])
-    weight_grad(lambda j: attn[:, j], D, [(cols_of(gxb, 3 * c), into_pair(3, pack_first), 3)])
+    ig_copies = pair_partial(back_a, psend.at[0], precv.at[2], 21)
+
+    scatter.pump(1)
     norm(lambda k: full[0, k].astype(F32), 0, na)
     weight_grad(lambda j: na[:, j], D, [
         (cols_of(gg), into_pair(0, pack_first), 3), (cols_of(gg, 3), into_pair(0, pack_second), 3),
         (cols_of(gu), into_pair(1, pack_first), 3)])
+    scatter.made(6)
+    scatter.pump(1)
+    norm(lambda k: x1[k], 1, nb)
+    weight_grad(lambda j: nb[:, j], D, [(cols_of(gcq, 3 * c), into_pair(1, pack_second), 3)])
+    scatter.made(7)
+    scatter.pump(1)
 
     flipped = (
         lax.broadcasted_iota(jnp.int32, (T, T), 0) + lax.broadcasted_iota(jnp.int32, (T, T), 1) == T - 1
@@ -705,10 +928,11 @@
     mem_out = remote(msend.at[1], late.at[0], 20, across)
     memory_grad[x] = psend[1, 2 * x + c].astype(F32) + precv[1, x].astype(F32)
 
+    scatter.pump(2)
     wait_all(ig_copies)
 
     def first_block(k, chunk):
-        upstream = psend[2, 2 * k + c].astype(F32) + precv[2, k].astype(F32)
+        upstream = psend[0, 2 * k + c].astype(F32) + precv[2, k].astype(F32)
         gv, gain = norm_back(full[0, chunk].astype(F32), gains[0:1], upstream)
         small[0:1, 0:D] += gain
         return gx2[chunk] + gv
@@ -716,52 +940,81 @@
     msend[2] = first_block(1 - x, other).astype(BF16)
     ig_out = remote(msend.at[2], late.at[1], 23, across)
     input_grad[x] = first_block(x, own)
+
+    if inside:
+        z, y, _, _ = place()
+
+        def small_send(slot, ref, peer):
+            copy = pltpu.make_async_remote_copy(
+                src_ref=ref, dst_ref=got.at[slot], send_sem=small_ssem.at[slot], recv_sem=small_rsem.at[slot],
+                device_id=peer, device_id_type=MESH)
+            copy.start()
+            started.append(copy)
+            return copy
+
+        held = small
+        for slot, peer in enumerate((mate, scatter.x_peer, scatter.y_peer)):
+            copy = small_send(slot, held, peer)
+            scatter.pump(3)
+            copy.wait_recv()
+            acc[slot] = held[...] + got[slot]
+            held = acc.at[slot]
+        last = [small_send(2 + j, held, scatter.z_peers[j - 1]) for j in range(1, 4)]
+        scatter.pump(100)
+        wait_all(last)
+        total[...] = held[...] + got[3] + got[4] + got[5]
 
     mem_out.wait_recv()
     memory_grad[1 - x] = late[0].astype(F32)
     ig_out.wait_recv()
     input_grad[1 - x] = late[1].astype(F32)
     mix_out.wait_recv()
-    wait_all(gd_copies)
-    for copy in started + weights.sent:
+    for copy in started + weights.sent + scatter.sent:
         copy.wait_send()
 
 
-def layer(blocks, segments, buckets, pos_bias, w, wd, inside):
+def layer(blocks, segments, buckets, pos_bias, packed, inside):
     def bf(*shape):
         return VMEM(shape, BF16)
 
     def fl(*shape):
         return VMEM(shape, F32)
 
-    outs = [
-        ((2, 128, D), BF16), ((2, 128, D), F32), ((2, 128, D), F32), ((16, D + 128), F32),
-        ((2, D, 2688), BF16), ((2, FH, H), BF16),
-    ]
+    blocks_out = [((2, 128, D), BF16), ((2, 128, D), F32), ((2, 128, D), F32)]
+    tiny = (16, D + 128)
+    if inside:
+        outs = blocks_out + [((96, 2560), F32), ((128, H), F32), (tiny, F32)]
+    else:
+        outs = blocks_out + [(tiny, F32), ((2, D, 2688), BF16), ((2, FH, H), BF16)]
     whole = pl.BlockSpec(memory_space=pltpu.VMEM)
     dma = pltpu.SemaphoreType.DMA
     gather_sems = [dma((len(GATHER), 15)), dma((len(GATHER), 15))] if inside else [dma((2,)), dma((2,))]
+    own = [
+        fl(*tiny), bf(2, D, 2688), bf(2, FH, H), fl(3, *tiny), fl(6, *tiny),
+        bf(2, 4, 96, 2560), bf(2, 4, 128, H), bf(4, 96, 2560), bf(4, 128, H), bf(3, 96, 2560), bf(3, 128, H),
+        dma((len(SCATTER), 12)), dma((len(SCATTER), 12)), dma((6,)), dma((6,)),
+    ] if inside else []
     return pl.pallas_call(
         functools.partial(layer_kernel, inside),
         out_shape=[jax.ShapeDtypeStruct(s, d) for s, d in outs],
-        in_specs=[whole] * 6 + [whole if inside else pl.BlockSpec(memory_space=pl.ANY)] * 2,
+        in_specs=[whole] * 6 + [whole if inside else pl.BlockSpec(memory_space=pl.ANY)] * len(packed),
         out_specs=[whole] * len(outs),
         scratch_shapes=[
             bf(2, D, H), bf(2, D, H), bf(2, D, H), bf(2, 4, 256, H), fl(8, D), fl(8, T), fl(8, T),
             bf(3, T, D), bf(T, D), bf(T, D), bf(T, 3 * H), bf(T, D), bf(T, D), fl(T, D),
-            bf(T, H), bf(T, D), bf(T, D), bf(T, D), fl(T, D),
-            bf(6, T, T), bf(6, T, T), bf(T, FH), bf(T, FH), bf(T, FH), bf(T, D), bf(T, D),
+            bf(T, H), bf(T, D), bf(T, D), fl(T, D),
+            bf(6, T, T), bf(6, 256, 3 * 256), bf(T, FH), bf(T, FH), bf(T, FH), bf(T, D), bf(T, D),
             fl(T, D), bf(T, D),
             bf(T, D), fl(128, T), fl(128, T), bf(128, T), bf(128, T),
             bf(D, T), fl(T, T),
-            bf(3, 4, 128, D), bf(3, 2, 128, D), bf(3, 128, D), bf(2, 128, D), bf(2, 2, 256, H),
-            pltpu.SemaphoreType.DMA((40,)), pltpu.SemaphoreType.DMA((40,)), *gather_sems,
+            bf(2, 4, 128, D), bf(3, 2, 128, D), bf(3, 128, D), bf(2, 128, D), bf(2, 2, 256, H),
+            pltpu.SemaphoreType.DMA((40,)), pltpu.SemaphoreType.DMA((40,)), *gather_sems, *own,
         ],
         input_output_aliases={},
         compiler_params=pltpu.CompilerParams(
             collective_id=0, has_side_effects=True, vmem_limit_bytes=67043328),
         name="layer",
-    )(*blocks, segments, buckets.reshape(1, T), pos_bias, w, wd)
+    )(*blocks, segments, buckets.reshape(1, T), pos_bias, *packed)
 
 
 PAIRS = ((0, 1), (2, 4), (5, 6), (3, 7))
@@ -799,167 +1052,46 @@
     return lax.all_gather(v, "seq", axis=0, axis_index_groups=[[0, 2], [1, 3]])
 
 
-def reduce_kernel(
-    gw, gwd, small_in, *refs,
-):
-    squares, (gate, up, down, total), refs = refs[:8], refs[8:12], refs[12:]
-    r1, r1d, r2, r2d, r3, r3d, acc, got, ssem, rsem, small_ssem, small_rsem = refs
-    z, y, x, c = place()
-    mate = device(z, y, x, 1 - c)
-    y_peer, x_peer = device(z, 1 - y, x, c), device(z, y, 1 - x, c)
-    z_peers = [device(lax.rem(z + j, 4), y, x, c) for j in range(1, 4)]
+def finish_kernel(mixed_in, input_in, memory_in, sums, sums_d, small, *outs):
+    x = lax.div(lax.axis_index("seq"), 2)
     low = low_lanes()
-
-    barrier = pltpu.get_barrier_semaphore()
-    for peer in [mate, y_peer, x_peer] + z_peers:
-        pl.semaphore_signal(barrier, inc=1, device_id=peer, device_id_type=MESH)
-    pl.semaphore_wait(barrier, 6)
-    sent = []
-
-    def copy(k, slot, src, dst, peer):
-        return pltpu.make_async_remote_copy(
-            src_ref=src, dst_ref=dst, send_sem=ssem.at[k, slot], recv_sem=rsem.at[k, slot],
-            device_id=peer, device_id_type=MESH)
-
-    def send(*args):
-        out = copy(*args)
-        out.start()
-        sent.append(out)
-        return out
-
-    def part(k, w_ref, d_ref, *lead):
-        kind, first, size, _ = SCATTER[k]
-        if kind == "w":
-            return w_ref.at[(*lead, slice(None), slice(first, first + size))]
-        return d_ref.at[(*lead, slice(first, first + size), slice(None))]
-
-    def grads(k, a, mine):
-        if SCATTER[k][3]:
-            return part(k, gw, gwd, a, slice(None), y if mine else 1 - y)
-        return part(k, gw, gwd, x if mine else 1 - x, slice(None), a)
-
-    def second_place(k):
-        return x if SCATTER[k][3] else y
-
-    def sides(k):
-        m = second_place(k)
-        return (1 - m, m)
-
-    def first_send(k):
-        peer = y_peer if SCATTER[k][3] else x_peer
-        for i, a in enumerate(sides(k)):
-            send(k, i, grads(k, a, False), part(k, r1, r1d, a, slice(None)), peer)
-
-    def add_blocks(dest, other):
-        def one(i):
-            dest[i] = (dest[i].astype(F32) + other[i].astype(F32)).astype(BF16)
-
-        repeat(4, one)
-
-    def after_first(k):
-        peer = y_peer if SCATTER[k][3] else x_peer
-        onward = x_peer if SCATTER[k][3] else y_peer
-        for i, a in enumerate(sides(k)):
-            block = part(k, r1, r1d, a, slice(None))
-            copy(k, i, block, block, peer).wait_recv()
-            add_blocks(block, grads(k, a, True))
-            if i == 0:
-                send(k, 2, block, part(k, r2, r2d, slice(None)), onward)
-
-    def after_second(k):
-        onward = x_peer if SCATTER[k][3] else y_peer
-        block = part(k, r2, r2d, slice(None))
-        copy(k, 2, block, block, onward).wait_recv()
-        add_blocks(block, part(k, r1, r1d, second_place(k), slice(None)))
-        for j in range(1, 4):
-            send(k, 2 + j, part(k, r2, r2d, lax.rem(z + j, 4)), part(k, r3, r3d, j - 1), z_peers[j - 1])
-
-    def after_third(k):
-        value = part(k, r2, r2d, z)[...].astype(F32)
-        for j in range(1, 4):
-            block = part(k, r3, r3d, j - 1)
-            copy(k, 2 + j, block, block, z_peers[j - 1]).wait_recv()
-            value = value + block[...].astype(F32)
-        kind, first, size, _ = SCATTER[k]
-        if kind == "w" and first >= 1536:
-            dest = gate if first == 1536 else up
-            for n, m in enumerate((0, 2, 1, 3)):
-                dest[:, 128 * m : 128 * m + 128] = value[:, 128 * n : 128 * n + 128]
-            return
+    mixed, input_grad, memory_grad = outs[:3]
+    squares, gate, up, down, gains, bias = outs[3:11], *outs[11:]
+    mixed[...] = mixed_in[...]
+    input_grad[...] = input_in[...]
+    memory_grad[...] = memory_in[...]
+
+    def unpack(value, one, two):
         tiles = [jnp.where(x == 0, v, roll_half(v)) for v in lane_tiles(value)]
         turned = [roll_half(v) for v in tiles]
-        if kind == "w":
-            one, two = PAIRS[first // H]
-            targets = ((squares[one], slice(0, 96)), (squares[two], slice(0, 96)))
-        else:
-            targets = ((down, slice(first, first + size)), (down, slice(128 + first, 128 + first + size)))
-        ref, rows = targets[0]
-        ref[rows, 0:128] = jnp.where(low, tiles[0], turned[1])
-        ref[rows, 128:192] = tiles[2][:, 0:64]
-        ref, rows = targets[1]
-        ref[rows, 0:128] = jnp.where(low, turned[0], tiles[1])
-        ref[rows, 128:192] = turned[2][:, 0:64]
-
-    def small_send(slot, src, peer):
-        out = pltpu.make_async_remote_copy(
-            src_ref=src, dst_ref=got.at[slot], send_sem=small_ssem.at[slot], recv_sem=small_rsem.at[slot],
-            device_id=peer, device_id_type=MESH)
-        out.start()
-        sent.append(out)
-        return out
-
-    count = len(SCATTER)
-    first = small_send(0, small_in, mate)
-    for k in range(count):
-        first_send(k)
-    first.wait_recv()
-    acc[0] = small_in[...] + got[0]
-    first = small_send(1, acc.at[0], x_peer)
-    after_first(0)
-    first.wait_recv()
-    acc[1] = acc[0] + got[1]
-    first = small_send(2, acc.at[1], y_peer)
-    after_first(1)
-    after_second(0)
-    first.wait_recv()
-    acc[2] = acc[1] + got[2]
-    last = [small_send(2 + j, acc.at[2], z_peers[j - 1]) for j in range(1, 4)]
-    for k in range(2, count):
-        after_first(k)
-        after_second(k - 1)
-        after_third(k - 2)
-    after_second(count - 1)
-    after_third(count - 2)
-    after_third(count - 1)
-    for out in last:
-        out.wait_recv()
-    total[...] = acc[2] + got[3] + got[4] + got[5]
-    for out in sent:
-        out.wait_send()
-
-
-def scatter_lines(gw, gwd, small, x):
-    def bf(*shape):
-        return VMEM(shape, BF16)
-
+        one[:, 0:128] = jnp.where(low, tiles[0], turned[1])
+        one[:, 128:192] = tiles[2][:, 0:64]
+        two[:, 0:128] = jnp.where(low, turned[0], tiles[1])
+        two[:, 128:192] = turned[2][:, 0:64]
+
+    for n, (a, b) in enumerate(PAIRS):
+        unpack(sums[:, H * n : H * n + H], squares[a], squares[b])
+    unpack(sums_d[...], down.at[0:128], down.at[128:256])
+    for n, m in enumerate((0, 2, 1, 3)):
+        gate[:, 128 * m : 128 * m + 128] = sums[:, 1536 + 128 * n : 1664 + 128 * n]
+        up[:, 128 * m : 128 * m + 128] = sums[:, 2048 + 128 * n : 2176 + 128 * n]
+    shift = lax.rem(D - 96 * lax.axis_index("rows"), D)
+    gains[...] = pltpu.roll(small[0:8, 0:D], shift, 1)[0:3, 0:96]
+    bias[...] = small[:, D:].T[0:BUCKETS, 0:HEADS]
+
+
+def finish(mixed, input_grad, memory_grad, sums, sums_d, small):
     whole = pl.BlockSpec(memory_space=pltpu.VMEM)
-    dma = pltpu.SemaphoreType.DMA
-    outs = [(96, 192)] * 8 + [(96, 512), (96, 512), (256, 192), small.shape]
-    out = pl.pallas_call(
-        reduce_kernel,
-        out_shape=[jax.ShapeDtypeStruct(s, F32) for s in outs],
-        in_specs=[whole] * 3,
+    outs = [jax.ShapeDtypeStruct(v.shape, v.dtype) for v in (mixed, input_grad, memory_grad)]
+    shapes = [(96, 192)] * 8 + [(96, 512), (96, 512), (256, 192), (3, 96), (BUCKETS, HEADS)]
+    outs += [jax.ShapeDtypeStruct(s, F32) for s in shapes]
+    return tuple(pl.pallas_call(
+        finish_kernel,
+        out_shape=outs,
+        in_specs=[whole] * 6,
         out_specs=[whole] * len(outs),
-        scratch_shapes=[
-            bf(2, 4, 96, 2560), bf(2, 4, 128, H), bf(4, 96, 2560), bf(4, 128, H), bf(3, 96, 2560), bf(3, 128, H),
-            VMEM((3,) + small.shape, F32), VMEM((6,) + small.shape, F32),
-            dma((len(SCATTER), 6)), dma((len(SCATTER), 6)), dma((6,)), dma((6,)),
-        ],
-        compiler_params=pltpu.CompilerParams(
-            collective_id=1, has_side_effects=True, vmem_limit_bytes=60000000),
-        name="reduce",
-    )(gw.reshape(2, 4, 2, 96, 2688), gwd.reshape(2, 4, 2, 128, H), small)
-    return list(out[:8]), *out[8:]
+        name="finish",
+    )(mixed, input_grad, memory_grad, sums, sums_d, small))
 
 
 def scatter_plain(gw, gwd, small, x):
@@ -990,14 +1122,16 @@
 ):
     x = lax.axis_index("seq") // 2
     squares = (self_query, self_key, self_value, self_output, cross_query, cross_key, cross_value, cross_output)
-    w, wd = payload(squares, gate_weight, up_weight, down_weight, norm_gains, x)
     inside = lax.axis_size("rows") == 8
+    packed = (*squares, gate_weight, up_weight, down_weight, norm_gains)
     if not inside:
-        w, wd = gather_plain(w), gather_plain(wd)
-    mixed, input_grad, memory_grad, small, gw, gwd = layer(
-        (layer_input, memory, output_grad), segments, buckets, position_bias, w, wd, inside)
-    scatter = scatter_lines if inside else scatter_plain
-    squares, gate, up, down, small = scatter(gw, gwd, small, x)
+        packed = [gather_plain(v) for v in payload(squares, gate_weight, up_weight, down_weight, norm_gains, x)]
+    result = layer(
+        (layer_input, memory, output_grad), segments, buckets, position_bias, packed, inside)
+    if inside:
+        return finish(*result)
+    mixed, input_grad, memory_grad, small, gw, gwd = result
+    squares, gate, up, down, small = scatter_plain(gw, gwd, small, x)
     width = D // lax.axis_size("rows")
     gains = lax.dynamic_slice(small, (0, lax.axis_index("rows") * width), (3, width))
     return (mixed, input_grad, memory_grad, *squares, gate, up, down, gains, small[:HEADS, D : D + BUCKETS].T)

time: 376 us -> 252 us (0.67)
  Pallas kernels: 331 us -> 245 us
  local copies, waits for them, and re-layouts: 40.5 us -> 6.15 us
    pallas_call x1, Pallas kernels: 124 us -> 4.07 us  [finish(): pl.pallas_call(finish_kernel, out_shape=outs, in_specs=[whole] * 6, out_s...]
    pallas_call x1, Pallas kernels: 207 us -> 241 us  [layer(): pl.pallas_call(functools.partial(layer_kernel, inside), out_shape=[jax.Sh...]
    unnamed x36 -> x4, local copies, waits for them, and re-layouts: 33.1 us -> 3.74 us
where the time goes in v4:
time: 252 us
  Pallas kernels  245 us (97%)
  local copies, waits for them, and re-layouts  6.15 us (2%)
    pallas_call x1, Pallas kernels, layer(): pl.pallas_call(functools.partial(layer_kernel, inside), out_shape=[jax.Sh...  241 us

profile of v4, /device:TPU:0, one launch (start us, length us, event | category | flops | bytes accessed | tf_op | source)
XLA Modules:
  0.0 252.0 jit_solution(5675504926158283602)
XLA Ops:
  0.6 1.4 copy.34.pos_bias
  2.0 1.7 copy.35.refs_10_
  3.7 241.1 %layer.1 = (bf16[2,128,768]{2,1,0:T(8,128)(2,1)}, f32[2,128,768]{2,1,0:T(8,128)}, f32[2,128,768]{2,1,0:T(8,128)}, f32[96,2560]{1,0:T(8,128)}, f32[128,384]{1,0:T(8,128)}, /*index=5*/f32[16,896]{1,0:T(8,128)}) custom-call(bf16[2,128,768]{2,1,0:T(8,128)(2,1)} %in_x.1, bf16[2,128,768]{2,1,0:T(8,128)(2,1)} %in_m.1, bf16[2,128,768]{2,1,0:T(8,128)(2,1)} %in_g.1, ...), custom_call_target="tpu_custom_call" | custom-call | tf_op jit(solution)/shard_map/layer/pallas_call | solution.py:997
  244.8 4.1 %finish.1 = (bf16[2,128,768]{2,1,0:T(8,128)(2,1)}, f32[2,128,768]{2,1,0:T(8,128)}, f32[2,128,768]{2,1,0:T(8,128)}, f32[96,192]{1,0:T(8,128)}, f32[96,192]{1,0:T(...) custom-call(bf16[2,128,768]{2,1,0:T(8,128)(2,1)} %get-tuple-element., ...), custom_call_target="tpu_custom_call" | custom-call | tf_op jit(solution)/shard_map/finish/pallas_call | solution.py:1088
  248.9 0.0 copy-start
  248.9 0.7 copy-done
  249.6 0.7 copy.37
  250.2 1.7 copy.36
Async XLA Ops:
  248.9 0.7 copy-start
